TPU v7x, 32 devices: a whole 2x2x4 slice. The times are simulated.
32 devices in a mesh: quad: 2 (over x), py: 4 (over y, core), pz: 4 (over z).
Axes of the slice: x: 2, y: 2, z: 4, core: 2. Of those that a mesh axis runs over, the one named last changes fastest.
Arguments:
- source_real: float32 [4, 16, 64, 512], P(None, None, 'py', 'pz'), may hold values from -6 to 6
- source_imag: float32 [4, 16, 64, 512], P(None, None, 'py', 'pz'), may hold values from -2 to 2
- potential: float32 [16, 64, 512], P(None, 'py', 'pz'), may hold values from 0 to 2
- center: float32 [1], replicated, may hold values from 4.5 to 6
- radius: float32 [1], replicated, may hold values from 1 to 2
Outputs:
- moments: float32 [4, 2, 4, 16, 64, 512], P(None, None, None, 'quad', 'py', 'pz')
All inputs are finite; a program needn't handle non-finite values.
Results may differ from a plain program's by a relative error of at most 0.0003.
Values sent between devices are 32-bit elements; how exact they have to be, the bound alone decides.
No kernel may reach another device: no remote copies, remote signals or barrier semaphores. Data moves between devices by JAX's collectives and lax.ppermute only.
A program may use at most 256 MiB of HBM per device.

v0:
```python
import math

import jax
import jax.numpy as jnp
from jax import lax
from jax.sharding import PartitionSpec as P

QPTS = 8
MOMS = 4


stencil_weights = (-205.0 / 72.0, 8.0 / 5.0, -1.0 / 5.0, 8.0 / 315.0, -1.0 / 560.0)


def padded_2(block, sides, width):
    for axis, dim in sides:
        count = lax.axis_size(axis)
        forward = [(i, i + 1) for i in range(count - 1)]
        forward.append((count - 1, 0))
        backward = [(target, source) for source, target in forward]
        low = lax.ppermute(
            lax.slice_in_dim(block, block.shape[dim] - width, None, axis=dim), axis, forward
        )
        high = lax.ppermute(lax.slice_in_dim(block, 0, width, axis=dim), axis, backward)
        block = jnp.concatenate([low, block, high], axis=dim)
    return block


def apply_operator(field, potential):
    padded = padded_2(field, (("py", 4), ("pz", 5)), 4)
    width_y = field.shape[4]
    width_z = field.shape[5]
    laplace = 3.0 * stencil_weights[0] * field
    for offset in range(1, 5):
        beside_all = jnp.roll(field, offset, 3) + jnp.roll(field, -offset, 3)
        beside_all = (
            beside_all + padded[:, :, :, :, 4 + offset : 4 + offset + width_y, 4 : 4 + width_z]
        )
        beside_all = (
            beside_all + padded[:, :, :, :, 4 - offset : 4 - offset + width_y, 4 : 4 + width_z]
        )
        beside_all = (
            beside_all + padded[:, :, :, :, 4 : 4 + width_y, 4 + offset : 4 + offset + width_z]
        )
        beside_all = (
            beside_all + padded[:, :, :, :, 4 : 4 + width_y, 4 - offset : 4 - offset + width_z]
        )
        laplace = laplace + stencil_weights[offset] * beside_all
    return -0.5 * laplace + potential * field


def complex_mul(left, right):
    return (left[0] * right[0] - left[1] * right[1], left[0] * right[1] + left[1] * right[0])


def complex_div(left, right):
    norm_sq = right[0] * right[0] + right[1] * right[1]
    return (
        (left[0] * right[0] + left[1] * right[1]) / norm_sq,
        (left[1] * right[0] - left[0] * right[1]) / norm_sq,
    )


def local_bilinear(left, right):
    both = complex_mul(left, right)
    return (jnp.sum(both[0], axis=(-3, -2, -1)), jnp.sum(both[1], axis=(-3, -2, -1)))


def spread(value):
    return (value[0][..., None, None, None], value[1][..., None, None, None])


def moment_terms(solution, angles, radius_value):
    orders = jnp.arange(1, MOMS + 1).astype(jnp.float32)
    phase = orders[:, None] * angles[None, :]
    weight_re = radius_value / QPTS * jnp.cos(phase)
    weight_im = radius_value / QPTS * jnp.sin(phase)
    highest = lax.Precision.HIGHEST
    real_part = jnp.einsum("kq,qsxyz->ksxyz", weight_re, solution[:, 0], precision=highest)
    real_part = real_part - jnp.einsum(
        "kq,qsxyz->ksxyz", weight_im, solution[:, 1], precision=highest
    )
    imag_part = jnp.einsum("kq,qsxyz->ksxyz", weight_re, solution[:, 1], precision=highest)
    imag_part = imag_part + jnp.einsum(
        "kq,qsxyz->ksxyz", weight_im, solution[:, 0], precision=highest
    )
    return jnp.stack([real_part, imag_part], 1)


def per_device(source_real, source_imag, potential, center, radius):
    groups = lax.axis_size("quad")
    local_count = QPTS // groups
    first_point = lax.axis_index("quad") * local_count
    indices = (first_point + jnp.arange(local_count)).astype(jnp.float32)
    angles = 2.0 * math.pi * (indices + 0.5) / QPTS
    shift_re = center[0] + radius[0] * jnp.cos(angles)
    shift_im = radius[0] * jnp.sin(angles)
    shift_pair = (shift_re[:, None], shift_im[:, None])
    shift_field = (shift_re[:, None, None, None, None], shift_im[:, None, None, None, None])
    source = (source_real, source_imag)
    applied = apply_operator(jnp.stack(source)[None], potential)[0]
    hsource = (applied[0], applied[1])
    rho_local = local_bilinear(source, source)
    curv_local = local_bilinear(source, hsource)
    totals = lax.psum((rho_local[0], rho_local[1], curv_local[0], curv_local[1]), ("py", "pz"))
    rho_first = (totals[0], totals[1])
    curv_first = (totals[2], totals[3])
    scaled = complex_mul(shift_pair, rho_first)
    denom = (scaled[0] - curv_first[0], scaled[1] - curv_first[1])
    alpha_first = complex_div(rho_first, denom)
    alpha_wide = spread(alpha_first)
    first_iterate = complex_mul(alpha_wide, source)
    shifted = complex_mul(shift_field, source)
    image = (shifted[0] - hsource[0], shifted[1] - hsource[1])
    moved = complex_mul(alpha_wide, image)
    residual = (source[0] - moved[0], source[1] - moved[1])
    hres = apply_operator(jnp.stack(residual, 1), potential)
    shifted_res = complex_mul(shift_field, residual)
    image_res = (shifted_res[0] - hres[:, 0], shifted_res[1] - hres[:, 1])
    rho_part = local_bilinear(residual, residual)
    mixed_part = local_bilinear(residual, image_res)
    paired = lax.psum((rho_part[0], rho_part[1], mixed_part[0], mixed_part[1]), ("py", "pz"))
    rho_next = (paired[0], paired[1])
    mixed = (paired[2], paired[3])
    beta = complex_div(rho_next, rho_first)
    carried = complex_mul(spread(beta), source)
    direction = (residual[0] + carried[0], residual[1] + carried[1])
    correction = complex_div(complex_mul(beta, rho_next), alpha_first)
    curv_next = (mixed[0] - correction[0], mixed[1] - correction[1])
    alpha_next = complex_div(rho_next, curv_next)
    step_part = complex_mul(spread(alpha_next), direction)
    solution = jnp.stack((first_iterate[0] + step_part[0], first_iterate[1] + step_part[1]), 1)
    terms = moment_terms(solution, angles, radius[0])
    return lax.psum_scatter(terms, "quad", scatter_dimension=3, tiled=True)


def solution(mesh):
    in_specs = (P(None, None, "py", "pz"), P(None, None, "py", "pz"), P(None, "py", "pz"), P(), P())
    out_specs = P(None, None, None, "quad", "py", "pz")
    return jax.shard_map(
        per_device, mesh=mesh, in_specs=in_specs, out_specs=out_specs, check_vma=False
    )
```

profile of v0, /device:TPU:0, one launch (start us, length us, event | category | flops | bytes accessed | tf_op | source)
XLA Modules:
  0.0 492.1 jit_solution(7060185690487794828)
XLA Ops:
  50.9 4.5 fusion.50
  63.6 17.7 %fusion.58 = f32[1,2,4,16,16,128]{5,4,3,2,1,0:T(8,128)S(1)} fusion(f32[1,2,4,16,24,4]{5,4,3,2,1,0:T(8,128)} %copy.96, f32[1,2,4,16,24,128]{5,4,3,2,1,0:T(8,128)} %copy.93, f32[1,2,4,16,24,4]{5,4,3,2,1,0:T(8,128)} %copy.94, f32[1,2,4,15,16,128]{5,4,3,2,1,0:T(8,128)} %copy.87, f32[1,2,4,1,16,128]{5,4,3,2,1,0:T(8,128)} %bitcast.76, ...), kind=kLoop, calls=%fused_computation.166 | loop fusion | flops 12845056 | bytes 20676608 | tf_op jit(solution)/shard_map/add | solution.py:49
  82.9 34.7 %all-reduce.1 = (f32[4]{0:T(128)S(1)}, f32[4]{0:T(128)S(1)}, f32[4]{0:T(128)S(1)}, f32[4]{0:T(128)S(1)}) all-reduce(f32[4]{0:T(128)S(1)} %get-tuple-element.10, f32[4]{0:T(128)S(1)} %get-tuple-element.9, f32[4]{0:T(128)S(1)} %get-tuple-element.12, f32[4]{0:T(128)S(1)} %get-tuple-element.11), channel_id=1, replica_groups=mesh['quad'=2,'py'=4,'pz'=4] {'py','pz'}, use_global_device_ids=true, to_apply=%region_7.8 | all-reduce | flops 16 | bytes 128 | tf_op jit(solution)/shard_map/psum | solution.py:105
  124.4 3.5 fusion.31
  133.7 19.1 %copy.121 = f32[4,2,4,16,16,128]{4,3,5,2,1,0:T(8,128)} copy(f32[4,2,4,16,16,128]{5,4,3,2,1,0:T(8,128)} %pad_maximum_fusion.1) | data formatting | bytes 8388608 | tf_op jit(solution)/shard_map/stack | solution.py:117
  155.4 3.4 fusion.29
  162.0 3.4 fusion.25
  165.4 18.9 %copy.122 = f32[4,2,4,16,4,128]{4,3,5,2,1,0:T(8,128)} copy(f32[4,2,4,16,4,128]{5,3,4,2,1,0:T(8,128)} %collective-permute-done.4) | data formatting | bytes 2097152 | tf_op jit(solution)/shard_map/ppermute | solution.py:24
  184.3 18.6 %copy.120 = f32[4,2,4,16,4,128]{4,3,5,2,1,0:T(8,128)} copy(f32[4,2,4,16,4,128]{5,3,4,2,1,0:T(8,128)} %collective-permute-done.5) | data formatting | bytes 2097152 | tf_op jit(solution)/shard_map/ppermute | solution.py:21
  202.9 43.9 %pad_maximum_fusion = f32[4,2,4,16,24,128]{4,3,5,2,1,0:T(8,128)} fusion(f32[4,2,4,16,4,128]{4,3,5,2,1,0:T(8,128)} %copy.122, f32[4,2,4,16,16,128]{4,3,5,2,1,0:T(8,128)} %copy.121, f32[4,2,4,16,4,128]{4,3,5,2,1,0:T(8,128)} %copy.120), kind=kLoop, calls=%fused_computation | loop fusion | flops 3145728 | bytes 12582912 | tf_op jit(solution)/shard_map/concatenate | solution.py:25
  250.0 4.1 collective-permute-start.6
  257.3 5.5 %pad_maximum_fusion.2 = (f32[4,2,4,16,20,128]{5,4,3,2,1,0:T(8,128)}, f32[4,2,4,16,20,128]{5,4,3,2,1,0:T(8,128)}) fusion(f32[4,2,4,16,4,128]{5,4,3,2,1,0:T(4,128)S(1)} %copy.117, f32[4,1,4,16,16,128]{5,4,3,2,1,0:T(8,128)S(1)} %get-tuple-element.48, f32[4,1,4,16,16,128]{5,4,3,2,1,0:T(8,128)S(1)} %copy-done.2, f32[4,2,4,16,4,128]{5,4,3,2,1,0:T(4,128)S(1)} %copy.119), kind=kLoop, calls=%fused_computation.50 | loop fusion | flops 5242880 | bytes 16777216 | tf_op jit(solution)/shard_map/concatenate | solution.py:25
  262.8 22.1 %copy.123 = f32[4,2,4,16,24,128]{5,4,3,2,1,0:T(8,128)} copy(f32[4,2,4,16,24,128]{4,3,5,2,1,0:T(8,128)} %pad_maximum_fusion) | data formatting | bytes 12582912 | tf_op jit(solution)/shard_map/concatenate | solution.py:25
  284.9 6.1 %copy.125 = f32[4,2,4,16,24,4]{5,4,3,2,1,0:T(8,128)} copy(f32[4,2,4,16,24,4]{4,3,5,2,1,0:T(8,128)} %collective-permute-done.7) | data formatting | bytes 393216 | tf_op jit(solution)/shard_map/ppermute | solution.py:21
  291.0 7.0 %collective-permute-done.6 = f32[4,2,4,16,24,4]{4,3,5,2,1,0:T(8,128)} collective-permute-done((f32[4,2,4,16,24,4]{4,3,5,2,1,0:T(8,128)}, f32[4,2,4,16,24,4]{4,3,5,2,1,0:T(8,128)}, u32[]{:S(2)}, u32[]{:S(2)}) %collective-permute-start.6) | collective-permute-done | bytes 196640 | tf_op jit(solution)/shard_map/ppermute | solution.py:24
  298.1 6.0 %copy.124 = f32[4,2,4,16,24,4]{5,4,3,2,1,0:T(8,128)} copy(f32[4,2,4,16,24,4]{4,3,5,2,1,0:T(8,128)} %collective-permute-done.6) | data formatting | bytes 393216 | tf_op jit(solution)/shard_map/ppermute | solution.py:24
  304.1 62.2 %fusion.6 = f32[4,2,4,16,16,128]{5,4,3,2,1,0:T(8,128)} fusion(f32[4,2,4,16,24,4]{5,4,3,2,1,0:T(8,128)} %copy.125, f32[4,2,4,16,24,128]{5,4,3,2,1,0:T(8,128)} %copy.123, f32[4,2,4,16,24,4]{5,4,3,2,1,0:T(8,128)} %copy.124, f32[4,2,4,16,20,128]{5,4,3,2,1,0:T(8,128)} %get-tuple-element.43, f32[4,2,4,16,20,128]{5,4,3,2,1,0:T(8,128)} %get-tuple-element.42, ...), kind=kLoop, calls=%fused_computation.70 | loop fusion | flops 51380224 | bytes 82313216 | tf_op jit(solution)/shard_map/add | solution.py:49
  366.4 5.0 %subtract_reduce_fusion = (f32[4,4]{1,0:T(4,128)S(1)}, f32[4,4]{1,0:T(4,128)S(1)}, f32[4,4]{1,0:T(4,128)S(1)}, f32[4,4]{1,0:T(4,128)S(1)}) fusion(f32[4,2,4,16,16,128]{5,4,3,2,1,0:T(8,128)} %fusion.6, f32[4]{0:T(128)S(1)} %get-tuple-element.88, f32[4]{0:T(128)S(1)} %get-tuple-element.89, f32[4,16,16,128]{3,2,1,0:T(8,128)S(1)} %copy-done.8, ...), kind=kLoop, calls=%fused_computation.129 | loop fusion | flops 20447168 | bytes 6291872 | tf_op jit(solution)/shard_map/reduce_sum | solution.py:66
  371.4 30.9 %all-reduce = (f32[4,4]{1,0:T(4,128)S(1)}, f32[4,4]{1,0:T(4,128)S(1)}, f32[4,4]{1,0:T(4,128)S(1)}, f32[4,4]{1,0:T(4,128)S(1)}) all-reduce(f32[4,4]{1,0:T(4,128)S(1)} %get-tuple-element.8, f32[4,4]{1,0:T(4,128)S(1)} %get-tuple-element.6, f32[4,4]{1,0:T(4,128)S(1)} %get-tuple-element.7, ...), channel_id=1, replica_groups=mesh['quad'=2,'py'=4,'pz'=4] {'py','pz'}, use_global_device_ids=true, to_apply=%region_9.10 | all-reduce | flops 64 | bytes 512 | tf_op jit(solution)/shard_map/psum | solution.py:122
  405.4 4.4 fusion.34
  409.8 4.4 fusion.36
  414.2 4.6 add_bitcast_fusion
  418.9 4.8 subtract_bitcast_fusion
  428.3 53.5 %reduce-scatter.2.cloned.1.call-done = f32[4,2,4,8,16,128]{5,4,2,1,0,3:T(8,128)} async-done(((f32[4,2,4,16,16,128]{5,4,2,1,0,3:T(8,128)}), f32[4,2,4,8,16,128]{5,4,2,1,0,3:T(8,128)}) %reduce-scatter.2.cloned.1.call-update) | async-done | bytes 2097168 | tf_op jit(solution)/shard_map/reduce_scatter | solution.py:134
  (136 shorter events, 88.4 us)
Async XLA Ops:
  6.5 475.3 %reduce-scatter.2.cloned.1.call-start = ((), (), s32[]{:S(2)}) async-start(), calls=%async_computation.1 | async-start | bytes 6291456 | tf_op jit(solution)/shard_map/reduce_scatter | solution.py:134
  9.0 28.6 %collective-permute-start = (f32[1,2,4,16,4,128]{5,3,4,2,1,0:T(8,128)}, f32[1,2,4,16,4,128]{5,3,4,2,1,0:T(8,128)}, u32[]{:S(2)}, u32[]{:S(2)}) collective-permute-start(f32[1,2,4,16,4,128]{5,3,4,2,1,0:T(8,128)} %get-tuple-element.83), channel_id=1, source_target_pairs={{4,0},{8,4},{12,8},{0,12},{5,1},{9,5},{13,9},{1,13},{6,2},{10,6},{... | collective-permute-start | bytes 786440 | tf_op jit(solution)/shard_map/ppermute | solution.py:24
  11.4 26.2 %collective-permute-start.1 = (f32[1,2,4,16,4,128]{5,3,4,2,1,0:T(8,128)}, f32[1,2,4,16,4,128]{5,3,4,2,1,0:T(8,128)}, u32[]{:S(2)}, u32[]{:S(2)}) collective-permute-start(f32[1,2,4,16,4,128]{5,3,4,2,1,0:T(8,128)} %get-tuple-element.82), channel_id=1, source_target_pairs={{0,4},{4,8},{8,12},{12,0},{1,5},{5,9},{9,13},{13,1},{2,6},{6,10},{... | collective-permute-start | bytes 786440 | tf_op jit(solution)/shard_map/ppermute | solution.py:21
  44.0 13.2 %collective-permute-start.3 = (f32[1,2,4,16,24,4]{4,3,5,2,1,0:T(8,128)}, f32[1,2,4,16,24,4]{4,3,5,2,1,0:T(8,128)}, u32[]{:S(2)}, u32[]{:S(2)}) collective-permute-start(f32[1,2,4,16,24,4]{4,3,5,2,1,0:T(8,128)} %copy.95), channel_id=1, source_target_pairs={{0,1},{1,2},{2,3},{3,0},{4,5},{5,6},{6,7},{7,4},{8,9},{9,10},{10,1... | collective-permute-start | bytes 147464 | tf_op jit(solution)/shard_map/ppermute | solution.py:21
  48.5 12.1 %collective-permute-start.2 = (f32[1,2,4,16,24,4]{4,3,5,2,1,0:T(8,128)}, f32[1,2,4,16,24,4]{4,3,5,2,1,0:T(8,128)}, u32[]{:S(2)}, u32[]{:S(2)}) collective-permute-start(f32[1,2,4,16,24,4]{4,3,5,2,1,0:T(8,128)} %copy.92), channel_id=1, source_target_pairs={{1,0},{2,1},{3,2},{0,3},{5,4},{6,5},{7,6},{4,7},{9,8},{10,9},{11,1... | collective-permute-start | bytes 147464 | tf_op jit(solution)/shard_map/ppermute | solution.py:24
  55.4 8.1 %copy-start.3 = (f32[4,16,16,128]{3,2,1,0:T(8,128)S(1)}, f32[4,16,16,128]{3,2,1,0:T(8,128)}, u32[]{:S(2)}) copy-start(f32[4,16,16,128]{3,2,1,0:T(8,128)} %param.6) | copy-start | bytes 1572868
  55.4 8.1 %copy-start.4 = (f32[4,16,16,128]{3,2,1,0:T(8,128)S(1)}, f32[4,16,16,128]{3,2,1,0:T(8,128)}, u32[]{:S(2)}) copy-start(f32[4,16,16,128]{3,2,1,0:T(8,128)} %param.5) | copy-start | bytes 1572868
  81.3 36.4 %copy-start.5 = (f32[4,16,16,128]{3,2,1,0:T(8,128)S(1)}, f32[4,16,16,128]{3,2,1,0:T(8,128)}, u32[]{:S(2)}) copy-start(f32[4,16,16,128]{3,2,1,0:T(8,128)} %param.5) | copy-start | bytes 1572868
  117.6 11.8 %copy-start.26 = (f32[4]{0:T(128)}, f32[4]{0:T(128)S(1)}, u32[]{:S(2)}) copy-start(f32[4]{0:T(128)S(1)} %get-tuple-element.19) | copy-start | bytes 52
  117.6 11.8 %copy-start.28 = (f32[4]{0:T(128)}, f32[4]{0:T(128)S(1)}, u32[]{:S(2)}) copy-start(f32[4]{0:T(128)S(1)} %get-tuple-element.20) | copy-start | bytes 52
  120.2 12.7 %copy-start = (f32[4,1,4,16,16,128]{5,4,3,2,1,0:T(8,128)}, f32[4,1,4,16,16,128]{5,4,3,2,1,0:T(8,128)S(1)}, u32[]{:S(2)}) copy-start(f32[4,1,4,16,16,128]{5,4,3,2,1,0:T(8,128)S(1)} %get-tuple-element.49) | copy-start | bytes 6291460
  131.1 34.3 %collective-permute-start.4 = (f32[4,2,4,16,4,128]{5,3,4,2,1,0:T(8,128)}, f32[4,2,4,16,4,128]{5,3,4,2,1,0:T(8,128)}, u32[]{:S(2)}, u32[]{:S(2)}) collective-permute-start(f32[4,2,4,16,4,128]{5,3,4,2,1,0:T(8,128)} %copy.144), channel_id=1, source_target_pairs={{4,0},{8,4},{12,8},{0,12},{5,1},{9,5},{13,9},{1,13},{6,2},{10,6},{... | collective-permute-start | bytes 3145736 | tf_op jit(solution)/shard_map/ppermute | solution.py:24
  132.2 52.1 %collective-permute-start.5 = (f32[4,2,4,16,4,128]{5,3,4,2,1,0:T(8,128)}, f32[4,2,4,16,4,128]{5,3,4,2,1,0:T(8,128)}, u32[]{:S(2)}, u32[]{:S(2)}) collective-permute-start(f32[4,2,4,16,4,128]{5,3,4,2,1,0:T(8,128)} %copy.145), channel_id=1, source_target_pairs={{0,4},{4,8},{8,12},{12,0},{1,5},{5,9},{9,13},{13,1},{2,6},{6,10},{... | collective-permute-start | bytes 3145736 | tf_op jit(solution)/shard_map/ppermute | solution.py:21
  250.0 34.9 %collective-permute-start.7 = (f32[4,2,4,16,24,4]{4,3,5,2,1,0:T(8,128)}, f32[4,2,4,16,24,4]{4,3,5,2,1,0:T(8,128)}, u32[]{:S(2)}, u32[]{:S(2)}) collective-permute-start(f32[4,2,4,16,24,4]{4,3,5,2,1,0:T(8,128)} %get-tuple-element.25), channel_id=1, source_target_pairs={{0,1},{1,2},{2,3},{3,0},{4,5},{5,6},{6,7},{7,4},{8,9},{9,10},{10,1... | collective-permute-start | bytes 589832 | tf_op jit(solution)/shard_map/ppermute | solution.py:21
  250.0 48.1 %collective-permute-start.6 = (f32[4,2,4,16,24,4]{4,3,5,2,1,0:T(8,128)}, f32[4,2,4,16,24,4]{4,3,5,2,1,0:T(8,128)}, u32[]{:S(2)}, u32[]{:S(2)}) collective-permute-start(f32[4,2,4,16,24,4]{4,3,5,2,1,0:T(8,128)} %get-tuple-element.24), channel_id=1, source_target_pairs={{1,0},{2,1},{3,2},{0,3},{5,4},{6,5},{7,6},{4,7},{9,8},{10,9},{11,1... | collective-permute-start | bytes 589832 | tf_op jit(solution)/shard_map/ppermute | solution.py:24
  304.1 62.2 %copy-start.6 = (f32[4,16,16,128]{3,2,1,0:T(8,128)S(1)}, f32[4,16,16,128]{3,2,1,0:T(8,128)}, u32[]{:S(2)}) copy-start(f32[4,16,16,128]{3,2,1,0:T(8,128)} %get-tuple-element.60) | copy-start | bytes 1572868
  304.1 62.2 %copy-start.8 = (f32[4,16,16,128]{3,2,1,0:T(8,128)S(1)}, f32[4,16,16,128]{3,2,1,0:T(8,128)}, u32[]{:S(2)}) copy-start(f32[4,16,16,128]{3,2,1,0:T(8,128)} %get-tuple-element.61) | copy-start | bytes 1572868
  366.4 36.0 %copy-start.23 = (f32[4]{0:T(128)S(1)}, f32[4]{0:T(128)}, u32[]{:S(2)}) copy-start(f32[4]{0:T(128)} %copy-done.22) | copy-start | bytes 52
  366.4 36.0 %copy-start.25 = (f32[4]{0:T(128)S(1)}, f32[4]{0:T(128)}, u32[]{:S(2)}) copy-start(f32[4]{0:T(128)} %copy-done.24) | copy-start | bytes 52
  366.4 36.0 %copy-start.27 = (f32[4]{0:T(128)S(1)}, f32[4]{0:T(128)}, u32[]{:S(2)}) copy-start(f32[4]{0:T(128)} %copy-done.26) | copy-start | bytes 52
  366.4 36.0 %copy-start.29 = (f32[4]{0:T(128)S(1)}, f32[4]{0:T(128)}, u32[]{:S(2)}) copy-start(f32[4]{0:T(128)} %copy-done.28) | copy-start | bytes 52
  366.4 36.0 %copy-start.30 = (f32[4]{0:T(128)S(1)}, f32[4]{0:T(128)}, u32[]{:S(2)}) copy-start(f32[4]{0:T(128)} %multiply_add_fusion.4) | copy-start | bytes 52
  366.4 36.1 %copy-start.7 = (f32[4,16,16,128]{3,2,1,0:T(8,128)S(1)}, f32[4,16,16,128]{3,2,1,0:T(8,128)}, u32[]{:S(2)}) copy-start(f32[4,16,16,128]{3,2,1,0:T(8,128)} %get-tuple-element.60) | copy-start | bytes 1572868
  366.4 36.1 %copy-start.9 = (f32[4,16,16,128]{3,2,1,0:T(8,128)S(1)}, f32[4,16,16,128]{3,2,1,0:T(8,128)}, u32[]{:S(2)}) copy-start(f32[4,16,16,128]{3,2,1,0:T(8,128)} %get-tuple-element.61) | copy-start | bytes 1572868
  (16 other events, 83.2 us)
Sparse Core Ops, SparseCore 0:
  428.4 53.3 reduce-scatter.1
where the time goes:
time: 499 us; the launch traced here: 492 us
  other arithmetic  173 us (35%)
  local copies, waits for them, and re-layouts  147 us (29%)
  blocking collectives  65.6 us (13%)
  waiting for transfers between devices  61.1 us (12%)
  matrix products  18.2 us (4%)
  between operations  15.3 us (3%)
  starting transfers between devices  11.2 us (2%)
    add x2, other arithmetic, apply_operator(): return -0.5 * laplace + potential * field  79.9 us
    concatenate x4, other arithmetic, padded_2(): block = jnp.concatenate([low, block, high], axis=dim)  55 us
    reduce_scatter x1, waiting for transfers between devices, per_device(): return lax.psum_scatter(terms, 'quad', scatter_dimension=3, tiled=True)  53.5 us
    psum x1, blocking collectives, per_device(): lax.psum((rho_local[0], rho_local[1], curv_local[0], curv_local[1]), ('py...  34.7 us
    psum x1, blocking collectives, per_device(): lax.psum((rho_part[0], rho_part[1], mixed_part[0], mixed_part[1]), ('py',...  30.9 us
    ppermute x4, local copies, waits for them, and re-layouts, padded_2(): lax.ppermute(lax.slice_in_dim(block, 0, width, axis=dim), axis, backward)  29.5 us
    ppermute x4, local copies, waits for them, and re-layouts, padded_2(): lax.ppermute(lax.slice_in_dim(block, block.shape[dim] - width, None, axis...  29.4 us
    concatenate x2, local copies, waits for them, and re-layouts, padded_2(): block = jnp.concatenate([low, block, high], axis=dim)  23.7 us
  transfers between devices with their start and end apart: 9, of which 3 were waited for; matrix products, arithmetic and copies ran while one was open for 26% of the time, Pallas kernels for 0%

commit v1 on v0

v1 whole, which is shorter than its diff:
```python
import functools
import math

import jax
import jax.numpy as jnp
import numpy as np
from jax import lax
from jax.experimental import pallas as pl
from jax.experimental.pallas import tpu as pltpu
from jax.sharding import PartitionSpec as P

QPTS = 8
MOMS = 4
REACH = 4
LANES = 128

stencil_weights = (-205.0 / 72.0, 8.0 / 5.0, -1.0 / 5.0, 8.0 / 315.0, -1.0 / 560.0)
DIAG = -1.5 * stencil_weights[0]
SIDE = tuple(-0.5 * w for w in stencil_weights)
HIGHEST = lax.Precision.HIGHEST


def dot(left, right, dims):
    return lax.dot_general(
        left, right, (dims, ((), ())), precision=HIGHEST, preferred_element_type=jnp.float32
    )


def band(shape, offset, signs, scale=1.0):
    step = offset + lax.broadcasted_iota(jnp.int32, shape, 0) - lax.broadcasted_iota(jnp.int32, shape, 1)
    out = jnp.zeros(shape, jnp.float32)
    for k in range(1, REACH + 1):
        for sign in signs:
            out = jnp.where(step == sign * k, scale * SIDE[k], out)
    return out


def edge_select(width):
    row = lax.broadcasted_iota(jnp.int32, (2 * REACH, width), 0)
    col = lax.broadcasted_iota(jnp.int32, (2 * REACH, width), 1)
    want = jnp.where(row < REACH, row, width - 2 * REACH + row)
    return jnp.where(col == want, 1.0, 0.0)


def pack_kernel(re_ref, im_ref, ylo_ref, yhi_ref, zlo_ref, zhi_ref):
    srcs, cx, ny, nz = re_ref.shape
    pick = edge_select(nz)
    for part, ref in enumerate((re_ref, im_ref)):
        for s in range(srcs):
            f = part * srcs + s
            ylo_ref[f] = ref[s, :, 0:REACH, :]
            yhi_ref[f] = ref[s, :, ny - REACH : ny, :]
            edges = dot(pick, ref[s].reshape(cx * ny, nz), ((1,), (1,)))
            zlo_ref[f * REACH : (f + 1) * REACH, :] = edges[0:REACH]
            zhi_ref[f * REACH : (f + 1) * REACH, :] = edges[REACH : 2 * REACH]


def inner_kernel(center_ref, re_ref, im_ref, pot_ref, out_ref, pad_ref):
    srcs, cx, ny, nz = re_ref.shape
    shift = DIAG - center_ref[0]
    matrix = band((nz, nz), 0, (1, -1))
    zero = jnp.zeros((cx, 8, nz), jnp.float32)
    pad_ref[:, 0:8, :] = zero
    pad_ref[:, 8 + ny : 16 + ny, :] = zero
    for part, ref in enumerate((re_ref, im_ref)):

        def field(s, _, ref=ref, part=part):
            f = part * srcs + s
            own = ref[s]
            pad_ref[:, 8 : 8 + ny, :] = own
            out_ref[f] = dot(own.reshape(cx * ny, nz), matrix, ((1,), (0,))).reshape(cx, ny, nz)
            for x in range(cx):
                total = out_ref[f, x] + (pot_ref[x] + shift) * ref[s, x]
                for k in range(1, REACH + 1):
                    beside = ref[s, (x + k) % cx] + ref[s, (x - k) % cx]
                    beside = beside + pad_ref[x, 8 + k : 8 + k + ny, :]
                    beside = beside + pad_ref[x, 8 - k : 8 - k + ny, :]
                    total = total + SIDE[k] * beside
                out_ref[f, x] = total
            return 0

        lax.fori_loop(0, srcs, field, 0)


def border_kernel(inner_ref, ylo_ref, yhi_ref, zlo_ref, zhi_ref, out_ref, oy_ref, oz_ref, own_ref, pad_ref):
    fields, cx, ny, nz = inner_ref.shape
    below = band((REACH, nz), -REACH, (1, -1))
    above = band((REACH, nz), nz, (1, -1))
    pick = edge_select(nz)
    zero = jnp.zeros((cx, 16, nz), jnp.float32)
    pad_ref[0] = zero
    pad_ref[1] = zero

    def field(f, _):
        at = pl.multiple_of(f * REACH, REACH)
        fix = dot(zlo_ref[f], below, ((0,), (0,))) + dot(zhi_ref[f], above, ((0,), (0,)))
        out_ref[f] = inner_ref[f] + fix.reshape(cx, ny, nz)
        pad_ref[0, :, 8 - REACH : 8, :] = ylo_ref[f]
        pad_ref[1, :, 8 : 8 + REACH, :] = yhi_ref[f]
        for x in range(cx):
            low = out_ref[f, x, 0:8, :]
            high = out_ref[f, x, ny - 8 : ny, :]
            for k in range(1, REACH + 1):
                low = low + SIDE[k] * pad_ref[0, x, 8 - k : 16 - k, :]
                high = high + SIDE[k] * pad_ref[1, x, k : 8 + k, :]
            out_ref[f, x, 0:8, :] = low
            out_ref[f, x, ny - 8 : ny, :] = high
        oy_ref[f] = out_ref[f, :, 0:REACH, :]
        edges = dot(pick, out_ref[f].reshape(cx * ny, nz), ((1,), (1,)))
        oz_ref[f] = edges[0:REACH]
        own_ref[f] = edges[REACH : 2 * REACH]
        return 0

    lax.fori_loop(0, fields, field, 0)


def fold(value):
    return jnp.sum(value, axis=0, keepdims=True)


def sums_kernel(center_ref, re_ref, im_ref, pot_ref, h_ref, acc_ref, step_ref):
    srcs, cx, ny, nz = re_ref.shape
    shift = DIAG - center_ref[0]
    matrix = band((nz, nz), 0, (1,), 2.0)
    row = lax.broadcasted_iota(jnp.int32, (ny, nz), 0)
    inside = [row < ny - k for k in range(REACH + 1)]
    for s in range(srcs):
        for part in range(2):
            f = part * srcs + s
            step_ref[part] = dot(h_ref[f].reshape(cx * ny, nz), matrix, ((1,), (0,))).reshape(cx, ny, nz)
        total = [jnp.zeros((ny, nz), jnp.float32) for _ in range(8)]
        for x in range(cx):
            local = pot_ref[x] + shift
            br, bi = re_ref[s, x], im_ref[s, x]
            h, g = [], []
            for part in range(2):
                f = part * srcs + s
                own = h_ref[f, x]
                image = step_ref[part, x] + local * own
                for k in range(1, REACH + 1):
                    up = jnp.where(inside[k], pltpu.roll(own, ny - k, 0), 0.0)
                    image = image + (2.0 * SIDE[k]) * (h_ref[f, (x + k) % cx] + up)
                h.append(own)
                g.append(image)
            terms = (
                br * br - bi * bi,
                2.0 * (br * bi),
                br * h[0] - bi * h[1],
                br * h[1] + bi * h[0],
                h[0] * h[0] - h[1] * h[1],
                2.0 * (h[0] * h[1]),
                h[0] * g[0] - h[1] * g[1],
                h[0] * g[1] + h[1] * g[0],
            )
            total = [t + v for t, v in zip(total, terms)]
        for i in range(8):
            acc_ref[i * srcs + s : i * srcs + s + 1, :] = fold(total[i])


def finish_kernel(acc_ref, h_ref, own_ref, yhi_ref, zhi_ref, out_ref, pad_ref):
    fields, cx, ny, nz = h_ref.shape
    srcs = fields // 2
    i = lax.broadcasted_iota(jnp.int32, (REACH, REACH), 0)
    j = lax.broadcasted_iota(jnp.int32, (REACH, REACH), 1)
    mix = jnp.zeros((REACH, REACH), jnp.float32)
    for k in range(1, REACH + 1):
        mix = jnp.where(j - i + REACH == k, 2.0 * SIDE[k], mix)
    out_ref[...] = acc_ref[...]
    pad_ref[...] = jnp.zeros(pad_ref.shape, jnp.float32)
    for s in range(srcs):
        edge = [own_ref[part * srcs + s] for part in range(2)]
        far = [dot(mix, zhi_ref[part * srcs + s], ((1,), (0,))) for part in range(2)]
        both = (edge[0] * far[0] - edge[1] * far[1], edge[0] * far[1] + edge[1] * far[0])
        sides = []
        for c in range(2):
            flat = fold(both[c])
            width = flat.shape[1]
            sides.append(sum(flat[:, at : at + nz] for at in range(0, width, nz)))
        total = [jnp.zeros((8, nz), jnp.float32) for _ in range(2)]
        for part in range(2):
            pad_ref[part, :, 8 : 8 + REACH, :] = yhi_ref[part * srcs + s]
        for x in range(cx):
            h = [h_ref[part * srcs + s, x, ny - 8 : ny, :] for part in range(2)]
            g = []
            for part in range(2):
                image = (2.0 * SIDE[1]) * pad_ref[part, x, 1:9, :]
                for k in range(2, REACH + 1):
                    image = image + (2.0 * SIDE[k]) * pad_ref[part, x, k : 8 + k, :]
                g.append(image)
            total[0] = total[0] + (h[0] * g[0] - h[1] * g[1])
            total[1] = total[1] + (h[0] * g[1] + h[1] * g[0])
        for c in range(2):
            at = (6 + c) * srcs + s
            out_ref[at : at + 1, :] = out_ref[at : at + 1, :] + fold(total[c]) + sides[c]


def complex_mul(left, right):
    return (left[0] * right[0] - left[1] * right[1], left[0] * right[1] + left[1] * right[0])


def complex_div(left, right):
    norm_sq = right[0] * right[0] + right[1] * right[1]
    return (
        (left[0] * right[0] + left[1] * right[1]) / norm_sq,
        (left[1] * right[0] - left[0] * right[1]) / norm_sq,
    )


def phase_table():
    lane = np.arange(LANES)
    angle = 2.0 * math.pi * (lane % QPTS + 0.5) / QPTS
    rows = [np.cos(angle), np.sin(angle)]
    for k in range(1, MOMS + 1):
        rows.append(np.where(lane < QPTS, np.cos(k * angle), 0.0) / QPTS)
        rows.append(np.where(lane < QPTS, np.sin(k * angle), 0.0) / QPTS)
    while len(rows) % 8:
        rows.append(np.zeros(LANES))
    return np.stack(rows).astype(np.float32)


def output_kernel(quad_ref, radius_ref, tot_ref, table_ref, re_ref, im_ref, hr_ref, hi_ref, out_ref, coef_ref):
    srcs = tot_ref.shape[0] // 8
    s = pl.program_id(0)

    @pl.when(s == 0)
    def _():
        radius = radius_ref[0]
        summed = jnp.sum(tot_ref[...], axis=1, keepdims=True)
        wide = jnp.broadcast_to(summed, (8 * srcs, LANES))
        nu = [
            (wide[2 * k * srcs : (2 * k + 1) * srcs], wide[(2 * k + 1) * srcs : (2 * k + 2) * srcs])
            for k in range(4)
        ]
        shape = (srcs, LANES)
        zeta = (
            jnp.broadcast_to(radius * table_ref[0:1, :], shape),
            jnp.broadcast_to(radius * table_ref[1:2, :], shape),
        )
        scaled = complex_mul(zeta, nu[0])
        alpha_first = complex_div(nu[0], (scaled[0] - nu[1][0], scaled[1] - nu[1][1]))
        mean = complex_div(nu[1], nu[0])
        t = complex_mul(mean, nu[1])
        spread2 = (nu[2][0] - t[0], nu[2][1] - t[1])
        t = complex_mul(mean, (nu[2][0] + spread2[0], nu[2][1] + spread2[1]))
        spread3 = (nu[3][0] - t[0], nu[3][1] - t[1])
        square = complex_mul(alpha_first, alpha_first)
        rho_next = complex_mul(square, spread2)
        beta = complex_div(rho_next, nu[0])
        first = complex_mul(zeta, rho_next)
        second = complex_mul(square, spread3)
        third = complex_div(complex_mul(beta, rho_next), alpha_first)
        alpha_next = complex_div(
            rho_next, (first[0] - second[0] - third[0], first[1] - second[1] - third[1])
        )
        t = complex_mul(alpha_first, mean)
        carried = complex_mul(alpha_next, (beta[0] - t[0], beta[1] - t[1]))
        on_source = (alpha_first[0] + carried[0], alpha_first[1] + carried[1])
        on_image = complex_mul(alpha_next, alpha_first)
        for k in range(MOMS):
            weight = (
                jnp.broadcast_to(radius * table_ref[2 + 2 * k : 3 + 2 * k, :], shape),
                jnp.broadcast_to(radius * table_ref[3 + 2 * k : 4 + 2 * k, :], shape),
            )
            for n, value in enumerate((on_source, on_image)):
                both = complex_mul(weight, value)
                for c in range(2):
                    column = jnp.sum(both[c], axis=1, keepdims=True)
                    coef_ref[4 * k + 2 * n + c, 0:srcs, :] = jnp.broadcast_to(column, shape)

    planes = re_ref.shape[1]
    plane = re_ref.shape[2:]
    for k in range(MOMS):
        c = [jnp.broadcast_to(coef_ref[4 * k + n, pl.ds(s, 1), :], plane) for n in range(4)]
        for x in range(planes):
            br, bi, hr, hi = re_ref[0, x], im_ref[0, x], hr_ref[0, x], hi_ref[0, x]
            out_ref[k, 0, 0, x] = c[0] * br - c[1] * bi + (c[2] * hr - c[3] * hi)
            out_ref[k, 1, 0, x] = c[0] * bi + c[1] * br + (c[2] * hi + c[3] * hr)


def ring(count, step):
    return [(i, (i + step) % count) for i in range(count)]


def total_over(value, axis):
    count = lax.axis_size(axis)
    if count & (count - 1):
        return lax.psum(value, axis)
    bit = 1
    while bit < count:
        value = value + lax.ppermute(value, axis, [(i, i ^ bit) for i in range(count)])
        bit *= 2
    return value


VMEM = pl.BlockSpec(memory_space=pltpu.VMEM)
SMEM = pl.BlockSpec(memory_space=pltpu.SMEM)


def shaped(*dims):
    return jax.ShapeDtypeStruct(dims, jnp.float32)


def cost(flops, nbytes):
    return pl.CostEstimate(flops=flops, bytes_accessed=nbytes, transcendentals=0)


def per_device(source_real, source_imag, potential, center, radius):
    srcs, cx, ny, nz = source_real.shape
    fields = 2 * srcs
    cells = cx * ny * nz
    py, pz, quads = lax.axis_size("py"), lax.axis_size("pz"), lax.axis_size("quad")

    ylo, yhi, zlo, zhi = pl.pallas_call(
        pack_kernel,
        out_shape=(
            shaped(fields, cx, REACH, nz),
            shaped(fields, cx, REACH, nz),
            shaped(fields * REACH, cx * ny),
            shaped(fields * REACH, cx * ny),
        ),
        in_specs=[VMEM] * 2,
        out_specs=(VMEM,) * 4,
        name="pack",
    )(source_real, source_imag)
    y_above = lax.ppermute(ylo, "py", ring(py, -1))
    y_below = lax.ppermute(yhi, "py", ring(py, 1))
    z_above = lax.ppermute(zlo, "pz", ring(pz, -1)).reshape(fields, REACH, cx * ny)
    z_below = lax.ppermute(zhi, "pz", ring(pz, 1)).reshape(fields, REACH, cx * ny)

    inner = pl.pallas_call(
        inner_kernel,
        out_shape=shaped(fields, cx, ny, nz),
        in_specs=[SMEM] + [VMEM] * 3,
        out_specs=VMEM,
        scratch_shapes=[pltpu.VMEM((cx, ny + 16, nz), jnp.float32)],
        cost_estimate=cost(fields * cells * 60, fields * cells * 12),
        name="inner",
    )(center, source_real, source_imag, potential)

    image, h_ylo, h_zlo, h_own = pl.pallas_call(
        border_kernel,
        out_shape=(
            shaped(fields, cx, ny, nz),
            shaped(fields, cx, REACH, nz),
            shaped(fields, REACH, cx * ny),
            shaped(fields, REACH, cx * ny),
        ),
        in_specs=[VMEM] * 5,
        out_specs=(VMEM,) * 4,
        scratch_shapes=[pltpu.VMEM((2, cx, 16, nz), jnp.float32)],
        name="border",
    )(inner, y_below, y_above, z_below, z_above)
    h_yabove = lax.ppermute(h_ylo, "py", ring(py, -1))
    h_zabove = lax.ppermute(h_zlo, "pz", ring(pz, -1))

    partial = pl.pallas_call(
        sums_kernel,
        out_shape=shaped(8 * srcs, nz),
        in_specs=[SMEM] + [VMEM] * 4,
        out_specs=VMEM,
        scratch_shapes=[pltpu.VMEM((2, cx, ny, nz), jnp.float32)],
        cost_estimate=cost(fields * cells * 60, fields * cells * 12),
        name="sums",
    )(center, source_real, source_imag, potential, image)

    partial = pl.pallas_call(
        finish_kernel,
        out_shape=shaped(8 * srcs, nz),
        in_specs=[VMEM] * 5,
        out_specs=VMEM,
        scratch_shapes=[pltpu.VMEM((2, cx, 16, nz), jnp.float32)],
        name="finish",
    )(partial, image, h_own, h_yabove, h_zabove)

    total = total_over(total_over(partial, "py"), "pz")

    planes = cx // quads
    quad = lax.axis_index("quad").reshape(1)
    table = jnp.asarray(phase_table())
    own = lambda shift: pl.BlockSpec((1, planes, ny, nz), lambda s, q: (s + shift, q[0], 0, 0))
    return pl.pallas_call(
        output_kernel,
        out_shape=shaped(MOMS, 2, srcs, planes, ny, nz),
        grid_spec=pltpu.PrefetchScalarGridSpec(
            num_scalar_prefetch=1,
            grid=(srcs,),
            in_specs=[
                SMEM,
                pl.BlockSpec(total.shape, lambda s, q: (0, 0)),
                pl.BlockSpec(table.shape, lambda s, q: (0, 0)),
                own(0),
                own(0),
                own(0),
                own(srcs),
            ],
            out_specs=pl.BlockSpec((MOMS, 2, 1, planes, ny, nz), lambda s, q: (0, 0, s, 0, 0, 0)),
            scratch_shapes=[pltpu.VMEM((4 * MOMS, 8, LANES), jnp.float32)],
        ),
        compiler_params=pltpu.CompilerParams(dimension_semantics=("arbitrary",)),
        name="output",
    )(quad, radius, total, table, source_real, source_imag, image, image)


def solution(mesh):
    in_specs = (P(None, None, "py", "pz"), P(None, None, "py", "pz"), P(None, "py", "pz"), P(), P())
    out_specs = P(None, None, None, "quad", "py", "pz")
    return jax.shard_map(
        per_device, mesh=mesh, in_specs=in_specs, out_specs=out_specs, check_vma=False
    )
```

time: 499 us -> 54.8 us (0.11); the launches traced: 492 us -> 54.3 us
  other arithmetic: 173 us -> 1.33 us
  local copies, waits for them, and re-layouts: 147 us -> 3.33 us
  blocking collectives: 65.6 us -> 0 us
  waiting for transfers between devices: 61.1 us -> 10.7 us
  Pallas kernels: 0 us -> 26.6 us
  matrix products: 18.2 us -> 0 us
  between operations: 15.3 us -> 1.34 us
    add x4, other arithmetic: 83.3 us -> 1.33 us  [total_over(): value + lax.ppermute(value, axis, [(i, i ^ bit) for i in range(count)])]
    psum x2 -> x0, blocking collectives: 65.6 us -> none  [the longest x1 34.7 us: per_device(): lax.psum((rho_local[0], rho_local[1], curv_local[0], curv_local[1]), ('py...]
    ppermute x8 -> x0, local copies, waits for them, and re-layouts: 58.9 us -> none  [the longest x4 29.5 us: padded_2(): lax.ppermute(lax.slice_in_dim(block, 0, width, axis=dim), axis, backward)]
    concatenate x4 -> x0, other arithmetic: 55 us -> none  [padded_2(): block = jnp.concatenate([low, block, high], axis=dim)]
    reduce_scatter x1 -> x0, waiting for transfers between devices: 53.5 us -> none  [per_device(): return lax.psum_scatter(terms, 'quad', scatter_dimension=3, tiled=True)]
    slice x27 -> x0, local copies, waits for them, and re-layouts: 35.9 us -> none  [the longest x22 23.7 us: apply_operator(): beside_all = jnp.roll(field, offset, 3) + jnp.roll(field, -offset, 3)]
    pallas_call x0 -> x6, Pallas kernels: none -> 26.6 us  [the longest x1 9.02 us: per_device(): pl.pallas_call(border_kernel, out_shape=(shaped(fields, cx, ny, nz), shap...]
    another operation x12 -> x0, other arithmetic: 26 us -> none  [the longest x10 22.6 us: per_device(): hres = apply_operator(jnp.stack(residual, 1), potential)]
  transfers between devices with their start and end apart: 9 -> 10, of which waited for: 3 -> 4; matrix products, arithmetic and copies ran while one was open for 26% -> 2% of each run, Pallas kernels for 0% -> 16%
where the time goes in v1:
time: 54.8 us; the launch traced here: 54.3 us
  Pallas kernels  26.6 us (49%)
  starting transfers between devices  11 us (20%)
  waiting for transfers between devices  10.7 us (20%)
  local copies, waits for them, and re-layouts  3.33 us (6%)
  between operations  1.34 us (2%)
  other arithmetic  1.33 us (2%)
    ppermute x4, waiting for transfers between devices, total_over(): lax.ppermute(value, axis, [(i, i ^ bit) for i in range(count)])  10.7 us
    pallas_call x1, Pallas kernels, per_device(): pl.pallas_call(border_kernel, out_shape=(shaped(fields, cx, ny, nz), shap...  9.02 us
    pallas_call x1, Pallas kernels, per_device(): pl.pallas_call(inner_kernel, out_shape=shaped(fields, cx, ny, nz), in_spe...  4.53 us
    pallas_call x1, Pallas kernels, per_device(): pl.pallas_call(sums_kernel, out_shape=shaped(8 * srcs, nz), in_specs=[SME...  4.08 us
    pallas_call x1, Pallas kernels, per_device(): pl.pallas_call(output_kernel, out_shape=shaped(MOMS, 2, srcs, planes, ny,...  3.95 us
    pallas_call x1, Pallas kernels, per_device(): pl.pallas_call(pack_kernel, out_shape=(shaped(fields, cx, REACH, nz), sha...  2.84 us
    ppermute x1, starting transfers between devices, per_device(): lax.ppermute(zhi, 'pz', ring(pz, 1)).reshape(fields, REACH, cx * ny)  2.36 us
    pallas_call x1, Pallas kernels, per_device(): pl.pallas_call(finish_kernel, out_shape=shaped(8 * srcs, nz), in_specs=[V...  2.2 us
  transfers between devices with their start and end apart: 10, of which 4 were waited for; matrix products, arithmetic and copies ran while one was open for 2% of the time, Pallas kernels for 16%

profile of v1, /device:TPU:0, one launch (start us, length us, event | category | flops | bytes accessed | tf_op | source)
XLA Modules:
  0.0 54.3 jit_solution(299158527316490328)
XLA Ops:
  0.0 2.8 %pack.1 = (f32[8,16,4,128]{3,2,1,0:T(4,128)}, f32[8,16,4,128]{3,2,1,0:T(4,128)}, f32[32,256]{1,0:T(8,128)}, f32[32,256]{1,0:T(8,128)}) custom-call(f32[4,16,16,128]{3,2,1,0:T(8,128)} %re_ref.7, f32[4,16,16,128]{3,2,1,0:T(8,128)} %im_ref.7), custom_call_target="tpu_custom_call" | custom-call | tf_op jit(solution)/shard_map/pack/pallas_call | solution.py:313
  2.8 0.5 collective-permute-start
  3.3 1.9 %collective-permute-start.1 = (f32[8,16,4,128]{3,2,1,0:T(4,128)}, f32[8,16,4,128]{3,2,1,0:T(4,128)S(1)}, u32[]{:S(2)}, u32[]{:S(2)}) collective-permute-start(f32[8,16,4,128]{3,2,1,0:T(4,128)} %get-tuple-element.14), channel_id=1, source_target_pairs={{0,12},{4,0},{8,4},{12,8},{1,13},{5,1},{9,5},{13,9},{2,14},{6,2},{... | collective-permute-start | bytes 786440 | tf_op jit(solution)/shard_map/ppermute | solution.py:325
  5.3 2.4 %collective-permute-start.2 = (f32[32,256]{1,0:T(8,128)}, f32[32,256]{1,0:T(8,128)S(1)}, u32[]{:S(2)}, u32[]{:S(2)}) collective-permute-start(f32[32,256]{1,0:T(8,128)} %get-tuple-element.15), channel_id=1, source_target_pairs={{0,1},{1,2},{2,3},{3,0},{4,5},{5,6},{6,7},{7,4},{8,9},{9,10},{10,1... | collective-permute-start | bytes 98312 | tf_op jit(solution)/shard_map/ppermute | solution.py:328
  7.6 2.0 %collective-permute-start.3 = (f32[32,256]{1,0:T(8,128)}, f32[32,256]{1,0:T(8,128)S(1)}, u32[]{:S(2)}, u32[]{:S(2)}) collective-permute-start(f32[32,256]{1,0:T(8,128)} %get-tuple-element.16), channel_id=1, source_target_pairs={{0,3},{1,0},{2,1},{3,2},{4,7},{5,4},{6,5},{7,6},{8,11},{9,8},{10,9... | collective-permute-start | bytes 98312 | tf_op jit(solution)/shard_map/ppermute | solution.py:327
  10.3 4.5 %inner.1.inner_ref = f32[8,16,16,128]{3,2,1,0:T(8,128)} custom-call(f32[1]{0:T(128)S(6)} %copy.7.center_ref, f32[4,16,16,128]{3,2,1,0:T(8,128)} %re_ref.7, f32[4,16,16,128]{3,2,1,0:T(8,128)} %im_ref.7, f32[16,16,128]{2,1,0:T(8,128)} %pot_ref.3), custom_call_target="tpu_custom_call" | custom-call | flops 15728640 | bytes 3145728 | tf_op jit(solution)/shard_map/inner/pallas_call | solution.py:330
  14.8 0.6 %reshape.10.zlo_ref = f32[8,4,256]{2,1,0:T(4,128)} reshape(f32[32,256]{1,0:T(8,128)S(1)} %collective-permute-done.2) | data formatting | bytes 65536 | tf_op jit(solution)/shard_map/reshape | solution.py:328
  15.5 0.6 %reshape.11.zhi_ref = f32[8,4,256]{2,1,0:T(4,128)} reshape(f32[32,256]{1,0:T(8,128)S(1)} %collective-permute-done.3) | data formatting | bytes 65536 | tf_op jit(solution)/shard_map/reshape | solution.py:327
  16.1 0.7 %copy-done = f32[8,16,4,128]{3,2,1,0:T(4,128)} copy-done((f32[8,16,4,128]{3,2,1,0:T(4,128)}, f32[8,16,4,128]{3,2,1,0:T(4,128)S(1)}, u32[]{:S(2)}) %copy-start) | copy-done | bytes 262168
  16.8 0.7 %copy-done.1 = f32[8,16,4,128]{3,2,1,0:T(4,128)} copy-done((f32[8,16,4,128]{3,2,1,0:T(4,128)}, f32[8,16,4,128]{3,2,1,0:T(4,128)S(1)}, u32[]{:S(2)}) %copy-start.1) | copy-done | bytes 262168
  17.5 9.0 %border.1 = (f32[8,16,16,128]{3,2,1,0:T(8,128)}, f32[8,16,4,128]{3,2,1,0:T(4,128)}, f32[8,4,256]{2,1,0:T(4,128)}, f32[8,4,256]{2,1,0:T(4,128)}) custom-call(f32[8,16,16,128]{3,2,1,0:T(8,128)} %inner.1.inner_ref, f32[8,16,4,128]{3,2,1,0:T(4,128)} %copy-done, f32[8,16,4,128]{3,2,1,0:T(4,128)} %copy-done.1, f32[8,4,256]{2,1,0:T(4,128)} %reshape.10.zlo_ref, ...), custom_call_target="tpu_custom_call" | custom-call | tf_op jit(solution)/shard_map/border/pallas_call | solution.py:340
  26.5 2.0 %collective-permute-start.5 = (f32[8,4,256]{2,1,0:T(4,128)}, f32[8,4,256]{2,1,0:T(4,128)S(1)}, u32[]{:S(2)}, u32[]{:S(2)}) collective-permute-start(f32[8,4,256]{2,1,0:T(4,128)} %get-tuple-element.20), channel_id=1, source_target_pairs={{0,3},{1,0},{2,1},{3,2},{4,7},{5,4},{6,5},{7,6},{8,11},{9,8},{10,9... | collective-permute-start | bytes 98312 | tf_op jit(solution)/shard_map/ppermute | solution.py:354
  28.5 4.1 %sums.1.acc_ref = f32[32,128]{1,0:T(8,128)} custom-call(f32[1]{0:T(128)S(6)} %copy.7.center_ref, f32[4,16,16,128]{3,2,1,0:T(8,128)} %re_ref.7, f32[4,16,16,128]{3,2,1,0:T(8,128)} %im_ref.7, f32[16,16,128]{2,1,0:T(8,128)} %pot_ref.3, f32[8,16,16,128]{3,2,1,0:T(8,128)} %get-tuple-element.17.h_ref.hr_ref.hi_ref), custom_call_target="tpu_custom_call" | custom-call | flops 15728640 | bytes 3145728 | tf_op jit(solution)/shard_map/sums/pallas_call | solution.py:356
  32.6 0.6 %copy-done.3 = f32[8,4,256]{2,1,0:T(4,128)} copy-done((f32[8,4,256]{2,1,0:T(4,128)}, f32[8,4,256]{2,1,0:T(4,128)S(1)}, u32[]{:S(2)}) %copy-start.3) | copy-done | bytes 32792
  33.3 2.2 %finish.1 = f32[32,128]{1,0:T(8,128)} custom-call(f32[32,128]{1,0:T(8,128)} %sums.1.acc_ref, f32[8,16,16,128]{3,2,1,0:T(8,128)} %get-tuple-element.17.h_ref.hr_ref.hi_ref, f32[8,4,256]{2,1,0:T(4,128)} %get-tuple-element.18.own_ref, f32[8,16,4,128]{3,2,1,0:T(4,128)} %copy-done.2, f32[8,4,256]{2,1,0:T(4,128)} %copy-done.3), custom_call_target="tpu_custom_call" | custom-call | tf_op jit(solution)/shard_map/finish/pallas_call | solution.py:366
  35.8 1.2 %collective-permute-done.6 = f32[32,128]{1,0:T(8,128)S(1)} collective-permute-done((f32[32,128]{1,0:T(8,128)}, f32[32,128]{1,0:T(8,128)S(1)}, u32[]{:S(2)}, u32[]{:S(2)}) %collective-permute-start.6) | collective-permute-done | bytes 16416 | tf_op jit(solution)/shard_map/ppermute | solution.py:290
  36.9 0.7 %add.12 = f32[32,128]{1,0:T(8,128)S(1)} add(f32[32,128]{1,0:T(8,128)} %finish.1, f32[32,128]{1,0:T(8,128)S(1)} %collective-permute-done.6) | non-fusion elementwise | flops 4096 | bytes 49152 | tf_op jit(solution)/shard_map/add | solution.py:290
  37.7 1.5 %collective-permute-start.7 = (f32[32,128]{1,0:T(8,128)S(1)}, f32[32,128]{1,0:T(8,128)S(1)}, u32[]{:S(2)}, u32[]{:S(2)}) collective-permute-start(f32[32,128]{1,0:T(8,128)S(1)} %add.12), channel_id=1, source_target_pairs={{0,8},{4,12},{8,0},{12,4},{1,9},{5,13},{9,1},{13,5},{2,10},{6,14},... | collective-permute-start | bytes 49160 | tf_op jit(solution)/shard_map/ppermute | solution.py:290
  39.2 2.2 %collective-permute-done.7 = f32[32,128]{1,0:T(8,128)S(1)} collective-permute-done((f32[32,128]{1,0:T(8,128)S(1)}, f32[32,128]{1,0:T(8,128)S(1)}, u32[]{:S(2)}, u32[]{:S(2)}) %collective-permute-start.7) | collective-permute-done | bytes 16416 | tf_op jit(solution)/shard_map/ppermute | solution.py:290
  41.4 3.7 %collective-permute-done.8 = f32[32,128]{1,0:T(8,128)S(1)} collective-permute-done((f32[32,128]{1,0:T(8,128)S(1)}, f32[32,128]{1,0:T(8,128)S(1)}, u32[]{:S(2)}, u32[]{:S(2)}) %collective-permute-start.8) | collective-permute-done | bytes 16416 | tf_op jit(solution)/shard_map/ppermute | solution.py:290
  45.1 0.4 collective-permute-start.9
  46.2 3.5 %collective-permute-done.9 = f32[32,128]{1,0:T(8,128)S(1)} collective-permute-done((f32[32,128]{1,0:T(8,128)S(1)}, f32[32,128]{1,0:T(8,128)S(1)}, u32[]{:S(2)}, u32[]{:S(2)}) %collective-permute-start.9) | collective-permute-done | bytes 16416 | tf_op jit(solution)/shard_map/ppermute | solution.py:290
  49.8 0.6 %add.15.tot_ref = f32[32,128]{1,0:T(8,128)} add(f32[32,128]{1,0:T(8,128)S(1)} %add.14, f32[32,128]{1,0:T(8,128)S(1)} %collective-permute-done.9) | non-fusion elementwise | flops 4096 | bytes 49152 | tf_op jit(solution)/shard_map/add | solution.py:290
  50.4 4.0 %output.1 = f32[4,2,4,8,16,128]{5,4,3,2,1,0:T(8,128)} custom-call(s32[1]{0:T(128)} %bitcast.quad_ref, f32[1]{0:T(128)S(6)} %copy.8.radius_ref, f32[32,128]{1,0:T(8,128)} %add.15.tot_ref, f32[16,128]{1,0:T(8,128)} %constant.8.clone.table_ref, f32[4,16,16,128]{3,2,1,0:T(8,128)} %re_ref.7, f32[4,16,16,128]{3,2,1,0:T(8,128)} %im_ref.7, ...), custom_call_target="tpu_custom_call" | custom-call | tf_op jit(solution)/shard_map/output/pallas_call | solution.py:381
  (16 shorter events, 0.4 us)
Async XLA Ops:
  2.8 13.2 %collective-permute-start = (f32[8,16,4,128]{3,2,1,0:T(4,128)}, f32[8,16,4,128]{3,2,1,0:T(4,128)S(1)}, u32[]{:S(2)}, u32[]{:S(2)}) collective-permute-start(f32[8,16,4,128]{3,2,1,0:T(4,128)} %get-tuple-element.13), channel_id=1, source_target_pairs={{0,4},{4,8},{8,12},{12,0},{1,5},{5,9},{9,13},{13,1},{2,6},{6,10},{... | collective-permute-start | bytes 786440 | tf_op jit(solution)/shard_map/ppermute | solution.py:326
  3.3 12.8 %collective-permute-start.1 = (f32[8,16,4,128]{3,2,1,0:T(4,128)}, f32[8,16,4,128]{3,2,1,0:T(4,128)S(1)}, u32[]{:S(2)}, u32[]{:S(2)}) collective-permute-start(f32[8,16,4,128]{3,2,1,0:T(4,128)} %get-tuple-element.14), channel_id=1, source_target_pairs={{0,12},{4,0},{8,4},{12,8},{1,13},{5,1},{9,5},{13,9},{2,14},{6,2},{... | collective-permute-start | bytes 786440 | tf_op jit(solution)/shard_map/ppermute | solution.py:325
  5.3 9.6 %collective-permute-start.2 = (f32[32,256]{1,0:T(8,128)}, f32[32,256]{1,0:T(8,128)S(1)}, u32[]{:S(2)}, u32[]{:S(2)}) collective-permute-start(f32[32,256]{1,0:T(8,128)} %get-tuple-element.15), channel_id=1, source_target_pairs={{0,1},{1,2},{2,3},{3,0},{4,5},{5,6},{6,7},{7,4},{8,9},{9,10},{10,1... | collective-permute-start | bytes 98312 | tf_op jit(solution)/shard_map/ppermute | solution.py:328
  7.6 7.8 %collective-permute-start.3 = (f32[32,256]{1,0:T(8,128)}, f32[32,256]{1,0:T(8,128)S(1)}, u32[]{:S(2)}, u32[]{:S(2)}) collective-permute-start(f32[32,256]{1,0:T(8,128)} %get-tuple-element.16), channel_id=1, source_target_pairs={{0,3},{1,0},{2,1},{3,2},{4,7},{5,4},{6,5},{7,6},{8,11},{9,8},{10,9... | collective-permute-start | bytes 98312 | tf_op jit(solution)/shard_map/ppermute | solution.py:327
  16.1 0.7 %copy-start = (f32[8,16,4,128]{3,2,1,0:T(4,128)}, f32[8,16,4,128]{3,2,1,0:T(4,128)S(1)}, u32[]{:S(2)}) copy-start(f32[8,16,4,128]{3,2,1,0:T(4,128)S(1)} %collective-permute-done.ylo_ref) | copy-start | bytes 786436
  16.8 0.7 %copy-start.1 = (f32[8,16,4,128]{3,2,1,0:T(4,128)}, f32[8,16,4,128]{3,2,1,0:T(4,128)S(1)}, u32[]{:S(2)}) copy-start(f32[8,16,4,128]{3,2,1,0:T(4,128)S(1)} %collective-permute-done.1.yhi_ref) | copy-start | bytes 786436
  26.5 6.1 %collective-permute-start.4 = (f32[8,16,4,128]{3,2,1,0:T(4,128)}, f32[8,16,4,128]{3,2,1,0:T(4,128)S(1)}, u32[]{:S(2)}, u32[]{:S(2)}) collective-permute-start(f32[8,16,4,128]{3,2,1,0:T(4,128)} %get-tuple-element.19), channel_id=1, source_target_pairs={{0,12},{4,0},{8,4},{12,8},{1,13},{5,1},{9,5},{13,9},{2,14},{6,2},{... | collective-permute-start | bytes 786440 | tf_op jit(solution)/shard_map/ppermute | solution.py:353
  26.5 6.1 %collective-permute-start.5 = (f32[8,4,256]{2,1,0:T(4,128)}, f32[8,4,256]{2,1,0:T(4,128)S(1)}, u32[]{:S(2)}, u32[]{:S(2)}) collective-permute-start(f32[8,4,256]{2,1,0:T(4,128)} %get-tuple-element.20), channel_id=1, source_target_pairs={{0,3},{1,0},{2,1},{3,2},{4,7},{5,4},{6,5},{7,6},{8,11},{9,8},{10,9... | collective-permute-start | bytes 98312 | tf_op jit(solution)/shard_map/ppermute | solution.py:354
  32.6 0.6 %copy-start.3 = (f32[8,4,256]{2,1,0:T(4,128)}, f32[8,4,256]{2,1,0:T(4,128)S(1)}, u32[]{:S(2)}) copy-start(f32[8,4,256]{2,1,0:T(4,128)S(1)} %collective-permute-done.5.zhi_ref) | copy-start | bytes 98308
  32.6 0.7 %copy-start.2 = (f32[8,16,4,128]{3,2,1,0:T(4,128)}, f32[8,16,4,128]{3,2,1,0:T(4,128)S(1)}, u32[]{:S(2)}) copy-start(f32[8,16,4,128]{3,2,1,0:T(4,128)S(1)} %collective-permute-done.4.yhi_ref) | copy-start | bytes 786436
  35.5 1.4 %collective-permute-start.6 = (f32[32,128]{1,0:T(8,128)}, f32[32,128]{1,0:T(8,128)S(1)}, u32[]{:S(2)}, u32[]{:S(2)}) collective-permute-start(f32[32,128]{1,0:T(8,128)} %finish.1), channel_id=1, source_target_pairs={{0,4},{4,0},{8,12},{12,8},{1,5},{5,1},{9,13},{13,9},{2,6},{6,2},{1... | collective-permute-start | bytes 49160 | tf_op jit(solution)/shard_map/ppermute | solution.py:290
  37.7 3.7 %collective-permute-start.7 = (f32[32,128]{1,0:T(8,128)S(1)}, f32[32,128]{1,0:T(8,128)S(1)}, u32[]{:S(2)}, u32[]{:S(2)}) collective-permute-start(f32[32,128]{1,0:T(8,128)S(1)} %add.12), channel_id=1, source_target_pairs={{0,8},{4,12},{8,0},{12,4},{1,9},{5,13},{9,1},{13,5},{2,10},{6,14},... | collective-permute-start | bytes 49160 | tf_op jit(solution)/shard_map/ppermute | solution.py:290
  41.4 3.7 %collective-permute-start.8 = (f32[32,128]{1,0:T(8,128)S(1)}, f32[32,128]{1,0:T(8,128)S(1)}, u32[]{:S(2)}, u32[]{:S(2)}) collective-permute-start(f32[32,128]{1,0:T(8,128)S(1)} %add.13), channel_id=1, source_target_pairs={{0,1},{1,0},{2,3},{3,2},{4,5},{5,4},{6,7},{7,6},{8,9},{9,8},{10,11... | collective-permute-start | bytes 49160 | tf_op jit(solution)/shard_map/ppermute | solution.py:290
  45.1 4.6 %collective-permute-start.9 = (f32[32,128]{1,0:T(8,128)S(1)}, f32[32,128]{1,0:T(8,128)S(1)}, u32[]{:S(2)}, u32[]{:S(2)}) collective-permute-start(f32[32,128]{1,0:T(8,128)S(1)} %add.14), channel_id=1, source_target_pairs={{0,2},{1,3},{2,0},{3,1},{4,6},{5,7},{6,4},{7,5},{8,10},{9,11},{10,... | collective-permute-start | bytes 49160 | tf_op jit(solution)/shard_map/ppermute | solution.py:290

commit v2 on v1

--- a/solution.py
+++ b/solution.py
@@ -35,103 +35,143 @@
     return out
 
 
-def edge_select(width):
-    row = lax.broadcasted_iota(jnp.int32, (2 * REACH, width), 0)
-    col = lax.broadcasted_iota(jnp.int32, (2 * REACH, width), 1)
-    want = jnp.where(row < REACH, row, width - 2 * REACH + row)
-    return jnp.where(col == want, 1.0, 0.0)
-
-
-def pack_kernel(re_ref, im_ref, ylo_ref, yhi_ref, zlo_ref, zhi_ref):
-    srcs, cx, ny, nz = re_ref.shape
-    pick = edge_select(nz)
-    for part, ref in enumerate((re_ref, im_ref)):
-        for s in range(srcs):
-            f = part * srcs + s
-            ylo_ref[f] = ref[s, :, 0:REACH, :]
-            yhi_ref[f] = ref[s, :, ny - REACH : ny, :]
-            edges = dot(pick, ref[s].reshape(cx * ny, nz), ((1,), (1,)))
-            zlo_ref[f * REACH : (f + 1) * REACH, :] = edges[0:REACH]
-            zhi_ref[f * REACH : (f + 1) * REACH, :] = edges[REACH : 2 * REACH]
-
-
-def inner_kernel(center_ref, re_ref, im_ref, pot_ref, out_ref, pad_ref):
-    srcs, cx, ny, nz = re_ref.shape
+def split(value):
+    high = value.astype(jnp.bfloat16)
+    return high, (value - high.astype(jnp.float32)).astype(jnp.bfloat16)
+
+
+def dot_split(left, right):
+    return mul(left[0], right[0]) + (mul(left[0], right[1]) + mul(left[1], right[0]))
+
+
+def mul(left, right):
+    return lax.dot_general(left, right, (((1,), (0,)), ((), ())), preferred_element_type=jnp.float32)
+
+
+def gather_edges(gathered, f, value):
+    lane = lax.broadcasted_iota(jnp.int32, value.shape, 1)
+    moved = pltpu.roll(value, 2 * REACH * f + REACH, 1)
+    return jnp.where(lane // (2 * REACH) == f, moved, gathered)
+
+
+def store_edges(gathered, fields, low_ref, high_ref):
+    turned = gathered.T
+    for f in range(fields):
+        at = 2 * REACH * f
+        high_ref[f * REACH : (f + 1) * REACH, :] = turned[at : at + REACH]
+        low_ref[f * REACH : (f + 1) * REACH, :] = turned[at + REACH : at + 2 * REACH]
+
+
+def load_kernel(
+    re_hbm, im_hbm, pot_hbm, b_ref, pot_ref, ylo_ref, yhi_ref, zlo_ref, zhi_ref, edge_ref, sems
+):
+    fields, cx, ny, nz = b_ref.shape
+    srcs = fields // 2
+    copies = [
+        pltpu.make_async_copy(hbm.at[s], b_ref.at[part * srcs + s], sems.at[part * srcs + s])
+        for part, hbm in enumerate((re_hbm, im_hbm))
+        for s in range(srcs)
+    ]
+    copies.append(pltpu.make_async_copy(pot_hbm, pot_ref, sems.at[fields]))
+    for copy in copies:
+        copy.start()
+    edge_ref[...] = jnp.zeros(edge_ref.shape, jnp.float32)
+    for f in range(fields):
+        copies[f].wait()
+        ylo_ref[f] = b_ref[f, :, 0:REACH, :]
+        yhi_ref[f] = b_ref[f, :, ny - REACH : ny, :]
+        edge_ref[...] = gather_edges(edge_ref[...], f, b_ref[f].reshape(cx * ny, nz))
+    store_edges(edge_ref[...], fields, zlo_ref, zhi_ref)
+    copies[fields].wait()
+
+
+def inner_kernel(center_ref, b_ref, pot_ref, out_ref, pad_ref):
+    fields, cx, ny, nz = b_ref.shape
     shift = DIAG - center_ref[0]
-    matrix = band((nz, nz), 0, (1, -1))
+    matrix = split(band((nz, nz), 0, (1, -1)))
     zero = jnp.zeros((cx, 8, nz), jnp.float32)
     pad_ref[:, 0:8, :] = zero
     pad_ref[:, 8 + ny : 16 + ny, :] = zero
-    for part, ref in enumerate((re_ref, im_ref)):
-
-        def field(s, _, ref=ref, part=part):
-            f = part * srcs + s
-            own = ref[s]
-            pad_ref[:, 8 : 8 + ny, :] = own
-            out_ref[f] = dot(own.reshape(cx * ny, nz), matrix, ((1,), (0,))).reshape(cx, ny, nz)
-            for x in range(cx):
-                total = out_ref[f, x] + (pot_ref[x] + shift) * ref[s, x]
-                for k in range(1, REACH + 1):
-                    beside = ref[s, (x + k) % cx] + ref[s, (x - k) % cx]
-                    beside = beside + pad_ref[x, 8 + k : 8 + k + ny, :]
-                    beside = beside + pad_ref[x, 8 - k : 8 - k + ny, :]
-                    total = total + SIDE[k] * beside
-                out_ref[f, x] = total
-            return 0
-
-        lax.fori_loop(0, srcs, field, 0)
-
-
-def border_kernel(inner_ref, ylo_ref, yhi_ref, zlo_ref, zhi_ref, out_ref, oy_ref, oz_ref, own_ref, pad_ref):
+
+    def field(f, _):
+        own = b_ref[f]
+        pad_ref[:, 8 : 8 + ny, :] = own
+        out_ref[f] = dot_split(split(own.reshape(cx * ny, nz)), matrix).reshape(cx, ny, nz)
+        for x in range(cx):
+            total = out_ref[f, x] + (pot_ref[x] + shift) * b_ref[f, x]
+            for k in range(1, REACH + 1):
+                beside = b_ref[f, (x + k) % cx] + b_ref[f, (x - k) % cx]
+                beside = beside + pad_ref[x, 8 + k : 8 + k + ny, :]
+                beside = beside + pad_ref[x, 8 - k : 8 - k + ny, :]
+                total = total + SIDE[k] * beside
+            out_ref[f, x] = total
+        return 0
+
+    lax.fori_loop(0, fields, field, 0)
+
+
+def border_kernel(
+    inner_ref, ylo_ref, yhi_ref, zlo_ref, zhi_ref, out_ref, oy_ref, oz_ref, own_ref, pad_ref, edge_ref
+):
     fields, cx, ny, nz = inner_ref.shape
-    below = band((REACH, nz), -REACH, (1, -1))
-    above = band((REACH, nz), nz, (1, -1))
-    pick = edge_select(nz)
+    rows = fields * REACH
+    turned = split(jnp.concatenate([zlo_ref[...], zhi_ref[...]], axis=0).T)
+    row = lax.broadcasted_iota(jnp.int32, (2 * rows, nz), 0)
+    col = lax.broadcasted_iota(jnp.int32, (2 * rows, nz), 1)
+    step = jnp.where(row < rows, row % REACH - REACH, nz + row % REACH) - col
+    base = jnp.zeros((2 * rows, nz), jnp.float32)
+    for k in range(1, REACH + 1):
+        base = jnp.where(jnp.abs(step) == k, SIDE[k], base)
+    owner = (row % rows) // REACH
+    for f in range(fields):
+        weights = split(jnp.where(owner == f, base, 0.0))
+        out_ref[f] = dot_split(turned, weights).reshape(cx, ny, nz)
     zero = jnp.zeros((cx, 16, nz), jnp.float32)
     pad_ref[0] = zero
     pad_ref[1] = zero
 
     def field(f, _):
-        at = pl.multiple_of(f * REACH, REACH)
-        fix = dot(zlo_ref[f], below, ((0,), (0,))) + dot(zhi_ref[f], above, ((0,), (0,)))
-        out_ref[f] = inner_ref[f] + fix.reshape(cx, ny, nz)
         pad_ref[0, :, 8 - REACH : 8, :] = ylo_ref[f]
         pad_ref[1, :, 8 : 8 + REACH, :] = yhi_ref[f]
         for x in range(cx):
-            low = out_ref[f, x, 0:8, :]
-            high = out_ref[f, x, ny - 8 : ny, :]
+            low = out_ref[f, x, 0:8, :] + inner_ref[f, x, 0:8, :]
+            high = out_ref[f, x, ny - 8 : ny, :] + inner_ref[f, x, ny - 8 : ny, :]
             for k in range(1, REACH + 1):
                 low = low + SIDE[k] * pad_ref[0, x, 8 - k : 16 - k, :]
                 high = high + SIDE[k] * pad_ref[1, x, k : 8 + k, :]
             out_ref[f, x, 0:8, :] = low
             out_ref[f, x, ny - 8 : ny, :] = high
+            if ny > 16:
+                out_ref[f, x, 8 : ny - 8, :] = out_ref[f, x, 8 : ny - 8, :] + inner_ref[f, x, 8 : ny - 8, :]
         oy_ref[f] = out_ref[f, :, 0:REACH, :]
-        edges = dot(pick, out_ref[f].reshape(cx * ny, nz), ((1,), (1,)))
-        oz_ref[f] = edges[0:REACH]
-        own_ref[f] = edges[REACH : 2 * REACH]
         return 0
 
     lax.fori_loop(0, fields, field, 0)
+    gathered = jnp.zeros((cx * ny, nz), jnp.float32)
+    for f in range(fields):
+        gathered = gather_edges(gathered, f, out_ref[f].reshape(cx * ny, nz))
+    store_edges(gathered, fields, oz_ref, own_ref)
 
 
 def fold(value):
     return jnp.sum(value, axis=0, keepdims=True)
 
 
-def sums_kernel(center_ref, re_ref, im_ref, pot_ref, h_ref, acc_ref, step_ref):
-    srcs, cx, ny, nz = re_ref.shape
+def sums_kernel(center_ref, b_ref, pot_ref, h_ref, acc_ref, step_ref):
+    fields, cx, ny, nz = b_ref.shape
+    srcs = fields // 2
     shift = DIAG - center_ref[0]
-    matrix = band((nz, nz), 0, (1,), 2.0)
+    matrix = split(band((nz, nz), 0, (1,), 2.0))
     row = lax.broadcasted_iota(jnp.int32, (ny, nz), 0)
     inside = [row < ny - k for k in range(REACH + 1)]
     for s in range(srcs):
         for part in range(2):
             f = part * srcs + s
-            step_ref[part] = dot(h_ref[f].reshape(cx * ny, nz), matrix, ((1,), (0,))).reshape(cx, ny, nz)
+            step_ref[part] = dot_split(split(h_ref[f].reshape(cx * ny, nz)), matrix).reshape(cx, ny, nz)
         total = [jnp.zeros((ny, nz), jnp.float32) for _ in range(8)]
         for x in range(cx):
             local = pot_ref[x] + shift
-            br, bi = re_ref[s, x], im_ref[s, x]
+            br, bi = b_ref[s, x], b_ref[srcs + s, x]
             h, g = [], []
             for part in range(2):
                 f = part * srcs + s
@@ -168,8 +208,9 @@
     out_ref[...] = acc_ref[...]
     pad_ref[...] = jnp.zeros(pad_ref.shape, jnp.float32)
     for s in range(srcs):
-        edge = [own_ref[part * srcs + s] for part in range(2)]
-        far = [dot(mix, zhi_ref[part * srcs + s], ((1,), (0,))) for part in range(2)]
+        at = [(part * srcs + s) * REACH for part in range(2)]
+        edge = [own_ref[n : n + REACH, :] for n in at]
+        far = [dot(mix, zhi_ref[n : n + REACH, :], ((1,), (0,))) for n in at]
         both = (edge[0] * far[0] - edge[1] * far[1], edge[0] * far[1] + edge[1] * far[0])
         sides = []
         for c in range(2):
@@ -292,12 +333,17 @@
     return value
 
 
+HBM = pl.BlockSpec(memory_space=pltpu.HBM)
 VMEM = pl.BlockSpec(memory_space=pltpu.VMEM)
 SMEM = pl.BlockSpec(memory_space=pltpu.SMEM)
 
 
 def shaped(*dims):
     return jax.ShapeDtypeStruct(dims, jnp.float32)
+
+
+def small(mib):
+    return pltpu.CompilerParams(vmem_limit_bytes=mib << 20)
 
 
 def cost(flops, nbytes):
@@ -310,44 +356,47 @@
     cells = cx * ny * nz
     py, pz, quads = lax.axis_size("py"), lax.axis_size("pz"), lax.axis_size("quad")
 
-    ylo, yhi, zlo, zhi = pl.pallas_call(
-        pack_kernel,
-        out_shape=(
-            shaped(fields, cx, REACH, nz),
-            shaped(fields, cx, REACH, nz),
-            shaped(fields * REACH, cx * ny),
-            shaped(fields * REACH, cx * ny),
-        ),
-        in_specs=[VMEM] * 2,
-        out_specs=(VMEM,) * 4,
-        name="pack",
-    )(source_real, source_imag)
+    whole = shaped(fields, cx, ny, nz)
+    thin = shaped(fields, cx, REACH, nz)
+    flat = shaped(fields * REACH, cx * ny)
+    b, pot, ylo, yhi, zlo, zhi = pl.pallas_call(
+        load_kernel,
+        out_shape=(whole, shaped(cx, ny, nz), thin, thin, flat, flat),
+        in_specs=[HBM] * 3,
+        out_specs=(VMEM,) * 6,
+        scratch_shapes=[
+            pltpu.VMEM((cx * ny, nz), jnp.float32),
+            pltpu.SemaphoreType.DMA((fields + 1,)),
+        ],
+        compiler_params=small(8),
+        name="load",
+    )(*(pltpu.with_memory_space_constraint(a, pltpu.HBM) for a in (source_real, source_imag, potential)))
     y_above = lax.ppermute(ylo, "py", ring(py, -1))
     y_below = lax.ppermute(yhi, "py", ring(py, 1))
-    z_above = lax.ppermute(zlo, "pz", ring(pz, -1)).reshape(fields, REACH, cx * ny)
-    z_below = lax.ppermute(zhi, "pz", ring(pz, 1)).reshape(fields, REACH, cx * ny)
+    z_above = lax.ppermute(zlo, "pz", ring(pz, -1))
+    z_below = lax.ppermute(zhi, "pz", ring(pz, 1))
 
     inner = pl.pallas_call(
         inner_kernel,
-        out_shape=shaped(fields, cx, ny, nz),
-        in_specs=[SMEM] + [VMEM] * 3,
+        out_shape=whole,
+        in_specs=[SMEM] + [VMEM] * 2,
         out_specs=VMEM,
         scratch_shapes=[pltpu.VMEM((cx, ny + 16, nz), jnp.float32)],
+        compiler_params=small(12),
         cost_estimate=cost(fields * cells * 60, fields * cells * 12),
         name="inner",
-    )(center, source_real, source_imag, potential)
+    )(center, b, pot)
 
     image, h_ylo, h_zlo, h_own = pl.pallas_call(
         border_kernel,
-        out_shape=(
-            shaped(fields, cx, ny, nz),
-            shaped(fields, cx, REACH, nz),
-            shaped(fields, REACH, cx * ny),
-            shaped(fields, REACH, cx * ny),
-        ),
+        out_shape=(whole, thin, flat, flat),
         in_specs=[VMEM] * 5,
         out_specs=(VMEM,) * 4,
-        scratch_shapes=[pltpu.VMEM((2, cx, 16, nz), jnp.float32)],
+        scratch_shapes=[
+            pltpu.VMEM((2, cx, 16, nz), jnp.float32),
+            pltpu.VMEM((cx * ny, nz), jnp.float32),
+        ],
+        compiler_params=small(12),
         name="border",
     )(inner, y_below, y_above, z_below, z_above)
     h_yabove = lax.ppermute(h_ylo, "py", ring(py, -1))
@@ -356,12 +405,13 @@
     partial = pl.pallas_call(
         sums_kernel,
         out_shape=shaped(8 * srcs, nz),
-        in_specs=[SMEM] + [VMEM] * 4,
+        in_specs=[SMEM] + [VMEM] * 3,
         out_specs=VMEM,
         scratch_shapes=[pltpu.VMEM((2, cx, ny, nz), jnp.float32)],
+        compiler_params=small(12),
         cost_estimate=cost(fields * cells * 60, fields * cells * 12),
         name="sums",
-    )(center, source_real, source_imag, potential, image)
+    )(center, b, pot, image)
 
     partial = pl.pallas_call(
         finish_kernel,
@@ -369,6 +419,7 @@
         in_specs=[VMEM] * 5,
         out_specs=VMEM,
         scratch_shapes=[pltpu.VMEM((2, cx, 16, nz), jnp.float32)],
+        compiler_params=small(12),
         name="finish",
     )(partial, image, h_own, h_yabove, h_zabove)
 
@@ -389,16 +440,16 @@
                 pl.BlockSpec(total.shape, lambda s, q: (0, 0)),
                 pl.BlockSpec(table.shape, lambda s, q: (0, 0)),
                 own(0),
-                own(0),
+                own(srcs),
                 own(0),
                 own(srcs),
             ],
             out_specs=pl.BlockSpec((MOMS, 2, 1, planes, ny, nz), lambda s, q: (0, 0, s, 0, 0, 0)),
             scratch_shapes=[pltpu.VMEM((4 * MOMS, 8, LANES), jnp.float32)],
         ),
-        compiler_params=pltpu.CompilerParams(dimension_semantics=("arbitrary",)),
+        compiler_params=small(12),
         name="output",
-    )(quad, radius, total, table, source_real, source_imag, image, image)
+    )(quad, radius, total, table, b, b, image, image)
 
 
 def solution(mesh):

time: 54.8 us -> 36.2 us (0.66)
  Pallas kernels: 26.6 us -> 9.72 us
  starting transfers between devices: 11 us -> 15.9 us
  local copies, waits for them, and re-layouts: 3.33 us -> 0.01 us
  waiting for transfers between devices: 10.7 us -> 9.06 us
  other arithmetic: 1.33 us -> 0.02 us
    pallas_call x3, Pallas kernels: 16.4 us -> 5.33 us  [the longest x1 1.93 us: per_device(): pl.pallas_call(load_kernel, out_shape=(whole, shaped(cx, ny, nz), thin, t...]
    pallas_call x1, Pallas kernels: 4.08 us -> 1.79 us  [per_device(): pl.pallas_call(sums_kernel, out_shape=shaped(8 * srcs, nz), in_specs=[SME...]
    unnamed x8 -> x2, local copies, waits for them, and re-layouts: 2.11 us -> 0.01 us
    ppermute x1, starting transfers between devices: 0.01 us -> 1.94 us  [per_device(): h_yabove = lax.ppermute(h_ylo, 'py', ring(py, -1))]
    pallas_call x1, Pallas kernels: 2.2 us -> 0.34 us  [per_device(): pl.pallas_call(finish_kernel, out_shape=shaped(8 * srcs, nz), in_specs=[V...]
    pallas_call x1, Pallas kernels: 3.95 us -> 2.26 us  [per_device(): pl.pallas_call(output_kernel, out_shape=shaped(MOMS, 2, srcs, planes, ny,...]
    ppermute x4, waiting for transfers between devices: 10.7 us -> 9.04 us  [total_over(): lax.ppermute(value, axis, [(i, i ^ bit) for i in range(count)])]
    ppermute x4, starting transfers between devices: 2.19 us -> 3.66 us  [total_over(): lax.ppermute(value, axis, [(i, i ^ bit) for i in range(count)])]
  transfers between devices with their start and end apart: 10 -> 10, of which waited for: 4 -> 4; matrix products, arithmetic and copies ran while one was open for 2% -> 0% of each run, Pallas kernels for 16% -> 10%
where the time goes in v2:
time: 36.2 us; the launch traced here: 36.1 us
  starting transfers between devices  15.9 us (44%)
  Pallas kernels  9.72 us (27%)
  waiting for transfers between devices  9.06 us (25%)
  between operations  1.4 us (4%)
    ppermute x4, waiting for transfers between devices, total_over(): lax.ppermute(value, axis, [(i, i ^ bit) for i in range(count)])  9.04 us
    ppermute x4, starting transfers between devices, total_over(): lax.ppermute(value, axis, [(i, i ^ bit) for i in range(count)])  3.66 us
    ppermute x1, starting transfers between devices, per_device(): h_zabove = lax.ppermute(h_zlo, 'pz', ring(pz, -1))  3.38 us
    ppermute x1, starting transfers between devices, per_device(): z_below = lax.ppermute(zhi, 'pz', ring(pz, 1))  2.3 us
    pallas_call x1, Pallas kernels, per_device(): pl.pallas_call(output_kernel, out_shape=shaped(MOMS, 2, srcs, planes, ny,...  2.26 us
    ppermute x1, starting transfers between devices, per_device(): z_above = lax.ppermute(zlo, 'pz', ring(pz, -1))  2.03 us
    ppermute x1, starting transfers between devices, per_device(): y_above = lax.ppermute(ylo, 'py', ring(py, -1))  2.01 us
    ppermute x1, starting transfers between devices, per_device(): h_yabove = lax.ppermute(h_ylo, 'py', ring(py, -1))  1.94 us
  transfers between devices with their start and end apart: 10, of which 4 were waited for; matrix products, arithmetic and copies ran while one was open for 0% of the time, Pallas kernels for 10%

profile of v2, /device:TPU:0, one launch (start us, length us, event | category | flops | bytes accessed | tf_op | source)
XLA Modules:
  0.0 36.1 jit_solution(6229207026793204778)
XLA Ops:
  0.0 1.9 %load.1 = (f32[8,16,16,128]{3,2,1,0:T(8,128)S(1)}, f32[16,16,128]{2,1,0:T(8,128)S(1)}, f32[8,16,4,128]{3,2,1,0:T(4,128)S(1)}, f32[8,16,4,128]{3,2,1,0:T(4,128)S(...) custom-call(f32[4,16,16,128]{3,2,1,0:T(8,128)} %re_hbm.1, f32[4,16,16,128]{3,2,1,0:T(8,128)} %im_hbm.1, ...), custom_call_target="tpu_custom_call" | custom-call | tf_op jit(solution)/shard_map/load/pallas_call | solution.py:362
  1.9 0.5 %collective-permute-start = (f32[8,16,4,128]{3,2,1,0:T(4,128)S(1)}, f32[8,16,4,128]{3,2,1,0:T(4,128)S(1)}, u32[]{:S(2)}, u32[]{:S(2)}) collective-permute-start(f32[8,16,4,128]{3,2,1,0:T(4,128)S(1)} %get-tuple-element.17), channel_id=1, source_target_pairs={{0,4},{4,8},{8,12},{12,0},{1,5},{5,9},{9,13},{13,1},{2,6},{6,10},{... | collective-permute-start | bytes 786440 | tf_op jit(solution)/shard_map/ppermute | solution.py:375
  2.5 2.0 %collective-permute-start.1 = (f32[8,16,4,128]{3,2,1,0:T(4,128)S(1)}, f32[8,16,4,128]{3,2,1,0:T(4,128)S(1)}, u32[]{:S(2)}, u32[]{:S(2)}) collective-permute-start(f32[8,16,4,128]{3,2,1,0:T(4,128)S(1)} %get-tuple-element.18), channel_id=1, source_target_pairs={{0,12},{4,0},{8,4},{12,8},{1,13},{5,1},{9,5},{13,9},{2,14},{6,2},{... | collective-permute-start | bytes 786440 | tf_op jit(solution)/shard_map/ppermute | solution.py:374
  4.5 2.3 %collective-permute-start.2 = (f32[32,256]{1,0:T(8,128)S(1)}, f32[32,256]{1,0:T(8,128)S(1)}, u32[]{:S(2)}, u32[]{:S(2)}) collective-permute-start(f32[32,256]{1,0:T(8,128)S(1)} %get-tuple-element.19), channel_id=1, source_target_pairs={{0,1},{1,2},{2,3},{3,0},{4,5},{5,6},{6,7},{7,4},{8,9},{9,10},{10,1... | collective-permute-start | bytes 98312 | tf_op jit(solution)/shard_map/ppermute | solution.py:377
  6.8 2.0 %collective-permute-start.3 = (f32[32,256]{1,0:T(8,128)S(1)}, f32[32,256]{1,0:T(8,128)S(1)}, u32[]{:S(2)}, u32[]{:S(2)}) collective-permute-start(f32[32,256]{1,0:T(8,128)S(1)} %get-tuple-element.20), channel_id=1, source_target_pairs={{0,3},{1,0},{2,1},{3,2},{4,7},{5,4},{6,5},{7,6},{8,11},{9,8},{10,9... | collective-permute-start | bytes 98312 | tf_op jit(solution)/shard_map/ppermute | solution.py:376
  9.5 1.8 %inner.1.inner_ref = f32[8,16,16,128]{3,2,1,0:T(8,128)S(1)} custom-call(f32[1]{0:T(128)S(6)} %copy.7.center_ref, f32[8,16,16,128]{3,2,1,0:T(8,128)S(1)} %get-tuple-element.15.b_ref.re_ref.im_ref, f32[16,16,128]{2,1,0:T(8,128)S(1)} %get-tuple-element.16.pot_ref), custom_call_target="tpu_custom_call" | custom-call | flops 15728640 | bytes 3145728 | tf_op jit(solution)/shard_map/inner/pallas_call | solution.py:379
  11.3 0.0 collective-permute-done.ylo_ref
  11.3 0.0 collective-permute-done.1.yhi_ref
  11.3 1.6 %border.1 = (f32[8,16,16,128]{3,2,1,0:T(8,128)S(1)}, f32[8,16,4,128]{3,2,1,0:T(4,128)S(1)}, f32[32,256]{1,0:T(8,128)S(1)}, f32[32,256]{1,0:T(8,128)S(1)}) custom-call(f32[8,16,16,128]{3,2,1,0:T(8,128)S(1)} %inner.1.inner_ref, f32[8,16,4,128]{3,2,1,0:T(4,128)S(1)} %collective-permute-done.ylo_ref, f32[8,16,4,128]{3,2,1,0:T(4,128)S(1)} %collective-permute-done.1.yhi_ref, ...), custom_call_target="tpu_custom_call" | custom-call | tf_op jit(solution)/shard_map/border/pallas_call | solution.py:390
  12.9 0.0 copy-start
  12.9 1.9 %collective-permute-start.4 = (f32[8,16,4,128]{3,2,1,0:T(4,128)S(1)}, f32[8,16,4,128]{3,2,1,0:T(4,128)S(1)}, u32[]{:S(2)}, u32[]{:S(2)}) collective-permute-start(f32[8,16,4,128]{3,2,1,0:T(4,128)S(1)} %get-tuple-element.23), channel_id=1, source_target_pairs={{0,12},{4,0},{8,4},{12,8},{1,13},{5,1},{9,5},{13,9},{2,14},{6,2},{... | collective-permute-start | bytes 786440 | tf_op jit(solution)/shard_map/ppermute | solution.py:402
  14.9 3.4 %collective-permute-start.5 = (f32[32,256]{1,0:T(8,128)S(1)}, f32[32,256]{1,0:T(8,128)S(1)}, u32[]{:S(2)}, u32[]{:S(2)}) collective-permute-start(f32[32,256]{1,0:T(8,128)S(1)} %get-tuple-element.24), channel_id=1, source_target_pairs={{0,3},{1,0},{2,1},{3,2},{4,7},{5,4},{6,5},{7,6},{8,11},{9,8},{10,9... | collective-permute-start | bytes 98312 | tf_op jit(solution)/shard_map/ppermute | solution.py:403
  18.3 1.8 %sums.1.acc_ref = f32[32,128]{1,0:T(8,128)S(1)} custom-call(f32[1]{0:T(128)S(6)} %copy.7.center_ref, f32[8,16,16,128]{3,2,1,0:T(8,128)S(1)} %get-tuple-element.15.b_ref.re_ref.im_ref, f32[16,16,128]{2,1,0:T(8,128)S(1)} %get-tuple-element.16.pot_ref, f32[8,16,16,128]{3,2,1,0:T(8,128)S(1)} %get-tuple-element.21.h_ref.hr_ref.hi_ref), custom_call_target="tpu_custom_call" | custom-call | flops 15728640 | bytes 3145728 | tf_op jit(solution)/shard_map/sums/pallas_call | solution.py:405
  20.1 0.0 collective-permute-done.5.zhi_ref
  20.1 0.3 finish.1
  20.4 0.1 collective-permute-start.6
  20.5 1.2 %collective-permute-done.6 = f32[32,128]{1,0:T(8,128)S(1)} collective-permute-done((f32[32,128]{1,0:T(8,128)S(1)}, f32[32,128]{1,0:T(8,128)S(1)}, u32[]{:S(2)}, u32[]{:S(2)}) %collective-permute-start.6) | collective-permute-done | bytes 16416 | tf_op jit(solution)/shard_map/ppermute | solution.py:331
  21.7 0.7 %collective-permute-start.7 = (f32[32,128]{1,0:T(8,128)S(1)}, f32[32,128]{1,0:T(8,128)S(1)}, u32[]{:S(2)}, u32[]{:S(2)}) collective-permute-start(f32[32,128]{1,0:T(8,128)S(1)} %add.12), channel_id=1, source_target_pairs={{0,8},{4,12},{8,0},{12,4},{1,9},{5,13},{9,1},{13,5},{2,10},{6,14},... | collective-permute-start | bytes 49160 | tf_op jit(solution)/shard_map/ppermute | solution.py:331
  22.3 3.1 %collective-permute-done.7 = f32[32,128]{1,0:T(8,128)S(1)} collective-permute-done((f32[32,128]{1,0:T(8,128)S(1)}, f32[32,128]{1,0:T(8,128)S(1)}, u32[]{:S(2)}, u32[]{:S(2)}) %collective-permute-start.7) | collective-permute-done | bytes 16416 | tf_op jit(solution)/shard_map/ppermute | solution.py:331
  25.4 0.5 %collective-permute-start.8 = (f32[32,128]{1,0:T(8,128)S(1)}, f32[32,128]{1,0:T(8,128)S(1)}, u32[]{:S(2)}, u32[]{:S(2)}) collective-permute-start(f32[32,128]{1,0:T(8,128)S(1)} %add.13), channel_id=1, source_target_pairs={{0,1},{1,0},{2,3},{3,2},{4,5},{5,4},{6,7},{7,6},{8,9},{9,8},{10,11... | collective-permute-start | bytes 49160 | tf_op jit(solution)/shard_map/ppermute | solution.py:331
  25.9 3.2 %collective-permute-done.8 = f32[32,128]{1,0:T(8,128)S(1)} collective-permute-done((f32[32,128]{1,0:T(8,128)S(1)}, f32[32,128]{1,0:T(8,128)S(1)}, u32[]{:S(2)}, u32[]{:S(2)}) %collective-permute-start.8) | collective-permute-done | bytes 16416 | tf_op jit(solution)/shard_map/ppermute | solution.py:331
  29.2 2.4 %collective-permute-start.9 = (f32[32,128]{1,0:T(8,128)S(1)}, f32[32,128]{1,0:T(8,128)S(1)}, u32[]{:S(2)}, u32[]{:S(2)}) collective-permute-start(f32[32,128]{1,0:T(8,128)S(1)} %add.14), channel_id=1, source_target_pairs={{0,2},{1,3},{2,0},{3,1},{4,6},{5,7},{6,4},{7,5},{8,10},{9,11},{10,... | collective-permute-start | bytes 49160 | tf_op jit(solution)/shard_map/ppermute | solution.py:331
  32.3 1.5 %collective-permute-done.9 = f32[32,128]{1,0:T(8,128)S(1)} collective-permute-done((f32[32,128]{1,0:T(8,128)S(1)}, f32[32,128]{1,0:T(8,128)S(1)}, u32[]{:S(2)}, u32[]{:S(2)}) %collective-permute-start.9) | collective-permute-done | bytes 16416 | tf_op jit(solution)/shard_map/ppermute | solution.py:331
  33.8 2.3 %output.1 = f32[4,2,4,8,16,128]{5,4,3,2,1,0:T(8,128)} custom-call(s32[1]{0:T(128)} %bitcast.quad_ref, f32[1]{0:T(128)S(6)} %copy.8.radius_ref, f32[32,128]{1,0:T(8,128)S(1)} %add.15.tot_ref, f32[16,128]{1,0:T(8,128)S(1)} %copy-done, f32[8,16,16,128]{3,2,1,0:T(8,128)S(1)} %get-tuple-element.15.b_ref.re_ref.im_ref, ...), custom_call_target="tpu_custom_call" | custom-call | tf_op jit(solution)/shard_map/output/pallas_call | solution.py:432
  (8 shorter events, 0.0 us)
Async XLA Ops:
  1.9 9.4 %collective-permute-start = (f32[8,16,4,128]{3,2,1,0:T(4,128)S(1)}, f32[8,16,4,128]{3,2,1,0:T(4,128)S(1)}, u32[]{:S(2)}, u32[]{:S(2)}) collective-permute-start(f32[8,16,4,128]{3,2,1,0:T(4,128)S(1)} %get-tuple-element.17), channel_id=1, source_target_pairs={{0,4},{4,8},{8,12},{12,0},{1,5},{5,9},{9,13},{13,1},{2,6},{6,10},{... | collective-permute-start | bytes 786440 | tf_op jit(solution)/shard_map/ppermute | solution.py:375
  2.5 8.9 %collective-permute-start.1 = (f32[8,16,4,128]{3,2,1,0:T(4,128)S(1)}, f32[8,16,4,128]{3,2,1,0:T(4,128)S(1)}, u32[]{:S(2)}, u32[]{:S(2)}) collective-permute-start(f32[8,16,4,128]{3,2,1,0:T(4,128)S(1)} %get-tuple-element.18), channel_id=1, source_target_pairs={{0,12},{4,0},{8,4},{12,8},{1,13},{5,1},{9,5},{13,9},{2,14},{6,2},{... | collective-permute-start | bytes 786440 | tf_op jit(solution)/shard_map/ppermute | solution.py:374
  4.5 6.8 %collective-permute-start.2 = (f32[32,256]{1,0:T(8,128)S(1)}, f32[32,256]{1,0:T(8,128)S(1)}, u32[]{:S(2)}, u32[]{:S(2)}) collective-permute-start(f32[32,256]{1,0:T(8,128)S(1)} %get-tuple-element.19), channel_id=1, source_target_pairs={{0,1},{1,2},{2,3},{3,0},{4,5},{5,6},{6,7},{7,4},{8,9},{9,10},{10,1... | collective-permute-start | bytes 98312 | tf_op jit(solution)/shard_map/ppermute | solution.py:377
  6.8 4.5 %collective-permute-start.3 = (f32[32,256]{1,0:T(8,128)S(1)}, f32[32,256]{1,0:T(8,128)S(1)}, u32[]{:S(2)}, u32[]{:S(2)}) collective-permute-start(f32[32,256]{1,0:T(8,128)S(1)} %get-tuple-element.20), channel_id=1, source_target_pairs={{0,3},{1,0},{2,1},{3,2},{4,7},{5,4},{6,5},{7,6},{8,11},{9,8},{10,9... | collective-permute-start | bytes 98312 | tf_op jit(solution)/shard_map/ppermute | solution.py:376
  12.9 20.9 %copy-start = (f32[16,128]{1,0:T(8,128)S(1)}, f32[16,128]{1,0:T(8,128)}, u32[]{:S(2)}) copy-start(f32[16,128]{1,0:T(8,128)} %constant.8.clone.table_ref) | copy-start | bytes 24580
  12.9 7.1 %collective-permute-start.4 = (f32[8,16,4,128]{3,2,1,0:T(4,128)S(1)}, f32[8,16,4,128]{3,2,1,0:T(4,128)S(1)}, u32[]{:S(2)}, u32[]{:S(2)}) collective-permute-start(f32[8,16,4,128]{3,2,1,0:T(4,128)S(1)} %get-tuple-element.23), channel_id=1, source_target_pairs={{0,12},{4,0},{8,4},{12,8},{1,13},{5,1},{9,5},{13,9},{2,14},{6,2},{... | collective-permute-start | bytes 786440 | tf_op jit(solution)/shard_map/ppermute | solution.py:402
  14.9 5.2 %collective-permute-start.5 = (f32[32,256]{1,0:T(8,128)S(1)}, f32[32,256]{1,0:T(8,128)S(1)}, u32[]{:S(2)}, u32[]{:S(2)}) collective-permute-start(f32[32,256]{1,0:T(8,128)S(1)} %get-tuple-element.24), channel_id=1, source_target_pairs={{0,3},{1,0},{2,1},{3,2},{4,7},{5,4},{6,5},{7,6},{8,11},{9,8},{10,9... | collective-permute-start | bytes 98312 | tf_op jit(solution)/shard_map/ppermute | solution.py:403
  20.4 1.2 %collective-permute-start.6 = (f32[32,128]{1,0:T(8,128)S(1)}, f32[32,128]{1,0:T(8,128)S(1)}, u32[]{:S(2)}, u32[]{:S(2)}) collective-permute-start(f32[32,128]{1,0:T(8,128)S(1)} %finish.1), channel_id=1, source_target_pairs={{0,4},{4,0},{8,12},{12,8},{1,5},{5,1},{9,13},{13,9},{2,6},{6,2},{1... | collective-permute-start | bytes 49160 | tf_op jit(solution)/shard_map/ppermute | solution.py:331
  21.7 3.7 %collective-permute-start.7 = (f32[32,128]{1,0:T(8,128)S(1)}, f32[32,128]{1,0:T(8,128)S(1)}, u32[]{:S(2)}, u32[]{:S(2)}) collective-permute-start(f32[32,128]{1,0:T(8,128)S(1)} %add.12), channel_id=1, source_target_pairs={{0,8},{4,12},{8,0},{12,4},{1,9},{5,13},{9,1},{13,5},{2,10},{6,14},... | collective-permute-start | bytes 49160 | tf_op jit(solution)/shard_map/ppermute | solution.py:331
  25.4 3.7 %collective-permute-start.8 = (f32[32,128]{1,0:T(8,128)S(1)}, f32[32,128]{1,0:T(8,128)S(1)}, u32[]{:S(2)}, u32[]{:S(2)}) collective-permute-start(f32[32,128]{1,0:T(8,128)S(1)} %add.13), channel_id=1, source_target_pairs={{0,1},{1,0},{2,3},{3,2},{4,5},{5,4},{6,7},{7,6},{8,9},{9,8},{10,11... | collective-permute-start | bytes 49160 | tf_op jit(solution)/shard_map/ppermute | solution.py:331
  29.2 4.6 %collective-permute-start.9 = (f32[32,128]{1,0:T(8,128)S(1)}, f32[32,128]{1,0:T(8,128)S(1)}, u32[]{:S(2)}, u32[]{:S(2)}) collective-permute-start(f32[32,128]{1,0:T(8,128)S(1)} %add.14), channel_id=1, source_target_pairs={{0,2},{1,3},{2,0},{3,1},{4,6},{5,7},{6,4},{7,5},{8,10},{9,11},{10,... | collective-permute-start | bytes 49160 | tf_op jit(solution)/shard_map/ppermute | solution.py:331

commit v3 on v2

--- a/solution.py
+++ b/solution.py
@@ -16,6 +16,7 @@
 
 stencil_weights = (-205.0 / 72.0, 8.0 / 5.0, -1.0 / 5.0, 8.0 / 315.0, -1.0 / 560.0)
 DIAG = -1.5 * stencil_weights[0]
+MIDDLE = 5.25
 SIDE = tuple(-0.5 * w for w in stencil_weights)
 HIGHEST = lax.Precision.HIGHEST
 
@@ -41,11 +42,9 @@
 
 
 def dot_split(left, right):
-    return mul(left[0], right[0]) + (mul(left[0], right[1]) + mul(left[1], right[0]))
-
-
-def mul(left, right):
-    return lax.dot_general(left, right, (((1,), (0,)), ((), ())), preferred_element_type=jnp.float32)
+    rows = jnp.concatenate([left[0], left[1], left[0]], axis=1)
+    cols = jnp.concatenate([right[0], right[0], right[1]], axis=0)
+    return lax.dot_general(rows, cols, (((1,), (0,)), ((), ())), preferred_element_type=jnp.float32)
 
 
 def gather_edges(gathered, f, value):
@@ -62,9 +61,7 @@
         low_ref[f * REACH : (f + 1) * REACH, :] = turned[at + REACH : at + 2 * REACH]
 
 
-def load_kernel(
-    re_hbm, im_hbm, pot_hbm, b_ref, pot_ref, ylo_ref, yhi_ref, zlo_ref, zhi_ref, edge_ref, sems
-):
+def load_kernel(re_hbm, im_hbm, pot_hbm, b_ref, pot_ref, ylo_ref, yhi_ref, zlo_ref, zhi_ref, edge_ref, sems):
     fields, cx, ny, nz = b_ref.shape
     srcs = fields // 2
     copies = [
@@ -81,24 +78,36 @@
         ylo_ref[f] = b_ref[f, :, 0:REACH, :]
         yhi_ref[f] = b_ref[f, :, ny - REACH : ny, :]
         edge_ref[...] = gather_edges(edge_ref[...], f, b_ref[f].reshape(cx * ny, nz))
+    copies[fields].wait()
+    pot_ref[...] = pot_ref[...] + (DIAG - MIDDLE)
     store_edges(edge_ref[...], fields, zlo_ref, zhi_ref)
-    copies[fields].wait()
-
-
-def inner_kernel(center_ref, b_ref, pot_ref, out_ref, pad_ref):
+
+
+def phase_table():
+    lane = np.arange(LANES)
+    angle = 2.0 * math.pi * (lane % QPTS + 0.5) / QPTS
+    rows = [np.cos(angle), np.sin(angle)]
+    for k in range(1, MOMS + 1):
+        rows.append(np.where(lane < QPTS, np.cos(k * angle), 0.0) / QPTS)
+        rows.append(np.where(lane < QPTS, np.sin(k * angle), 0.0) / QPTS)
+    rows += [np.zeros(LANES)] * (-len(rows) % 8)
+    return np.stack(rows).astype(np.float32)
+
+
+def inner_kernel(b_ref, pot_ref, out_ref, pad_ref):
     fields, cx, ny, nz = b_ref.shape
-    shift = DIAG - center_ref[0]
     matrix = split(band((nz, nz), 0, (1, -1)))
     zero = jnp.zeros((cx, 8, nz), jnp.float32)
     pad_ref[:, 0:8, :] = zero
     pad_ref[:, 8 + ny : 16 + ny, :] = zero
 
+    for f in range(fields):
+        out_ref[f] = dot_split(split(b_ref[f].reshape(cx * ny, nz)), matrix).reshape(cx, ny, nz)
+
     def field(f, _):
-        own = b_ref[f]
-        pad_ref[:, 8 : 8 + ny, :] = own
-        out_ref[f] = dot_split(split(own.reshape(cx * ny, nz)), matrix).reshape(cx, ny, nz)
+        pad_ref[:, 8 : 8 + ny, :] = b_ref[f]
         for x in range(cx):
-            total = out_ref[f, x] + (pot_ref[x] + shift) * b_ref[f, x]
+            total = out_ref[f, x] + pot_ref[x] * b_ref[f, x]
             for k in range(1, REACH + 1):
                 beside = b_ref[f, (x + k) % cx] + b_ref[f, (x - k) % cx]
                 beside = beside + pad_ref[x, 8 + k : 8 + k + ny, :]
@@ -157,10 +166,9 @@
     return jnp.sum(value, axis=0, keepdims=True)
 
 
-def sums_kernel(center_ref, b_ref, pot_ref, h_ref, acc_ref, step_ref):
+def sums_kernel(b_ref, pot_ref, h_ref, acc_ref, step_ref):
     fields, cx, ny, nz = b_ref.shape
     srcs = fields // 2
-    shift = DIAG - center_ref[0]
     matrix = split(band((nz, nz), 0, (1,), 2.0))
     row = lax.broadcasted_iota(jnp.int32, (ny, nz), 0)
     inside = [row < ny - k for k in range(REACH + 1)]
@@ -170,7 +178,7 @@
             step_ref[part] = dot_split(split(h_ref[f].reshape(cx * ny, nz)), matrix).reshape(cx, ny, nz)
         total = [jnp.zeros((ny, nz), jnp.float32) for _ in range(8)]
         for x in range(cx):
-            local = pot_ref[x] + shift
+            local = pot_ref[x]
             br, bi = b_ref[s, x], b_ref[srcs + s, x]
             h, g = [], []
             for part in range(2):
@@ -197,15 +205,15 @@
             acc_ref[i * srcs + s : i * srcs + s + 1, :] = fold(total[i])
 
 
-def finish_kernel(acc_ref, h_ref, own_ref, yhi_ref, zhi_ref, out_ref, pad_ref):
+def finish_kernel(sums_ref, h_ref, own_ref, yhi_ref, zhi_ref, out_ref, pad_ref, acc_ref):
     fields, cx, ny, nz = h_ref.shape
     srcs = fields // 2
+    acc_ref[...] = sums_ref[...]
     i = lax.broadcasted_iota(jnp.int32, (REACH, REACH), 0)
     j = lax.broadcasted_iota(jnp.int32, (REACH, REACH), 1)
     mix = jnp.zeros((REACH, REACH), jnp.float32)
     for k in range(1, REACH + 1):
         mix = jnp.where(j - i + REACH == k, 2.0 * SIDE[k], mix)
-    out_ref[...] = acc_ref[...]
     pad_ref[...] = jnp.zeros(pad_ref.shape, jnp.float32)
     for s in range(srcs):
         at = [(part * srcs + s) * REACH for part in range(2)]
@@ -232,7 +240,8 @@
             total[1] = total[1] + (h[0] * g[1] + h[1] * g[0])
         for c in range(2):
             at = (6 + c) * srcs + s
-            out_ref[at : at + 1, :] = out_ref[at : at + 1, :] + fold(total[c]) + sides[c]
+            acc_ref[at : at + 1, :] = acc_ref[at : at + 1, :] + fold(total[c]) + sides[c]
+    out_ref[...] = squeeze_rows(acc_ref[...])
 
 
 def complex_mul(left, right):
@@ -247,75 +256,82 @@
     )
 
 
-def phase_table():
-    lane = np.arange(LANES)
-    angle = 2.0 * math.pi * (lane % QPTS + 0.5) / QPTS
-    rows = [np.cos(angle), np.sin(angle)]
-    for k in range(1, MOMS + 1):
-        rows.append(np.where(lane < QPTS, np.cos(k * angle), 0.0) / QPTS)
-        rows.append(np.where(lane < QPTS, np.sin(k * angle), 0.0) / QPTS)
-    while len(rows) % 8:
-        rows.append(np.zeros(LANES))
-    return np.stack(rows).astype(np.float32)
-
-
-def output_kernel(quad_ref, radius_ref, tot_ref, table_ref, re_ref, im_ref, hr_ref, hi_ref, out_ref, coef_ref):
-    srcs = tot_ref.shape[0] // 8
-    s = pl.program_id(0)
-
-    @pl.when(s == 0)
-    def _():
-        radius = radius_ref[0]
-        summed = jnp.sum(tot_ref[...], axis=1, keepdims=True)
-        wide = jnp.broadcast_to(summed, (8 * srcs, LANES))
-        nu = [
-            (wide[2 * k * srcs : (2 * k + 1) * srcs], wide[(2 * k + 1) * srcs : (2 * k + 2) * srcs])
-            for k in range(4)
-        ]
-        shape = (srcs, LANES)
-        zeta = (
-            jnp.broadcast_to(radius * table_ref[0:1, :], shape),
-            jnp.broadcast_to(radius * table_ref[1:2, :], shape),
+def squeeze_rows(value):
+    rows, width = value.shape
+    part = width // 4
+    lane = lax.broadcasted_iota(jnp.int32, (rows // 4, width), 1) // part
+    value = value + pltpu.roll(value, 2 * part, 1)
+    value = value + pltpu.roll(value, part, 1)
+    out = value[0 : rows // 4]
+    for g in range(1, 4):
+        out = jnp.where(lane == g, value[g * rows // 4 : (g + 1) * rows // 4], out)
+    return out
+
+
+def output_kernel(tot_ref, table_ref, b_ref, h_ref, out_hbm, coef_ref, buf_ref, sems):
+    fields, cx, ny, nz = b_ref.shape
+    srcs = fields // 2
+    planes = buf_ref.shape[3]
+    first = lax.axis_index("quad") * planes
+    tot = tot_ref[...]
+    lane = lax.broadcasted_iota(jnp.int32, tot.shape, 1) // (tot.shape[1] // 4)
+    shape = (srcs, LANES)
+    nu = []
+    for k in range(4):
+        column = jnp.sum(jnp.where(lane == k, tot, 0.0), axis=1, keepdims=True)
+        wide = jnp.broadcast_to(column, (2 * srcs, LANES))
+        nu.append((wide[0:srcs], wide[srcs : 2 * srcs]))
+    zeta = (
+        jnp.broadcast_to(table_ref[0:1, :], shape),
+        jnp.broadcast_to(table_ref[1:2, :], shape),
+    )
+    scaled = complex_mul(zeta, nu[0])
+    alpha_first = complex_div(nu[0], (scaled[0] - nu[1][0], scaled[1] - nu[1][1]))
+    mean = complex_div(nu[1], nu[0])
+    t = complex_mul(mean, nu[1])
+    spread2 = (nu[2][0] - t[0], nu[2][1] - t[1])
+    t = complex_mul(mean, (nu[2][0] + spread2[0], nu[2][1] + spread2[1]))
+    spread3 = (nu[3][0] - t[0], nu[3][1] - t[1])
+    square = complex_mul(alpha_first, alpha_first)
+    rho_next = complex_mul(square, spread2)
+    beta = complex_div(rho_next, nu[0])
+    first_part = complex_mul(zeta, rho_next)
+    second = complex_mul(square, spread3)
+    third = complex_div(complex_mul(beta, rho_next), alpha_first)
+    alpha_next = complex_div(
+        rho_next, (first_part[0] - second[0] - third[0], first_part[1] - second[1] - third[1])
+    )
+    t = complex_mul(alpha_first, mean)
+    carried = complex_mul(alpha_next, (beta[0] - t[0], beta[1] - t[1]))
+    on_source = (alpha_first[0] + carried[0], alpha_first[1] + carried[1])
+    on_image = complex_mul(alpha_next, alpha_first)
+    for k in range(MOMS):
+        weight = (
+            jnp.broadcast_to(table_ref[2 + 2 * k : 3 + 2 * k, :], shape),
+            jnp.broadcast_to(table_ref[3 + 2 * k : 4 + 2 * k, :], shape),
         )
-        scaled = complex_mul(zeta, nu[0])
-        alpha_first = complex_div(nu[0], (scaled[0] - nu[1][0], scaled[1] - nu[1][1]))
-        mean = complex_div(nu[1], nu[0])
-        t = complex_mul(mean, nu[1])
-        spread2 = (nu[2][0] - t[0], nu[2][1] - t[1])
-        t = complex_mul(mean, (nu[2][0] + spread2[0], nu[2][1] + spread2[1]))
-        spread3 = (nu[3][0] - t[0], nu[3][1] - t[1])
-        square = complex_mul(alpha_first, alpha_first)
-        rho_next = complex_mul(square, spread2)
-        beta = complex_div(rho_next, nu[0])
-        first = complex_mul(zeta, rho_next)
-        second = complex_mul(square, spread3)
-        third = complex_div(complex_mul(beta, rho_next), alpha_first)
-        alpha_next = complex_div(
-            rho_next, (first[0] - second[0] - third[0], first[1] - second[1] - third[1])
-        )
-        t = complex_mul(alpha_first, mean)
-        carried = complex_mul(alpha_next, (beta[0] - t[0], beta[1] - t[1]))
-        on_source = (alpha_first[0] + carried[0], alpha_first[1] + carried[1])
-        on_image = complex_mul(alpha_next, alpha_first)
+        for n, value in enumerate((on_source, on_image)):
+            both = complex_mul(weight, value)
+            for c in range(2):
+                column = jnp.sum(both[c], axis=1, keepdims=True)
+                coef_ref[4 * k + 2 * n + c, 0:srcs, :] = jnp.broadcast_to(column, shape)
+
+    copies = []
+    for s in range(srcs):
         for k in range(MOMS):
-            weight = (
-                jnp.broadcast_to(radius * table_ref[2 + 2 * k : 3 + 2 * k, :], shape),
-                jnp.broadcast_to(radius * table_ref[3 + 2 * k : 4 + 2 * k, :], shape),
-            )
-            for n, value in enumerate((on_source, on_image)):
-                both = complex_mul(weight, value)
-                for c in range(2):
-                    column = jnp.sum(both[c], axis=1, keepdims=True)
-                    coef_ref[4 * k + 2 * n + c, 0:srcs, :] = jnp.broadcast_to(column, shape)
-
-    planes = re_ref.shape[1]
-    plane = re_ref.shape[2:]
-    for k in range(MOMS):
-        c = [jnp.broadcast_to(coef_ref[4 * k + n, pl.ds(s, 1), :], plane) for n in range(4)]
-        for x in range(planes):
-            br, bi, hr, hi = re_ref[0, x], im_ref[0, x], hr_ref[0, x], hi_ref[0, x]
-            out_ref[k, 0, 0, x] = c[0] * br - c[1] * bi + (c[2] * hr - c[3] * hi)
-            out_ref[k, 1, 0, x] = c[0] * bi + c[1] * br + (c[2] * hi + c[3] * hr)
+            c = [
+                jnp.broadcast_to(coef_ref[4 * k + n, s : s + 1, :], (ny, nz)) for n in range(4)
+            ]
+            for x in range(planes):
+                br, bi = b_ref[s, first + x], b_ref[srcs + s, first + x]
+                hr, hi = h_ref[s, first + x], h_ref[srcs + s, first + x]
+                buf_ref[s, k, 0, x] = c[0] * br - c[1] * bi + (c[2] * hr - c[3] * hi)
+                buf_ref[s, k, 1, x] = c[0] * bi + c[1] * br + (c[2] * hi + c[3] * hr)
+        copy = pltpu.make_async_copy(buf_ref.at[s], out_hbm.at[:, :, s], sems.at[s])
+        copy.start()
+        copies.append(copy)
+    for copy in copies:
+        copy.wait()
 
 
 def ring(count, step):
@@ -333,6 +349,7 @@
     return value
 
 
+ANY = pl.BlockSpec(memory_space=pl.ANY)
 HBM = pl.BlockSpec(memory_space=pltpu.HBM)
 VMEM = pl.BlockSpec(memory_space=pltpu.VMEM)
 SMEM = pl.BlockSpec(memory_space=pltpu.SMEM)
@@ -359,6 +376,10 @@
     whole = shaped(fields, cx, ny, nz)
     thin = shaped(fields, cx, REACH, nz)
     flat = shaped(fields * REACH, cx * ny)
+    source_real, source_imag, potential = (
+        pltpu.with_memory_space_constraint(a, pltpu.HBM)
+        for a in (source_real, source_imag, potential)
+    )
     b, pot, ylo, yhi, zlo, zhi = pl.pallas_call(
         load_kernel,
         out_shape=(whole, shaped(cx, ny, nz), thin, thin, flat, flat),
@@ -370,7 +391,7 @@
         ],
         compiler_params=small(8),
         name="load",
-    )(*(pltpu.with_memory_space_constraint(a, pltpu.HBM) for a in (source_real, source_imag, potential)))
+    )(source_real, source_imag, potential)
     y_above = lax.ppermute(ylo, "py", ring(py, -1))
     y_below = lax.ppermute(yhi, "py", ring(py, 1))
     z_above = lax.ppermute(zlo, "pz", ring(pz, -1))
@@ -379,13 +400,13 @@
     inner = pl.pallas_call(
         inner_kernel,
         out_shape=whole,
-        in_specs=[SMEM] + [VMEM] * 2,
+        in_specs=[VMEM] * 2,
         out_specs=VMEM,
         scratch_shapes=[pltpu.VMEM((cx, ny + 16, nz), jnp.float32)],
         compiler_params=small(12),
         cost_estimate=cost(fields * cells * 60, fields * cells * 12),
         name="inner",
-    )(center, b, pot)
+    )(b, pot)
 
     image, h_ylo, h_zlo, h_own = pl.pallas_call(
         border_kernel,
@@ -405,20 +426,23 @@
     partial = pl.pallas_call(
         sums_kernel,
         out_shape=shaped(8 * srcs, nz),
-        in_specs=[SMEM] + [VMEM] * 3,
+        in_specs=[VMEM] * 3,
         out_specs=VMEM,
         scratch_shapes=[pltpu.VMEM((2, cx, ny, nz), jnp.float32)],
         compiler_params=small(12),
         cost_estimate=cost(fields * cells * 60, fields * cells * 12),
         name="sums",
-    )(center, b, pot, image)
+    )(b, pot, image)
 
     partial = pl.pallas_call(
         finish_kernel,
-        out_shape=shaped(8 * srcs, nz),
+        out_shape=shaped(2 * srcs, nz),
         in_specs=[VMEM] * 5,
         out_specs=VMEM,
-        scratch_shapes=[pltpu.VMEM((2, cx, 16, nz), jnp.float32)],
+        scratch_shapes=[
+            pltpu.VMEM((2, cx, 16, nz), jnp.float32),
+            pltpu.VMEM((8 * srcs, nz), jnp.float32),
+        ],
         compiler_params=small(12),
         name="finish",
     )(partial, image, h_own, h_yabove, h_zabove)
@@ -426,30 +450,22 @@
     total = total_over(total_over(partial, "py"), "pz")
 
     planes = cx // quads
-    quad = lax.axis_index("quad").reshape(1)
     table = jnp.asarray(phase_table())
-    own = lambda shift: pl.BlockSpec((1, planes, ny, nz), lambda s, q: (s + shift, q[0], 0, 0))
+    row = lax.broadcasted_iota(jnp.int32, table.shape, 0)
+    table = radius * table + jnp.where(row == 0, center - MIDDLE, 0.0)
     return pl.pallas_call(
         output_kernel,
         out_shape=shaped(MOMS, 2, srcs, planes, ny, nz),
-        grid_spec=pltpu.PrefetchScalarGridSpec(
-            num_scalar_prefetch=1,
-            grid=(srcs,),
-            in_specs=[
-                SMEM,
-                pl.BlockSpec(total.shape, lambda s, q: (0, 0)),
-                pl.BlockSpec(table.shape, lambda s, q: (0, 0)),
-                own(0),
-                own(srcs),
-                own(0),
-                own(srcs),
-            ],
-            out_specs=pl.BlockSpec((MOMS, 2, 1, planes, ny, nz), lambda s, q: (0, 0, s, 0, 0, 0)),
-            scratch_shapes=[pltpu.VMEM((4 * MOMS, 8, LANES), jnp.float32)],
-        ),
+        in_specs=[VMEM] * 4,
+        out_specs=HBM,
+        scratch_shapes=[
+            pltpu.VMEM((4 * MOMS, 8, LANES), jnp.float32),
+            pltpu.VMEM((srcs, MOMS, 2, planes, ny, nz), jnp.float32),
+            pltpu.SemaphoreType.DMA((srcs,)),
+        ],
         compiler_params=small(12),
         name="output",
-    )(quad, radius, total, table, b, b, image, image)
+    )(total, table, b, image)
 
 
 def solution(mesh):

time: 36.2 us -> 35.3 us (0.975)
  Pallas kernels: 9.72 us -> 8.91 us
  waiting for transfers between devices: 9.06 us -> 8.58 us
    ppermute x4, waiting for transfers between devices: 9.04 us -> 7.76 us  [total_over(): lax.ppermute(value, axis, [(i, i ^ bit) for i in range(count)])]
    pallas_call x1, Pallas kernels: 2.26 us -> 1.7 us  [per_device(): pl.pallas_call(output_kernel, out_shape=shaped(MOMS, 2, srcs, planes, ny,...]
    ppermute x1, waiting for transfers between devices: 0.01 us -> 0.52 us  [per_device(): z_below = lax.ppermute(zhi, 'pz', ring(pz, 1))]
  transfers between devices with their start and end apart: 10 -> 10, of which waited for: 4 -> 7; matrix products, arithmetic and copies ran while one was open for 0% -> 0% of each run, Pallas kernels for 10% -> 9%
where the time goes in v3:
time: 35.3 us; the launch traced here: 35.1 us
  starting transfers between devices  16.2 us (46%)
  Pallas kernels  8.91 us (25%)
  waiting for transfers between devices  8.58 us (24%)
  between operations  1.36 us (4%)
    ppermute x4, waiting for transfers between devices, total_over(): lax.ppermute(value, axis, [(i, i ^ bit) for i in range(count)])  7.76 us
    ppermute x4, starting transfers between devices, total_over(): lax.ppermute(value, axis, [(i, i ^ bit) for i in range(count)])  3.75 us
    ppermute x1, starting transfers between devices, per_device(): h_zabove = lax.ppermute(h_zlo, 'pz', ring(pz, -1))  3.39 us
    ppermute x1, starting transfers between devices, per_device(): z_below = lax.ppermute(zhi, 'pz', ring(pz, 1))  2.3 us
    ppermute x1, starting transfers between devices, per_device(): h_yabove = lax.ppermute(h_ylo, 'py', ring(py, -1))  2.17 us
    ppermute x1, starting transfers between devices, per_device(): z_above = lax.ppermute(zlo, 'pz', ring(pz, -1))  2.03 us
    ppermute x1, starting transfers between devices, per_device(): y_above = lax.ppermute(ylo, 'py', ring(py, -1))  2.01 us
    pallas_call x1, Pallas kernels, per_device(): pl.pallas_call(load_kernel, out_shape=(whole, shaped(cx, ny, nz), thin, t...  1.96 us
  transfers between devices with their start and end apart: 10, of which 7 were waited for; matrix products, arithmetic and copies ran while one was open for 0% of the time, Pallas kernels for 9%

profile of v3, /device:TPU:0, one launch (start us, length us, event | category | flops | bytes accessed | tf_op | source)
XLA Modules:
  0.0 35.1 jit_solution(15663039087650636006)
XLA Ops:
  0.0 2.0 %load.1 = (f32[8,16,16,128]{3,2,1,0:T(8,128)S(1)}, f32[16,16,128]{2,1,0:T(8,128)S(1)}, f32[8,16,4,128]{3,2,1,0:T(4,128)S(1)}, f32[8,16,4,128]{3,2,1,0:T(4,128)S(...) custom-call(f32[4,16,16,128]{3,2,1,0:T(8,128)} %re_hbm.1, f32[4,16,16,128]{3,2,1,0:T(8,128)} %im_hbm.1, ...), custom_call_target="tpu_custom_call" | custom-call | tf_op jit(solution)/shard_map/load/pallas_call | solution.py:383
  2.0 0.5 %collective-permute-start = (f32[8,16,4,128]{3,2,1,0:T(4,128)S(1)}, f32[8,16,4,128]{3,2,1,0:T(4,128)S(1)}, u32[]{:S(2)}, u32[]{:S(2)}) collective-permute-start(f32[8,16,4,128]{3,2,1,0:T(4,128)S(1)} %get-tuple-element.17), channel_id=1, source_target_pairs={{0,4},{4,8},{8,12},{12,0},{1,5},{5,9},{9,13},{13,1},{2,6},{6,10},{... | collective-permute-start | bytes 786440 | tf_op jit(solution)/shard_map/ppermute | solution.py:396
  2.5 2.0 %collective-permute-start.1 = (f32[8,16,4,128]{3,2,1,0:T(4,128)S(1)}, f32[8,16,4,128]{3,2,1,0:T(4,128)S(1)}, u32[]{:S(2)}, u32[]{:S(2)}) collective-permute-start(f32[8,16,4,128]{3,2,1,0:T(4,128)S(1)} %get-tuple-element.18), channel_id=1, source_target_pairs={{0,12},{4,0},{8,4},{12,8},{1,13},{5,1},{9,5},{13,9},{2,14},{6,2},{... | collective-permute-start | bytes 786440 | tf_op jit(solution)/shard_map/ppermute | solution.py:395
  4.5 2.3 %collective-permute-start.2 = (f32[32,256]{1,0:T(8,128)S(1)}, f32[32,256]{1,0:T(8,128)S(1)}, u32[]{:S(2)}, u32[]{:S(2)}) collective-permute-start(f32[32,256]{1,0:T(8,128)S(1)} %get-tuple-element.19), channel_id=1, source_target_pairs={{0,1},{1,2},{2,3},{3,0},{4,5},{5,6},{6,7},{7,4},{8,9},{9,10},{10,1... | collective-permute-start | bytes 98312 | tf_op jit(solution)/shard_map/ppermute | solution.py:398
  6.8 2.0 %collective-permute-start.3 = (f32[32,256]{1,0:T(8,128)S(1)}, f32[32,256]{1,0:T(8,128)S(1)}, u32[]{:S(2)}, u32[]{:S(2)}) collective-permute-start(f32[32,256]{1,0:T(8,128)S(1)} %get-tuple-element.20), channel_id=1, source_target_pairs={{0,3},{1,0},{2,1},{3,2},{4,7},{5,4},{6,5},{7,6},{8,11},{9,8},{10,9... | collective-permute-start | bytes 98312 | tf_op jit(solution)/shard_map/ppermute | solution.py:397
  8.8 1.5 %inner.1.inner_ref = f32[8,16,16,128]{3,2,1,0:T(8,128)S(1)} custom-call(f32[8,16,16,128]{3,2,1,0:T(8,128)S(1)} %get-tuple-element.15.b_ref, f32[16,16,128]{2,1,0:T(8,128)S(1)} %get-tuple-element.16.pot_ref), custom_call_target="tpu_custom_call" | custom-call | flops 15728640 | bytes 3145728 | tf_op jit(solution)/shard_map/inner/pallas_call | solution.py:400
  10.3 0.5 %collective-permute-done.2.zlo_ref = f32[32,256]{1,0:T(8,128)S(1)} collective-permute-done((f32[32,256]{1,0:T(8,128)S(1)}, f32[32,256]{1,0:T(8,128)S(1)}, u32[]{:S(2)}, u32[]{:S(2)}) %collective-permute-start.2) | collective-permute-done | bytes 32800 | tf_op jit(solution)/shard_map/ppermute | solution.py:398
  10.8 0.2 collective-permute-done.3.zhi_ref
  11.1 0.1 collective-permute-done.1.yhi_ref
  11.1 1.6 %border.1 = (f32[8,16,16,128]{3,2,1,0:T(8,128)S(1)}, f32[8,16,4,128]{3,2,1,0:T(4,128)S(1)}, f32[32,256]{1,0:T(8,128)S(1)}, f32[32,256]{1,0:T(8,128)S(1)}) custom-call(f32[8,16,16,128]{3,2,1,0:T(8,128)S(1)} %inner.1.inner_ref, f32[8,16,4,128]{3,2,1,0:T(4,128)S(1)} %collective-permute-done.ylo_ref, f32[8,16,4,128]{3,2,1,0:T(4,128)S(1)} %collective-permute-done.1.yhi_ref, ...), custom_call_target="tpu_custom_call" | custom-call | tf_op jit(solution)/shard_map/border/pallas_call | solution.py:411
  12.7 0.0 copy-start
  12.7 2.2 %collective-permute-start.4 = (f32[8,16,4,128]{3,2,1,0:T(4,128)S(1)}, f32[8,16,4,128]{3,2,1,0:T(4,128)S(1)}, u32[]{:S(2)}, u32[]{:S(2)}) collective-permute-start(f32[8,16,4,128]{3,2,1,0:T(4,128)S(1)} %get-tuple-element.23), channel_id=1, source_target_pairs={{0,12},{4,0},{8,4},{12,8},{1,13},{5,1},{9,5},{13,9},{2,14},{6,2},{... | collective-permute-start | bytes 786440 | tf_op jit(solution)/shard_map/ppermute | solution.py:423
  14.9 3.4 %collective-permute-start.5 = (f32[32,256]{1,0:T(8,128)S(1)}, f32[32,256]{1,0:T(8,128)S(1)}, u32[]{:S(2)}, u32[]{:S(2)}) collective-permute-start(f32[32,256]{1,0:T(8,128)S(1)} %get-tuple-element.24), channel_id=1, source_target_pairs={{0,3},{1,0},{2,1},{3,2},{4,7},{5,4},{6,5},{7,6},{8,11},{9,8},{10,9... | collective-permute-start | bytes 98312 | tf_op jit(solution)/shard_map/ppermute | solution.py:424
  18.3 1.7 %sums.1.sums_ref = f32[32,128]{1,0:T(8,128)S(1)} custom-call(f32[8,16,16,128]{3,2,1,0:T(8,128)S(1)} %get-tuple-element.15.b_ref, f32[16,16,128]{2,1,0:T(8,128)S(1)} %get-tuple-element.16.pot_ref, f32[8,16,16,128]{3,2,1,0:T(8,128)S(1)} %get-tuple-element.21.h_ref), custom_call_target="tpu_custom_call" | custom-call | flops 15728640 | bytes 3145728 | tf_op jit(solution)/shard_map/sums/pallas_call | solution.py:426
  20.1 0.5 %finish.1 = f32[8,128]{1,0:T(8,128)S(1)} custom-call(f32[32,128]{1,0:T(8,128)S(1)} %sums.1.sums_ref, f32[8,16,16,128]{3,2,1,0:T(8,128)S(1)} %get-tuple-element.21.h_ref, f32[32,256]{1,0:T(8,128)S(1)} %get-tuple-element.22.own_ref, f32[8,16,4,128]{3,2,1,0:T(4,128)S(1)} %collective-permute-done.4.yhi_ref, f32[32,256]{1,0:T(8,128)S(1)} %collective-permute-done.5.zhi_ref), custom_call_target="tpu_custom_call" | custom-call | tf_op jit(solution)/shard_map/finish/pallas_call | solution.py:437
  20.5 1.2 %collective-permute-done.6 = f32[8,128]{1,0:T(8,128)S(1)} collective-permute-done((f32[8,128]{1,0:T(8,128)S(1)}, f32[8,128]{1,0:T(8,128)S(1)}, u32[]{:S(2)}, u32[]{:S(2)}) %collective-permute-start.6) | collective-permute-done | bytes 4128 | tf_op jit(solution)/shard_map/ppermute | solution.py:347
  21.7 0.7 %collective-permute-start.7 = (f32[8,128]{1,0:T(8,128)S(1)}, f32[8,128]{1,0:T(8,128)S(1)}, u32[]{:S(2)}, u32[]{:S(2)}) collective-permute-start(f32[8,128]{1,0:T(8,128)S(1)} %add.16), channel_id=1, source_target_pairs={{0,8},{4,12},{8,0},{12,4},{1,9},{5,13},{9,1},{13,5},{2,10},{6,14},... | collective-permute-start | bytes 12296 | tf_op jit(solution)/shard_map/ppermute | solution.py:347
  23.1 2.3 %collective-permute-done.7 = f32[8,128]{1,0:T(8,128)S(1)} collective-permute-done((f32[8,128]{1,0:T(8,128)S(1)}, f32[8,128]{1,0:T(8,128)S(1)}, u32[]{:S(2)}, u32[]{:S(2)}) %collective-permute-start.7) | collective-permute-done | bytes 4128 | tf_op jit(solution)/shard_map/ppermute | solution.py:347
  25.3 0.5 %collective-permute-start.8 = (f32[8,128]{1,0:T(8,128)S(1)}, f32[8,128]{1,0:T(8,128)S(1)}, u32[]{:S(2)}, u32[]{:S(2)}) collective-permute-start(f32[8,128]{1,0:T(8,128)S(1)} %add.17), channel_id=1, source_target_pairs={{0,1},{1,0},{2,3},{3,2},{4,5},{5,4},{6,7},{7,6},{8,9},{9,8},{10,11... | collective-permute-start | bytes 12296 | tf_op jit(solution)/shard_map/ppermute | solution.py:347
  26.5 2.4 %collective-permute-done.8 = f32[8,128]{1,0:T(8,128)S(1)} collective-permute-done((f32[8,128]{1,0:T(8,128)S(1)}, f32[8,128]{1,0:T(8,128)S(1)}, u32[]{:S(2)}, u32[]{:S(2)}) %collective-permute-start.8) | collective-permute-done | bytes 4128 | tf_op jit(solution)/shard_map/ppermute | solution.py:347
  28.9 2.5 %collective-permute-start.9 = (f32[8,128]{1,0:T(8,128)S(1)}, f32[8,128]{1,0:T(8,128)S(1)}, u32[]{:S(2)}, u32[]{:S(2)}) collective-permute-start(f32[8,128]{1,0:T(8,128)S(1)} %add.18), channel_id=1, source_target_pairs={{0,2},{1,3},{2,0},{3,1},{4,6},{5,7},{6,4},{7,5},{8,10},{9,11},{10,... | collective-permute-start | bytes 12296 | tf_op jit(solution)/shard_map/ppermute | solution.py:347
  31.4 0.1 multiply_add_fusion.table_ref
  31.5 1.9 %collective-permute-done.9 = f32[8,128]{1,0:T(8,128)S(1)} collective-permute-done((f32[8,128]{1,0:T(8,128)S(1)}, f32[8,128]{1,0:T(8,128)S(1)}, u32[]{:S(2)}, u32[]{:S(2)}) %collective-permute-start.9) | collective-permute-done | bytes 4128 | tf_op jit(solution)/shard_map/ppermute | solution.py:347
  33.4 1.7 %output.1 = f32[4,2,4,8,16,128]{5,4,3,2,1,0:T(8,128)} custom-call(f32[8,128]{1,0:T(8,128)S(1)} %add.19.tot_ref, f32[16,128]{1,0:T(8,128)S(1)} %multiply_add_fusion.table_ref, f32[8,16,16,128]{3,2,1,0:T(8,128)S(1)} %get-tuple-element.15.b_ref, f32[8,16,16,128]{3,2,1,0:T(8,128)S(1)} %get-tuple-element.21.h_ref), custom_call_target="tpu_custom_call" | custom-call | tf_op jit(solution)/shard_map/output/pallas_call | solution.py:456
  (10 shorter events, 0.0 us)
Async XLA Ops:
  2.0 9.1 %collective-permute-start = (f32[8,16,4,128]{3,2,1,0:T(4,128)S(1)}, f32[8,16,4,128]{3,2,1,0:T(4,128)S(1)}, u32[]{:S(2)}, u32[]{:S(2)}) collective-permute-start(f32[8,16,4,128]{3,2,1,0:T(4,128)S(1)} %get-tuple-element.17), channel_id=1, source_target_pairs={{0,4},{4,8},{8,12},{12,0},{1,5},{5,9},{9,13},{13,1},{2,6},{6,10},{... | collective-permute-start | bytes 786440 | tf_op jit(solution)/shard_map/ppermute | solution.py:396
  2.5 8.6 %collective-permute-start.1 = (f32[8,16,4,128]{3,2,1,0:T(4,128)S(1)}, f32[8,16,4,128]{3,2,1,0:T(4,128)S(1)}, u32[]{:S(2)}, u32[]{:S(2)}) collective-permute-start(f32[8,16,4,128]{3,2,1,0:T(4,128)S(1)} %get-tuple-element.18), channel_id=1, source_target_pairs={{0,12},{4,0},{8,4},{12,8},{1,13},{5,1},{9,5},{13,9},{2,14},{6,2},{... | collective-permute-start | bytes 786440 | tf_op jit(solution)/shard_map/ppermute | solution.py:395
  4.5 6.3 %collective-permute-start.2 = (f32[32,256]{1,0:T(8,128)S(1)}, f32[32,256]{1,0:T(8,128)S(1)}, u32[]{:S(2)}, u32[]{:S(2)}) collective-permute-start(f32[32,256]{1,0:T(8,128)S(1)} %get-tuple-element.19), channel_id=1, source_target_pairs={{0,1},{1,2},{2,3},{3,0},{4,5},{5,6},{6,7},{7,4},{8,9},{9,10},{10,1... | collective-permute-start | bytes 98312 | tf_op jit(solution)/shard_map/ppermute | solution.py:398
  6.8 4.3 %collective-permute-start.3 = (f32[32,256]{1,0:T(8,128)S(1)}, f32[32,256]{1,0:T(8,128)S(1)}, u32[]{:S(2)}, u32[]{:S(2)}) collective-permute-start(f32[32,256]{1,0:T(8,128)S(1)} %get-tuple-element.20), channel_id=1, source_target_pairs={{0,3},{1,0},{2,1},{3,2},{4,7},{5,4},{6,5},{7,6},{8,11},{9,8},{10,9... | collective-permute-start | bytes 98312 | tf_op jit(solution)/shard_map/ppermute | solution.py:397
  12.7 18.7 %copy-start = (f32[16,128]{1,0:T(8,128)S(1)}, f32[16,128]{1,0:T(8,128)}, u32[]{:S(2)}) copy-start(f32[16,128]{1,0:T(8,128)} %constant.9.clone) | copy-start | bytes 24580
  12.7 7.3 %collective-permute-start.4 = (f32[8,16,4,128]{3,2,1,0:T(4,128)S(1)}, f32[8,16,4,128]{3,2,1,0:T(4,128)S(1)}, u32[]{:S(2)}, u32[]{:S(2)}) collective-permute-start(f32[8,16,4,128]{3,2,1,0:T(4,128)S(1)} %get-tuple-element.23), channel_id=1, source_target_pairs={{0,12},{4,0},{8,4},{12,8},{1,13},{5,1},{9,5},{13,9},{2,14},{6,2},{... | collective-permute-start | bytes 786440 | tf_op jit(solution)/shard_map/ppermute | solution.py:423
  14.9 5.1 %collective-permute-start.5 = (f32[32,256]{1,0:T(8,128)S(1)}, f32[32,256]{1,0:T(8,128)S(1)}, u32[]{:S(2)}, u32[]{:S(2)}) collective-permute-start(f32[32,256]{1,0:T(8,128)S(1)} %get-tuple-element.24), channel_id=1, source_target_pairs={{0,3},{1,0},{2,1},{3,2},{4,7},{5,4},{6,5},{7,6},{8,11},{9,8},{10,9... | collective-permute-start | bytes 98312 | tf_op jit(solution)/shard_map/ppermute | solution.py:424
  20.5 1.2 %collective-permute-start.6 = (f32[8,128]{1,0:T(8,128)S(1)}, f32[8,128]{1,0:T(8,128)S(1)}, u32[]{:S(2)}, u32[]{:S(2)}) collective-permute-start(f32[8,128]{1,0:T(8,128)S(1)} %finish.1), channel_id=1, source_target_pairs={{0,4},{4,0},{8,12},{12,8},{1,5},{5,1},{9,13},{13,9},{2,6},{6,2},{1... | collective-permute-start | bytes 12296 | tf_op jit(solution)/shard_map/ppermute | solution.py:347
  21.7 3.6 %collective-permute-start.7 = (f32[8,128]{1,0:T(8,128)S(1)}, f32[8,128]{1,0:T(8,128)S(1)}, u32[]{:S(2)}, u32[]{:S(2)}) collective-permute-start(f32[8,128]{1,0:T(8,128)S(1)} %add.16), channel_id=1, source_target_pairs={{0,8},{4,12},{8,0},{12,4},{1,9},{5,13},{9,1},{13,5},{2,10},{6,14},... | collective-permute-start | bytes 12296 | tf_op jit(solution)/shard_map/ppermute | solution.py:347
  25.3 3.6 %collective-permute-start.8 = (f32[8,128]{1,0:T(8,128)S(1)}, f32[8,128]{1,0:T(8,128)S(1)}, u32[]{:S(2)}, u32[]{:S(2)}) collective-permute-start(f32[8,128]{1,0:T(8,128)S(1)} %add.17), channel_id=1, source_target_pairs={{0,1},{1,0},{2,3},{3,2},{4,5},{5,4},{6,7},{7,6},{8,9},{9,8},{10,11... | collective-permute-start | bytes 12296 | tf_op jit(solution)/shard_map/ppermute | solution.py:347
  28.9 4.5 %collective-permute-start.9 = (f32[8,128]{1,0:T(8,128)S(1)}, f32[8,128]{1,0:T(8,128)S(1)}, u32[]{:S(2)}, u32[]{:S(2)}) collective-permute-start(f32[8,128]{1,0:T(8,128)S(1)} %add.18), channel_id=1, source_target_pairs={{0,2},{1,3},{2,0},{3,1},{4,6},{5,7},{6,4},{7,5},{8,10},{9,11},{10,... | collective-permute-start | bytes 12296 | tf_op jit(solution)/shard_map/ppermute | solution.py:347

commit v4 on v3

v4 whole, which is shorter than its diff:
```python
import functools
import math

import jax
import jax.numpy as jnp
import numpy as np
from jax import lax
from jax.experimental import pallas as pl
from jax.experimental.pallas import tpu as pltpu
from jax.sharding import PartitionSpec as P

QPTS = 8
MOMS = 4
REACH = 4
LANES = 128

stencil_weights = (-205.0 / 72.0, 8.0 / 5.0, -1.0 / 5.0, 8.0 / 315.0, -1.0 / 560.0)
DIAG = -1.5 * stencil_weights[0]
MIDDLE = 5.25
SIDE = tuple(-0.5 * w for w in stencil_weights)
HIGHEST = lax.Precision.HIGHEST


def dot(left, right, dims):
    return lax.dot_general(
        left, right, (dims, ((), ())), precision=HIGHEST, preferred_element_type=jnp.float32
    )


def band(shape, offset, signs, scale=1.0):
    step = offset + lax.broadcasted_iota(jnp.int32, shape, 0) - lax.broadcasted_iota(jnp.int32, shape, 1)
    out = jnp.zeros(shape, jnp.float32)
    for k in range(1, REACH + 1):
        for sign in signs:
            out = jnp.where(step == sign * k, scale * SIDE[k], out)
    return out


def split(value):
    high = value.astype(jnp.bfloat16)
    return high, (value - high.astype(jnp.float32)).astype(jnp.bfloat16)


def dot_split(left, right):
    rows = jnp.concatenate([left[0], left[1], left[0]], axis=1)
    cols = jnp.concatenate([right[0], right[0], right[1]], axis=0)
    return lax.dot_general(rows, cols, (((1,), (0,)), ((), ())), preferred_element_type=jnp.float32)


def gather_edges(gathered, f, value):
    lane = lax.broadcasted_iota(jnp.int32, value.shape, 1)
    moved = pltpu.roll(value, 4 * REACH * f + 2 * REACH, 1)
    return jnp.where(lane // (4 * REACH) == f, moved, gathered)


def beside(owned, cx):
    return [x % cx for x in range(-REACH, owned + REACH)]


def load_kernel(
    owned, re_hbm, im_hbm, pot_hbm, b_ref, pot_ref, up_ref, down_ref, zup_ref, zdown_ref, edge_ref, sems
):
    fields, cx, ny, nz = b_ref.shape
    srcs = fields // 2
    parts = cx // owned
    reach = up_ref.shape[0] // (fields * REACH)
    near = beside(owned, cx)
    first = lax.axis_index("quad")
    copies = []
    for f in range(fields + 1):
        source = pot_hbm if f == fields else (re_hbm, im_hbm)[f // srcs].at[f % srcs]
        target = pot_ref if f == fields else b_ref.at[f]
        group = []
        for j in range(parts):
            at = pl.multiple_of(lax.rem(first + j, parts) * owned, owned)
            group.append(
                pltpu.make_async_copy(
                    source.at[pl.ds(at, owned)], target.at[pl.ds(j * owned, owned)], sems.at[f, j]
                )
            )
        copies.append(group)
    for group in copies:
        for copy in group:
            copy.start()
    edge_ref[...] = jnp.zeros(edge_ref.shape, jnp.float32)
    far = fields * len(near)
    for f in range(fields):
        for copy in copies[f]:
            copy.wait()
        for x in range(reach):
            at = (f * reach + x) * REACH
            up_ref[at : at + REACH, :] = b_ref[f, x, ny - REACH : ny, :]
        for i, x in enumerate(near):
            at = (f * len(near) + i) * REACH
            down_ref[at : at + REACH, :] = b_ref[f, x, 0:REACH, :]
        for x in range(owned):
            at = (far + f * owned + x) * REACH
            down_ref[at : at + REACH, :] = b_ref[f, x, REACH : 2 * REACH, :]
        edge_ref[...] = gather_edges(edge_ref[...], f, b_ref[f].reshape(cx * ny, nz))
    for copy in copies[fields]:
        copy.wait()
    pot_ref[...] = pot_ref[...] + (DIAG - MIDDLE)
    for x in range(owned):
        at = (far + fields * owned + x) * REACH
        down_ref[at : at + REACH, :] = pot_ref[x, 0:REACH, :]
    turned = edge_ref[...].T
    rows = fields * REACH
    for f in range(fields):
        at = 4 * REACH * f
        low, high = f * REACH, (f + 1) * REACH
        zup_ref[rows + low : rows + high, :] = turned[at : at + REACH]
        zup_ref[low:high, :] = turned[at + REACH : at + 2 * REACH]
        zdown_ref[low:high, :] = turned[at + 2 * REACH : at + 3 * REACH]
        zdown_ref[rows + low : rows + high, :] = turned[at + 3 * REACH : at + 4 * REACH]
    turned = pltpu.roll(pot_ref[...].reshape(cx * ny, nz), 2 * REACH, 1).T
    zup_ref[2 * rows : 2 * rows + REACH, :] = turned[REACH : 2 * REACH]
    zup_ref[2 * rows + REACH : 2 * rows + 2 * REACH, :] = turned[0:REACH]
    zdown_ref[2 * rows : 2 * rows + 2 * REACH, :] = turned[2 * REACH : 4 * REACH]


def phase_table():
    lane = np.arange(LANES)
    angle = 2.0 * math.pi * (lane % QPTS + 0.5) / QPTS
    rows = [np.cos(angle), np.sin(angle)]
    for k in range(1, MOMS + 1):
        rows.append(np.where(lane < QPTS, np.cos(k * angle), 0.0) / QPTS)
        rows.append(np.where(lane < QPTS, np.sin(k * angle), 0.0) / QPTS)
    rows += [np.zeros(LANES)] * (-len(rows) % 8)
    return np.stack(rows).astype(np.float32)


def inner_kernel(b_ref, pot_ref, out_ref, pad_ref):
    fields, cx, ny, nz = b_ref.shape
    reach = out_ref.shape[1]
    matrix = split(band((nz, nz), 0, (1, -1)))
    zero = jnp.zeros((reach, 8, nz), jnp.float32)
    pad_ref[:, 0:8, :] = zero
    pad_ref[:, 8 + ny : 16 + ny, :] = zero
    for f in range(fields):
        own = b_ref[f, 0:reach].reshape(reach * ny, nz)
        out_ref[f] = dot_split(split(own), matrix).reshape(reach, ny, nz)

    def field(f, _):
        pad_ref[:, 8 : 8 + ny, :] = b_ref[f, 0:reach]
        for x in range(reach):
            total = out_ref[f, x] + pot_ref[x] * b_ref[f, x]
            for k in range(1, REACH + 1):
                sides = b_ref[f, (x + k) % cx] + b_ref[f, (x - k) % cx]
                sides = sides + pad_ref[x, 8 + k : 8 + k + ny, :]
                sides = sides + pad_ref[x, 8 - k : 8 - k + ny, :]
                total = total + SIDE[k] * sides
            out_ref[f, x] = total
        return 0

    lax.fori_loop(0, fields, field, 0)


def links(row_at, col_at, row_field, col_field):
    step = jnp.abs(row_at - col_at)
    out = jnp.zeros(step.shape, jnp.float32)
    for k in range(1, REACH + 1):
        out = jnp.where((step == k) & (row_field == col_field), SIDE[k], out)
    return out


def layer_of(index, starts, rows):
    layer = jnp.full(index.shape, 1 << 20, jnp.int32)
    for n, start in enumerate(starts):
        layer = jnp.where(index // rows == n, start + index % REACH, layer)
    return layer, index % rows // REACH


def border_kernel(owned, inner_ref, below_ref, above_ref, zbelow_ref, zabove_ref, out_ref, u_ref, pad_ref, edge_ref):
    fields, reach, ny, nz = inner_ref.shape
    rows = fields * REACH
    count = owned + 2 * REACH
    turned = jnp.concatenate([zbelow_ref[0:rows], zabove_ref[0:rows]], axis=0).T
    turned = split(turned[0 : reach * ny])
    shape = (2 * rows, nz)
    layer, owner = layer_of(lax.broadcasted_iota(jnp.int32, shape, 0), (-REACH, nz), rows)
    cell = lax.broadcasted_iota(jnp.int32, shape, 1)
    for f in range(fields):
        weights = split(links(layer, cell, owner, f))
        out_ref[f] = dot_split(turned, weights).reshape(reach, ny, nz)
    zero = jnp.zeros((reach, 16, nz), jnp.float32)
    pad_ref[0] = zero
    pad_ref[1] = zero
    edge_ref[...] = jnp.zeros(edge_ref.shape, jnp.float32)
    for f in range(fields):
        for x in range(reach):
            at = (f * reach + x) * REACH
            pad_ref[0, x, 8 - REACH : 8, :] = below_ref[at : at + REACH, :]
            at = (f * count + REACH + x) * REACH
            pad_ref[1, x, 8 : 8 + REACH, :] = above_ref[at : at + REACH, :]
        for x in range(reach):
            low = SIDE[1] * pad_ref[0, x, 7:15, :]
            high = SIDE[1] * pad_ref[1, x, 1:9, :]
            for k in range(2, REACH + 1):
                low = low + SIDE[k] * pad_ref[0, x, 8 - k : 16 - k, :]
                high = high + SIDE[k] * pad_ref[1, x, k : 8 + k, :]
            total = out_ref[f, x] + inner_ref[f, x]
            middle = [total[8 : ny - 8]] if ny > 16 else []
            first, last = total[0:8] + low, total[ny - 8 : ny] + high
            out_ref[f, x] = jnp.concatenate([first] + middle + [last], axis=0)
            if x < owned:
                u = jnp.concatenate([first + low] + middle + [last + 3.0 * high], axis=0)
                spot = pl.ds(x * ny, ny)
                edge_ref[spot, :] = gather_edges(edge_ref[spot, :], f, u)
    turned = edge_ref[...].T
    for f in range(fields):
        at = 4 * REACH * f
        low, high = f * REACH, (f + 1) * REACH
        u_ref[low:high, :] = turned[at + 2 * REACH : at + 3 * REACH]
        u_ref[rows + low : rows + high, :] = turned[at + REACH : at + 2 * REACH]


def fold(value):
    return jnp.sum(value, axis=0, keepdims=True)


def sums_kernel(
    owned,
    b_ref,
    pot_ref,
    h_ref,
    u_ref,
    above_ref,
    zup_ref,
    zdown_ref,
    zbelow_ref,
    zabove_ref,
    out_ref,
    acc_ref,
    step_ref,
    far_ref,
):
    fields, cx, ny, nz = b_ref.shape
    srcs = fields // 2
    count = owned + 2 * REACH
    matrix = split(band((nz, nz), 0, (1,), 2.0))
    row = lax.broadcasted_iota(jnp.int32, (ny, nz), 0)
    inside = [row < ny - k for k in range(REACH + 1)]
    for f in range(fields):
        own = h_ref[f, 0:owned].reshape(owned * ny, nz)
        step_ref[f] = dot_split(split(own), matrix).reshape(owned, ny, nz)

    matrix = split(band((nz, nz), 0, (1, -1)))
    for f in range(fields):
        at = (f * count + REACH) * REACH
        far_ref[f] = dot_split(split(above_ref[at : at + owned * REACH, :]), matrix)
    quad_row = lax.broadcasted_iota(jnp.int32, (8, nz), 0) % REACH
    early = lax.broadcasted_iota(jnp.int32, (8, nz), 0) < REACH

    def top(ref, f, x):
        return jnp.where(early, pltpu.roll(ref[f, x, ny - 8 : ny, :], REACH, 0), ref[f, x + 1, ny - 8 : ny, :])

    def shifted(lower, upper, k):
        if k == REACH:
            return lower
        return jnp.where(quad_row >= k, pltpu.roll(upper, k, 0), pltpu.roll(lower, REACH + k, 0))

    def raised(lower, upper, k):
        if k == REACH:
            return upper
        return jnp.where(quad_row < REACH - k, pltpu.roll(lower, 8 - k, 0), pltpu.roll(upper, REACH - k, 0))

    for s in range(srcs):
        total = [jnp.zeros((ny, nz), jnp.float32) for _ in range(8)]
        for x in range(owned):
            local = pot_ref[x]
            br, bi = b_ref[s, x], b_ref[srcs + s, x]
            h, g = [], []
            for part in range(2):
                f = part * srcs + s
                own = h_ref[f, x]
                image = step_ref[f, x] + local * own
                for k in range(1, REACH + 1):
                    up = jnp.where(inside[k], pltpu.roll(own, ny - k, 0), 0.0)
                    image = image + (2.0 * SIDE[k]) * (h_ref[f, (x + k) % cx] + up)
                h.append(own)
                g.append(image)
            terms = (
                br * br - bi * bi,
                2.0 * (br * bi),
                br * h[0] - bi * h[1],
                br * h[1] + bi * h[0],
                h[0] * h[0] - h[1] * h[1],
                2.0 * (h[0] * h[1]),
                h[0] * g[0] - h[1] * g[1],
                h[0] * g[1] + h[1] * g[0],
            )
            total = [t + v for t, v in zip(total, terms)]
        cross = [jnp.zeros((8, nz), jnp.float32) for _ in range(2)]
        for x in range(0, owned, 2):
            at = (fields * (count + owned) + x) * REACH
            local = above_ref[at : at + 8, :]
            left, right = [], []
            for part in range(2):
                f = part * srcs + s
                at = (f * count + REACH + x) * REACH
                near = above_ref[at : at + 8, :]
                start = (fields * count + f * owned + x) * REACH
                far = above_ref[start : start + 8, :]
                own, own_h = top(b_ref, f, x), top(h_ref, f, x)
                image = far_ref[f, x * REACH : x * REACH + 8, :] + local * near
                pull = SIDE[REACH] * own_h
                for k in range(1, REACH + 1):
                    sides = above_ref[at + k * REACH : at + k * REACH + 8, :]
                    sides = sides + above_ref[at - k * REACH : at - k * REACH + 8, :]
                    sides = sides + raised(near, far, k) + shifted(own, near, k)
                    image = image + SIDE[k] * sides
                    if k < REACH:
                        pull = pull + SIDE[k] * jnp.where(quad_row < k, pltpu.roll(own_h, REACH + k, 0), 0.0)
                left.append(pull)
                right.append(image)
            cross[0] = cross[0] + (left[0] * right[0] - left[1] * right[1])
            cross[1] = cross[1] + (left[0] * right[1] + left[1] * right[0])
        for i in range(8):
            value = fold(total[i])
            if i >= 6:
                value = value + 2.0 * fold(cross[i - 6])
            acc_ref[i * srcs + s : i * srcs + s + 1, :] = value

    rows = fields * REACH
    width = cx * ny
    low, high = zdown_ref[0:rows, :], zup_ref[0:rows, :]
    below, above = zbelow_ref[0:rows, :], zabove_ref[0:rows, :]
    outer = jnp.concatenate([below, above], axis=0)
    stack = jnp.concatenate(
        [low, high, below, zbelow_ref[rows : 2 * rows, :], above, zabove_ref[rows : 2 * rows, :], outer], axis=0
    )
    shape = (2 * rows, 8 * rows)
    row_at, row_field = layer_of(lax.broadcasted_iota(jnp.int32, shape, 0), (-REACH, nz), rows)
    col = lax.broadcasted_iota(jnp.int32, shape, 1)
    starts = (0, nz - REACH, -REACH, -2 * REACH, nz, nz + REACH)
    col_at, col_field = layer_of(col, starts, rows)
    mix = split(links(row_at, col_at, row_field, col_field))
    image = dot_split(mix, split(stack))
    local = jnp.concatenate(
        [zbelow_ref[2 * rows : 2 * rows + REACH, :]] * fields + [zabove_ref[2 * rows : 2 * rows + REACH, :]] * fields,
        axis=0,
    )
    image = image + local * outer
    lane = lax.broadcasted_iota(jnp.int32, (2 * rows, width), 1)
    y = lane % ny
    for k in range(1, REACH + 1):
        sides = pltpu.roll(outer, ny * k, 1) + pltpu.roll(outer, width - ny * k, 1)
        sides = sides + jnp.where(y >= k, pltpu.roll(outer, k, 1), 0.0)
        sides = sides + jnp.where(y < ny - k, pltpu.roll(outer, width - k, 1), 0.0)
        image = image + SIDE[k] * sides
    shape = (4 * rows, 4 * rows)
    row = lax.broadcasted_iota(jnp.int32, shape, 0)
    col = lax.broadcasted_iota(jnp.int32, shape, 1)
    row_at, row_field = layer_of(row % (2 * rows), (0, nz - REACH), rows)
    col_at, col_field = layer_of(col % (2 * rows), (-REACH, nz), rows)
    mix = jnp.where(row // (2 * rows) == col // (2 * rows), links(row_at, col_at, row_field, col_field), 0.0)
    reached = dot_split(split(mix), split(jnp.concatenate([image, outer], axis=0)))

    def around(value):
        out = jnp.zeros(value.shape, jnp.float32)
        for k in range(1, REACH + 1):
            sides = jnp.where(y >= ny - k, pltpu.roll(value, ny - k, 1), 0.0)
            sides = sides + jnp.where(y < k, pltpu.roll(value, width + k - ny, 1), 0.0)
            out = out + SIDE[k] * sides
        return out

    weight = jnp.where(lane < owned * ny, jnp.where(y >= ny // 2, 3.0, 1.0), 0.0)
    edges = around(jnp.concatenate([low, high], axis=0)) * weight
    turned = around(reached[2 * rows : 4 * rows])
    half = rows // 2

    def product(left, right):
        re = im = 0.0
        for at in (0, rows):
            lr, li = left[at : at + half], left[at + half : at + rows]
            rr, ri = right[at : at + half], right[at + half : at + rows]
            re = re + (lr * rr - li * ri)
            im = im + (lr * ri + li * rr)
        return re, im

    first = product(u_ref[...], reached[0 : 2 * rows])
    second = product(edges, turned)
    for c in range(2):
        both = first[c] + second[c]
        both = sum(both[:, at : at + nz] for at in range(0, width, nz))
        for s in range(srcs):
            at = (6 + c) * srcs + s
            acc_ref[at : at + 1, :] = acc_ref[at : at + 1, :] + fold(both[s * REACH : (s + 1) * REACH])

    column = jnp.sum(acc_ref[...], axis=1, keepdims=True)
    row = lax.broadcasted_iota(jnp.int32, acc_ref.shape, 0)
    lane = lax.broadcasted_iota(jnp.int32, acc_ref.shape, 1)
    out_ref[...] = jnp.broadcast_to(fold(jnp.where(row == lane, column, 0.0)), out_ref.shape)


def complex_mul(left, right):
    return (left[0] * right[0] - left[1] * right[1], left[0] * right[1] + left[1] * right[0])


def complex_div(left, right):
    norm_sq = right[0] * right[0] + right[1] * right[1]
    return (
        (left[0] * right[0] + left[1] * right[1]) / norm_sq,
        (left[1] * right[0] - left[0] * right[1]) / norm_sq,
    )


def output_kernel(tot_ref, table_ref, b_ref, h_ref, out_hbm, coef_ref, buf_ref, sems):
    fields, cx, ny, nz = b_ref.shape
    srcs = fields // 2
    planes = buf_ref.shape[3]
    shape = (srcs, LANES)
    wide = jnp.broadcast_to(fold(tot_ref[...]), (8 * srcs, LANES))
    row = lax.broadcasted_iota(jnp.int32, wide.shape, 0)
    lane = lax.broadcasted_iota(jnp.int32, wide.shape, 1)
    wide = jnp.broadcast_to(jnp.sum(jnp.where(row == lane, wide, 0.0), axis=1, keepdims=True), wide.shape)
    nu = [
        (wide[2 * k * srcs : (2 * k + 1) * srcs], wide[(2 * k + 1) * srcs : (2 * k + 2) * srcs])
        for k in range(4)
    ]
    zeta = (
        jnp.broadcast_to(table_ref[0:1, :], shape),
        jnp.broadcast_to(table_ref[1:2, :], shape),
    )
    scaled = complex_mul(zeta, nu[0])
    alpha_first = complex_div(nu[0], (scaled[0] - nu[1][0], scaled[1] - nu[1][1]))
    mean = complex_div(nu[1], nu[0])
    t = complex_mul(mean, nu[1])
    spread2 = (nu[2][0] - t[0], nu[2][1] - t[1])
    t = complex_mul(mean, (nu[2][0] + spread2[0], nu[2][1] + spread2[1]))
    spread3 = (nu[3][0] - t[0], nu[3][1] - t[1])
    square = complex_mul(alpha_first, alpha_first)
    rho_next = complex_mul(square, spread2)
    beta = complex_div(rho_next, nu[0])
    first_part = complex_mul(zeta, rho_next)
    second = complex_mul(square, spread3)
    third = complex_div(complex_mul(beta, rho_next), alpha_first)
    alpha_next = complex_div(
        rho_next, (first_part[0] - second[0] - third[0], first_part[1] - second[1] - third[1])
    )
    t = complex_mul(alpha_first, mean)
    carried = complex_mul(alpha_next, (beta[0] - t[0], beta[1] - t[1]))
    on_source = (alpha_first[0] + carried[0], alpha_first[1] + carried[1])
    on_image = complex_mul(alpha_next, alpha_first)
    for k in range(MOMS):
        weight = (
            jnp.broadcast_to(table_ref[2 + 2 * k : 3 + 2 * k, :], shape),
            jnp.broadcast_to(table_ref[3 + 2 * k : 4 + 2 * k, :], shape),
        )
        for n, value in enumerate((on_source, on_image)):
            both = complex_mul(weight, value)
            for c in range(2):
                column = jnp.sum(both[c], axis=1, keepdims=True)
                coef_ref[4 * k + 2 * n + c, 0:srcs, :] = jnp.broadcast_to(column, shape)

    copies = []
    for s in range(srcs):
        for k in range(MOMS):
            c = [
                jnp.broadcast_to(coef_ref[4 * k + n, s : s + 1, :], (ny, nz)) for n in range(4)
            ]
            for x in range(planes):
                br, bi = b_ref[s, x], b_ref[srcs + s, x]
                hr, hi = h_ref[s, x], h_ref[srcs + s, x]
                buf_ref[s, k, 0, x] = c[0] * br - c[1] * bi + (c[2] * hr - c[3] * hi)
                buf_ref[s, k, 1, x] = c[0] * bi + c[1] * br + (c[2] * hi + c[3] * hr)
        copy = pltpu.make_async_copy(buf_ref.at[s], out_hbm.at[:, :, s], sems.at[s])
        copy.start()
        copies.append(copy)
    for copy in copies:
        copy.wait()


def ring(count, step):
    return [(i, (i + step) % count) for i in range(count)]


ANY = pl.BlockSpec(memory_space=pl.ANY)
HBM = pl.BlockSpec(memory_space=pltpu.HBM)
VMEM = pl.BlockSpec(memory_space=pltpu.VMEM)
SMEM = pl.BlockSpec(memory_space=pltpu.SMEM)


def shaped(*dims):
    return jax.ShapeDtypeStruct(dims, jnp.float32)


def small(mib):
    return pltpu.CompilerParams(vmem_limit_bytes=mib << 20)


def cost(flops, nbytes):
    return pl.CostEstimate(flops=flops, bytes_accessed=nbytes, transcendentals=0)


def per_device(source_real, source_imag, potential, center, radius):
    srcs, cx, ny, nz = source_real.shape
    fields = 2 * srcs
    py, pz, quads = lax.axis_size("py"), lax.axis_size("pz"), lax.axis_size("quad")
    owned = cx // quads
    reach = min(cx, owned + REACH)
    count = owned + 2 * REACH
    cells = reach * ny * nz

    source_real, source_imag, potential = (
        pltpu.with_memory_space_constraint(a, pltpu.HBM)
        for a in (source_real, source_imag, potential)
    )
    part = shaped(fields, reach, ny, nz)
    flat = shaped(2 * fields * REACH + 2 * REACH, cx * ny)
    b, pot, up, down, zup, zdown = pl.pallas_call(
        functools.partial(load_kernel, owned),
        out_shape=(
            shaped(fields, cx, ny, nz),
            shaped(cx, ny, nz),
            shaped(fields * reach * REACH, nz),
            shaped((fields * (count + owned) + owned) * REACH, nz),
            flat,
            flat,
        ),
        in_specs=[HBM] * 3,
        out_specs=(VMEM,) * 6,
        scratch_shapes=[
            pltpu.VMEM((cx * ny, nz), jnp.float32),
            pltpu.SemaphoreType.DMA((fields + 1, quads)),
        ],
        compiler_params=small(8),
        name="load",
    )(source_real, source_imag, potential)
    above = lax.ppermute(down, "py", ring(py, -1))
    below = lax.ppermute(up, "py", ring(py, 1))
    zabove = lax.ppermute(zdown, "pz", ring(pz, -1))
    zbelow = lax.ppermute(zup, "pz", ring(pz, 1))

    inner = pl.pallas_call(
        inner_kernel,
        out_shape=part,
        in_specs=[VMEM] * 2,
        out_specs=VMEM,
        scratch_shapes=[pltpu.VMEM((reach, ny + 16, nz), jnp.float32)],
        compiler_params=small(12),
        cost_estimate=cost(fields * cells * 60, fields * cells * 12),
        name="inner",
    )(b, pot)

    image, u = pl.pallas_call(
        functools.partial(border_kernel, owned),
        out_shape=(part, shaped(2 * fields * REACH, cx * ny)),
        in_specs=[VMEM] * 5,
        out_specs=(VMEM,) * 2,
        scratch_shapes=[
            pltpu.VMEM((2, reach, 16, nz), jnp.float32),
            pltpu.VMEM((cx * ny, nz), jnp.float32),
        ],
        compiler_params=small(12),
        name="border",
    )(inner, below, above, zbelow, zabove)

    devices = quads * py * pz
    partial = pl.pallas_call(
        functools.partial(sums_kernel, owned),
        out_shape=shaped(devices, LANES),
        in_specs=[VMEM] * 9,
        out_specs=VMEM,
        scratch_shapes=[
            pltpu.VMEM((8 * srcs, nz), jnp.float32),
            pltpu.VMEM((fields, owned, ny, nz), jnp.float32),
            pltpu.VMEM((fields, owned * REACH, nz), jnp.float32),
        ],
        compiler_params=small(12),
        name="sums",
    )(b, pot, image, u, above, zup, zdown, zbelow, zabove)

    total = lax.all_to_all(partial, ("quad", "py", "pz"), 0, 0)

    table = jnp.asarray(phase_table())
    row = lax.broadcasted_iota(jnp.int32, table.shape, 0)
    table = radius * table + jnp.where(row == 0, center - MIDDLE, 0.0)
    return pl.pallas_call(
        output_kernel,
        out_shape=shaped(MOMS, 2, srcs, owned, ny, nz),
        in_specs=[VMEM] * 4,
        out_specs=HBM,
        scratch_shapes=[
            pltpu.VMEM((4 * MOMS, 8, LANES), jnp.float32),
            pltpu.VMEM((srcs, MOMS, 2, owned, ny, nz), jnp.float32),
            pltpu.SemaphoreType.DMA((srcs,)),
        ],
        compiler_params=small(12),
        name="output",
    )(total, table, b, image)


def solution(mesh):
    in_specs = (P(None, None, "py", "pz"), P(None, None, "py", "pz"), P(None, "py", "pz"), P(), P())
    out_specs = P(None, None, None, "quad", "py", "pz")
    return jax.shard_map(
        per_device, mesh=mesh, in_specs=in_specs, out_specs=out_specs, check_vma=False
    )
```

time: 35.3 us -> 30.9 us (0.88)
  starting transfers between devices: 16.2 us -> 12.3 us
  Pallas kernels: 8.91 us -> 8.44 us
    ppermute x10 -> x4, starting transfers between devices: 16.2 us -> 6.31 us  [the longest x1 2.49 us: per_device(): above = lax.ppermute(down, 'py', ring(py, -1))]
    ppermute x10 -> x4, waiting for transfers between devices: 8.58 us -> 1.46 us  [the longest x1 0.9 us: per_device(): zabove = lax.ppermute(zdown, 'pz', ring(pz, -1))]
    all_to_all x0 -> x1, waiting for transfers between devices: none -> 7.04 us  [per_device(): total = lax.all_to_all(partial, ('quad', 'py', 'pz'), 0, 0)]
    all_to_all x0 -> x1, starting transfers between devices: none -> 6.01 us  [per_device(): total = lax.all_to_all(partial, ('quad', 'py', 'pz'), 0, 0)]
    pallas_call x6 -> x5, Pallas kernels: 8.91 us -> 8.44 us  [the longest x1 2.58 us: per_device(): pl.pallas_call(functools.partial(sums_kernel, owned), out_shape=shaped(de...]
  transfers between devices with their start and end apart: 10 -> 5, of which waited for: 7 -> 3; matrix products, arithmetic and copies ran while one was open for 0% -> 0% of each run, Pallas kernels for 9% -> 4%
where the time goes in v4:
time: 30.9 us; the launch traced here: 30.7 us
  starting transfers between devices  12.3 us (40%)
  waiting for transfers between devices  8.5 us (28%)
  Pallas kernels  8.44 us (27%)
  between operations  1.36 us (4%)
    all_to_all x1, waiting for transfers between devices, per_device(): total = lax.all_to_all(partial, ('quad', 'py', 'pz'), 0, 0)  7.04 us
    all_to_all x1, starting transfers between devices, per_device(): total = lax.all_to_all(partial, ('quad', 'py', 'pz'), 0, 0)  6.01 us
    pallas_call x1, Pallas kernels, per_device(): pl.pallas_call(functools.partial(sums_kernel, owned), out_shape=shaped(de...  2.58 us
    ppermute x1, starting transfers between devices, per_device(): above = lax.ppermute(down, 'py', ring(py, -1))  2.49 us
    ppermute x1, starting transfers between devices, per_device(): zabove = lax.ppermute(zdown, 'pz', ring(pz, -1))  2.25 us
    pallas_call x1, Pallas kernels, per_device(): pl.pallas_call(functools.partial(load_kernel, owned), out_shape=(shaped(f...  2.12 us
    pallas_call x1, Pallas kernels, per_device(): pl.pallas_call(output_kernel, out_shape=shaped(MOMS, 2, srcs, owned, ny,...  1.7 us
    ppermute x1, starting transfers between devices, per_device(): zbelow = lax.ppermute(zup, 'pz', ring(pz, 1))  1.58 us
  transfers between devices with their start and end apart: 5, of which 3 were waited for; matrix products, arithmetic and copies ran while one was open for 0% of the time, Pallas kernels for 4%

profile of v4, /device:TPU:0, one launch (start us, length us, event | category | flops | bytes accessed | tf_op | source)
XLA Modules:
  0.0 30.7 jit_solution(5448237552166231247)
XLA Ops:
  0.0 2.1 %load.1 = (f32[8,16,16,128]{3,2,1,0:T(8,128)S(1)}, f32[16,16,128]{2,1,0:T(8,128)S(1)}, f32[384,128]{1,0:T(8,128)S(1)}, f32[800,128]{1,0:T(8,128)S(1)}, f32[72,256]{1,0:T(8,128)S(1)}, /*index=5*/f32[72,256]{1,0:T(8,128)S(1)}) custom-call(f32[4,16,16,128]{3,2,1,0:T(8,128)} %re_hbm.1, f32[4,16,16,128]{3,2,1,0:T(8,128)} %im_hbm.1, f32[16,16,128]{2,1,0:T(8,128)} %pot_hbm.1), custom_call_target="tpu_custom_call" | custom-call | tf_op jit(solution)/shard_map/load/pallas_call | solution.py:511
  2.1 2.5 %collective-permute-start.1 = (f32[800,128]{1,0:T(8,128)S(1)}, f32[800,128]{1,0:T(8,128)S(1)}, u32[]{:S(2)}, u32[]{:S(2)}) collective-permute-start(f32[800,128]{1,0:T(8,128)S(1)} %get-tuple-element.16), channel_id=1, source_target_pairs={{0,12},{4,0},{8,4},{12,8},{1,13},{5,1},{9,5},{13,9},{2,14},{6,2},{... | collective-permute-start | bytes 1228808 | tf_op jit(solution)/shard_map/ppermute | solution.py:530
  4.6 0.0 collective-permute-start
  4.6 1.6 %collective-permute-start.2 = (f32[72,256]{1,0:T(8,128)S(1)}, f32[72,256]{1,0:T(8,128)S(1)}, u32[]{:S(2)}, u32[]{:S(2)}) collective-permute-start(f32[72,256]{1,0:T(8,128)S(1)} %get-tuple-element.17.zup_ref), channel_id=1, source_target_pairs={{0,1},{1,2},{2,3},{3,0},{4,5},{5,6},{6,7},{7,4},{8,9},{9,10},{10,1... | collective-permute-start | bytes 221192 | tf_op jit(solution)/shard_map/ppermute | solution.py:533
  6.2 2.2 %collective-permute-start.3 = (f32[72,256]{1,0:T(8,128)S(1)}, f32[72,256]{1,0:T(8,128)S(1)}, u32[]{:S(2)}, u32[]{:S(2)}) collective-permute-start(f32[72,256]{1,0:T(8,128)S(1)} %get-tuple-element.18.zdown_ref), channel_id=1, source_target_pairs={{0,3},{1,0},{2,1},{3,2},{4,7},{5,4},{6,5},{7,6},{8,11},{9,8},{10,9... | collective-permute-start | bytes 221192 | tf_op jit(solution)/shard_map/ppermute | solution.py:532
  9.7 1.2 %inner.1.inner_ref = f32[8,12,16,128]{3,2,1,0:T(8,128)S(1)} custom-call(f32[8,16,16,128]{3,2,1,0:T(8,128)S(1)} %get-tuple-element.13.b_ref, f32[16,16,128]{2,1,0:T(8,128)S(1)} %get-tuple-element.14.pot_ref), custom_call_target="tpu_custom_call" | custom-call | flops 11796480 | bytes 2359296 | tf_op jit(solution)/shard_map/inner/pallas_call | solution.py:535
  10.9 0.0 copy-start
  11.0 0.6 %collective-permute-done.2.zbelow_ref = f32[72,256]{1,0:T(8,128)S(1)} collective-permute-done((f32[72,256]{1,0:T(8,128)S(1)}, f32[72,256]{1,0:T(8,128)S(1)}, u32[]{:S(2)}, u32[]{:S(2)}) %collective-permute-start.2) | collective-permute-done | bytes 73760 | tf_op jit(solution)/shard_map/ppermute | solution.py:533
  11.5 0.9 %collective-permute-done.3.zabove_ref = f32[72,256]{1,0:T(8,128)S(1)} collective-permute-done((f32[72,256]{1,0:T(8,128)S(1)}, f32[72,256]{1,0:T(8,128)S(1)}, u32[]{:S(2)}, u32[]{:S(2)}) %collective-permute-start.3) | collective-permute-done | bytes 73760 | tf_op jit(solution)/shard_map/ppermute | solution.py:532
  12.4 0.0 collective-permute-done.below_ref
  12.4 0.0 collective-permute-done.1.above_ref
  12.4 0.9 %border.1 = (f32[8,12,16,128]{3,2,1,0:T(8,128)S(1)}, f32[64,256]{1,0:T(8,128)S(1)}) custom-call(f32[8,12,16,128]{3,2,1,0:T(8,128)S(1)} %inner.1.inner_ref, f32[384,128]{1,0:T(8,128)S(1)} %collective-permute-done.below_ref, f32[800,128]{1,0:T(8,128)S(1)} %collective-permute-done.1.above_ref, f32[72,256]{1,0:T(8,128)S(1)} %collective-permute-done.2.zbelow_ref, ...), custom_call_target="tpu_custom_call" | custom-call | tf_op jit(solution)/shard_map/border/pallas_call | solution.py:546
  13.3 2.6 %sums.1 = f32[32,128]{1,0:T(8,128)} custom-call(f32[8,16,16,128]{3,2,1,0:T(8,128)S(1)} %get-tuple-element.13.b_ref, f32[16,16,128]{2,1,0:T(8,128)S(1)} %get-tuple-element.14.pot_ref, f32[8,12,16,128]{3,2,1,0:T(8,128)S(1)} %get-tuple-element.19.h_ref, f32[64,256]{1,0:T(8,128)S(1)} %get-tuple-element.20.u_ref, ...), custom_call_target="tpu_custom_call" | custom-call | tf_op jit(solution)/shard_map/sums/pallas_call | solution.py:560
  15.9 6.0 %all-to-all-start = ((f32[32,1,128]{2,1,0:T(1,128)}), f32[32,1,128]{2,1,0:T(1,128)S(1)}, u32[]{:S(2)}, u32[]{:S(2)}) async-start(f32[32,1,128]{2,1,0:T(1,128)} %bitcast.1), calls=%async_computation | async-start | bytes 32768 | tf_op jit(solution)/shard_map/all_to_all | solution.py:574
  21.9 0.0 copy-done
  21.9 0.1 multiply_add_fusion.table_ref
  22.0 7.0 %all-to-all-done = f32[32,1,128]{2,1,0:T(1,128)S(1)} async-done(((f32[32,1,128]{2,1,0:T(1,128)}), f32[32,1,128]{2,1,0:T(1,128)S(1)}, u32[]{:S(2)}, u32[]{:S(2)}) %all-to-all-start) | async-done | bytes 16416 | tf_op jit(solution)/shard_map/all_to_all | solution.py:574
  29.0 1.7 %output.1 = f32[4,2,4,8,16,128]{5,4,3,2,1,0:T(8,128)} custom-call(f32[32,128]{1,0:T(8,128)S(1)} %bitcast.7, f32[16,128]{1,0:T(8,128)S(1)} %multiply_add_fusion.table_ref, f32[8,16,16,128]{3,2,1,0:T(8,128)S(1)} %get-tuple-element.13.b_ref, f32[8,12,16,128]{3,2,1,0:T(8,128)S(1)} %get-tuple-element.19.h_ref), custom_call_target="tpu_custom_call" | custom-call | tf_op jit(solution)/shard_map/output/pallas_call | solution.py:579
  (1 shorter events, 0.0 us)
Async XLA Ops:
  2.1 10.3 %collective-permute-start.1 = (f32[800,128]{1,0:T(8,128)S(1)}, f32[800,128]{1,0:T(8,128)S(1)}, u32[]{:S(2)}, u32[]{:S(2)}) collective-permute-start(f32[800,128]{1,0:T(8,128)S(1)} %get-tuple-element.16), channel_id=1, source_target_pairs={{0,12},{4,0},{8,4},{12,8},{1,13},{5,1},{9,5},{13,9},{2,14},{6,2},{... | collective-permute-start | bytes 1228808 | tf_op jit(solution)/shard_map/ppermute | solution.py:530
  4.6 7.8 %collective-permute-start = (f32[384,128]{1,0:T(8,128)S(1)}, f32[384,128]{1,0:T(8,128)S(1)}, u32[]{:S(2)}, u32[]{:S(2)}) collective-permute-start(f32[384,128]{1,0:T(8,128)S(1)} %get-tuple-element.15), channel_id=1, source_target_pairs={{0,4},{4,8},{8,12},{12,0},{1,5},{5,9},{9,13},{13,1},{2,6},{6,10},{... | collective-permute-start | bytes 589832 | tf_op jit(solution)/shard_map/ppermute | solution.py:531
  4.6 6.9 %collective-permute-start.2 = (f32[72,256]{1,0:T(8,128)S(1)}, f32[72,256]{1,0:T(8,128)S(1)}, u32[]{:S(2)}, u32[]{:S(2)}) collective-permute-start(f32[72,256]{1,0:T(8,128)S(1)} %get-tuple-element.17.zup_ref), channel_id=1, source_target_pairs={{0,1},{1,2},{2,3},{3,0},{4,5},{5,6},{6,7},{7,4},{8,9},{9,10},{10,1... | collective-permute-start | bytes 221192 | tf_op jit(solution)/shard_map/ppermute | solution.py:533
  6.2 6.2 %collective-permute-start.3 = (f32[72,256]{1,0:T(8,128)S(1)}, f32[72,256]{1,0:T(8,128)S(1)}, u32[]{:S(2)}, u32[]{:S(2)}) collective-permute-start(f32[72,256]{1,0:T(8,128)S(1)} %get-tuple-element.18.zdown_ref), channel_id=1, source_target_pairs={{0,3},{1,0},{2,1},{3,2},{4,7},{5,4},{6,5},{7,6},{8,11},{9,8},{10,9... | collective-permute-start | bytes 221192 | tf_op jit(solution)/shard_map/ppermute | solution.py:532
  10.9 10.9 %copy-start = (f32[16,128]{1,0:T(8,128)S(1)}, f32[16,128]{1,0:T(8,128)}, u32[]{:S(2)}) copy-start(f32[16,128]{1,0:T(8,128)} %constant.9.clone) | copy-start | bytes 24580
  15.9 13.1 %all-to-all-start = ((f32[32,1,128]{2,1,0:T(1,128)}), f32[32,1,128]{2,1,0:T(1,128)S(1)}, u32[]{:S(2)}, u32[]{:S(2)}) async-start(f32[32,1,128]{2,1,0:T(1,128)} %bitcast.1), calls=%async_computation | async-start | bytes 32768 | tf_op jit(solution)/shard_map/all_to_all | solution.py:574

commit v5 on v4

v5 whole, which is shorter than its diff:
```python
import functools
import math

import jax
import jax.numpy as jnp
import numpy as np
from jax import lax
from jax.experimental import pallas as pl
from jax.experimental.pallas import tpu as pltpu
from jax.sharding import PartitionSpec as P

QPTS = 8
MOMS = 4
REACH = 4
LANES = 128

stencil_weights = (-205.0 / 72.0, 8.0 / 5.0, -1.0 / 5.0, 8.0 / 315.0, -1.0 / 560.0)
DIAG = -1.5 * stencil_weights[0]
MIDDLE = 5.25
SIDE = tuple(-0.5 * w for w in stencil_weights)
HIGHEST = lax.Precision.HIGHEST


def dot(left, right, dims):
    return lax.dot_general(
        left, right, (dims, ((), ())), precision=HIGHEST, preferred_element_type=jnp.float32
    )


def band(shape, offset, signs, scale=1.0):
    step = offset + lax.broadcasted_iota(jnp.int32, shape, 0) - lax.broadcasted_iota(jnp.int32, shape, 1)
    out = jnp.zeros(shape, jnp.float32)
    for k in range(1, REACH + 1):
        for sign in signs:
            out = jnp.where(step == sign * k, scale * SIDE[k], out)
    return out


def split(value):
    high = value.astype(jnp.bfloat16)
    return high, (value - high.astype(jnp.float32)).astype(jnp.bfloat16)


def wide_left(value):
    high, low = split(value)
    return jnp.concatenate([high, low, high], axis=1)


def wide_right(value):
    high, low = split(value)
    return jnp.concatenate([high, high, low], axis=0)


def mul(left, right):
    return lax.dot_general(left, right, (((1,), (0,)), ((), ())), preferred_element_type=jnp.float32)


def gather_edges(gathered, f, value):
    lane = lax.broadcasted_iota(jnp.int32, value.shape, 1)
    moved = pltpu.roll(value, 4 * REACH * f + 2 * REACH, 1)
    return jnp.where(lane // (4 * REACH) == f, moved, gathered)


def load_kernel(
    owned, re_hbm, im_hbm, pot_hbm, b_ref, pot_ref, up_ref, down_ref, zup_ref, zdown_ref, edge_ref, sems
):
    fields, cx, ny, nz = b_ref.shape
    srcs = fields // 2
    parts = cx // owned
    reach = up_ref.shape[0] // (fields * REACH)
    first = lax.axis_index("quad")
    copies = []
    for f in range(fields + 1):
        source = pot_hbm if f == fields else (re_hbm, im_hbm)[f // srcs].at[f % srcs]
        target = pot_ref if f == fields else b_ref.at[f]
        group = []
        for j in range(parts):
            at = pl.multiple_of(lax.rem(first + j, parts) * owned, owned)
            group.append(
                pltpu.make_async_copy(
                    source.at[pl.ds(at, owned)], target.at[pl.ds(j * owned, owned)], sems.at[f, j]
                )
            )
        copies.append(group)
    for group in copies:
        for copy in group:
            copy.start()
    edge_ref[...] = jnp.zeros(edge_ref.shape, jnp.float32)
    far = fields * reach
    for f in range(fields):
        for copy in copies[f]:
            copy.wait()
        for x in range(reach):
            at = (f * reach + x) * REACH
            up_ref[at : at + REACH, :] = b_ref[f, x, ny - REACH : ny, :]
            down_ref[at : at + REACH, :] = b_ref[f, x, 0:REACH, :]
        for x in range(owned):
            at = (far + f * owned + x) * REACH
            down_ref[at : at + REACH, :] = b_ref[f, x, REACH : 2 * REACH, :]
        edge_ref[...] = gather_edges(edge_ref[...], f, b_ref[f].reshape(cx * ny, nz))
    for copy in copies[fields]:
        copy.wait()
    pot_ref[...] = pot_ref[...] + (DIAG - MIDDLE)
    for x in range(owned):
        at = (far + fields * owned + x) * REACH
        down_ref[at : at + REACH, :] = pot_ref[x, 0:REACH, :]
    turned = pltpu.roll(pot_ref[...].reshape(cx * ny, nz), 2 * REACH, 1).T
    rows = fields * REACH
    after = rows + rows // 2
    zup_ref[after : after + REACH, :] = turned[REACH : 2 * REACH]
    zup_ref[after + REACH : after + 2 * REACH, :] = turned[0:REACH]
    zdown_ref[after : after + 2 * REACH, :] = turned[2 * REACH : 4 * REACH]
    turned = edge_ref[...].T
    for f in range(fields):
        at = 4 * REACH * f
        low, high = f * REACH, (f + 1) * REACH
        zup_ref[low:high, :] = turned[at + REACH : at + 2 * REACH]
        zdown_ref[low:high, :] = turned[at + 2 * REACH : at + 3 * REACH]
        side, spot = f // srcs * LANES, rows + f % srcs * REACH
        lanes = slice(side, side + LANES)
        zup_ref[spot : spot + REACH, lanes] = turned[at : at + REACH, 0:LANES]
        zdown_ref[spot : spot + REACH, lanes] = turned[at + 3 * REACH : at + 4 * REACH, 0:LANES]


def phase_table():
    lane = np.arange(LANES)
    angle = 2.0 * math.pi * (lane % QPTS + 0.5) / QPTS
    rows = [np.cos(angle), np.sin(angle)]
    for k in range(1, MOMS + 1):
        rows.append(np.where(lane < QPTS, np.cos(k * angle), 0.0) / QPTS)
        rows.append(np.where(lane < QPTS, np.sin(k * angle), 0.0) / QPTS)
    rows += [np.zeros(LANES)] * (-len(rows) % 8)
    return np.stack(rows).astype(np.float32)


def links(row_at, col_at, row_field, col_field):
    step = jnp.abs(row_at - col_at)
    out = jnp.zeros(step.shape, jnp.float32)
    for k in range(1, REACH + 1):
        out = jnp.where((step == k) & (row_field == col_field), SIDE[k], out)
    return out


def layer_of(index, starts, rows):
    layer = jnp.full(index.shape, 1 << 20, jnp.int32)
    for n, start in enumerate(starts):
        layer = jnp.where(index // rows == n, start + index % REACH, layer)
    return layer, index % rows // REACH


def around(value, ny):
    y = lax.broadcasted_iota(jnp.int32, value.shape, 1) % ny
    width = value.shape[1]
    out = jnp.zeros(value.shape, jnp.float32)
    for k in range(1, REACH + 1):
        sides = jnp.where(y >= ny - k, pltpu.roll(value, ny - k, 1), 0.0)
        sides = sides + jnp.where(y < k, pltpu.roll(value, width + k - ny, 1), 0.0)
        out = out + SIDE[k] * sides
    return out


def inner_kernel(
    owned,
    b_ref,
    pot_ref,
    zup_ref,
    zdown_ref,
    out_ref,
    both_ref,
    half_ref,
    beyond_ref,
    back_ref,
    fix_ref,
    edges_ref,
    pad_ref,
):
    fields, cx, ny, nz = b_ref.shape
    reach = out_ref.shape[1]
    rows = fields * REACH
    both_ref[...] = wide_right(band((nz, nz), 0, (1, -1)))
    half_ref[...] = wide_right(band((nz, nz), 0, (1,), 2.0))
    for f in range(fields):
        own = b_ref[f, 0:reach].reshape(reach * ny, nz)
        out_ref[f] = mul(wide_left(own), both_ref[...]).reshape(reach, ny, nz)
    zero = jnp.zeros((reach, 8, nz), jnp.float32)
    pad_ref[:, 0:8, :] = zero
    pad_ref[:, 8 + ny : 16 + ny, :] = zero

    def field(f, _):
        pad_ref[:, 8 : 8 + ny, :] = b_ref[f, 0:reach]
        for x in range(reach):
            total = out_ref[f, x] + pot_ref[x] * b_ref[f, x]
            for k in range(1, REACH + 1):
                sides = b_ref[f, (x + k) % cx] + b_ref[f, (x - k) % cx]
                sides = sides + pad_ref[x, 8 + k : 8 + k + ny, :]
                sides = sides + pad_ref[x, 8 - k : 8 - k + ny, :]
                total = total + SIDE[k] * sides
            out_ref[f, x] = total
        return 0

    lax.fori_loop(0, fields, field, 0)

    shape = (2 * rows, 8 * rows)
    row_at, row_field = layer_of(lax.broadcasted_iota(jnp.int32, shape, 0), (-REACH, nz), rows)
    starts = (0, nz - REACH, -REACH, -2 * REACH, nz, nz + REACH)
    col_at, col_field = layer_of(lax.broadcasted_iota(jnp.int32, shape, 1), starts, rows)
    beyond_ref[...] = wide_left(links(row_at, col_at, row_field, col_field))
    shape = (4 * rows, 4 * rows)
    row = lax.broadcasted_iota(jnp.int32, shape, 0)
    col = lax.broadcasted_iota(jnp.int32, shape, 1)
    row_at, row_field = layer_of(row % (2 * rows), (0, nz - REACH), rows)
    col_at, col_field = layer_of(col % (2 * rows), (-REACH, nz), rows)
    same = row // (2 * rows) == col // (2 * rows)
    back_ref[...] = wide_left(jnp.where(same, links(row_at, col_at, row_field, col_field), 0.0))
    shape = (2 * rows, nz)
    layer, owner = layer_of(lax.broadcasted_iota(jnp.int32, shape, 0), (-REACH, nz), rows)
    cell = lax.broadcasted_iota(jnp.int32, shape, 1)
    for f in range(fields):
        fix_ref[f] = wide_right(links(layer, cell, owner, f))
    lane = lax.broadcasted_iota(jnp.int32, (2 * rows, LANES), 1)
    weight = jnp.where(lane < owned * ny, jnp.where(lane % ny >= ny // 2, 3.0, 1.0), 0.0)
    edges = jnp.concatenate([zdown_ref[0:rows, 0:LANES], zup_ref[0:rows, 0:LANES]], axis=0)
    edges_ref[...] = around(edges, ny) * weight


def fold(value):
    return jnp.sum(value, axis=0, keepdims=True)


def product(left, right):
    return left[0] * right[0] - left[1] * right[1], left[0] * right[1] + left[1] * right[0]


def main_kernel(
    owned,
    b_ref,
    pot_ref,
    inner_ref,
    below_ref,
    above_ref,
    zup_ref,
    zdown_ref,
    zbelow_ref,
    zabove_ref,
    both_ref,
    half_ref,
    beyond_ref,
    back_ref,
    fix_ref,
    edges_ref,
    h_ref,
    out_ref,
    pad_ref,
    edge_ref,
    acc_ref,
    step_ref,
    far_ref,
    pull_ref,
):
    fields, reach, ny, nz = inner_ref.shape
    cx = b_ref.shape[1]
    srcs = fields // 2
    rows = fields * REACH
    after = rows + rows // 2

    outer = jnp.concatenate([zbelow_ref[0:rows], zabove_ref[0:rows]], axis=0)
    wide = wide_left(outer.T[0 : reach * ny])
    near = outer[:, 0:LANES]

    def second(ref):
        return [ref[rows:after, 0:LANES], ref[rows:after, LANES : 2 * LANES]]

    stack = jnp.concatenate(
        [zdown_ref[0:rows, 0:LANES], zup_ref[0:rows, 0:LANES], near[0:rows]]
        + second(zbelow_ref)
        + [near[rows : 2 * rows]]
        + second(zabove_ref)
        + [near],
        axis=0,
    )
    image = mul(beyond_ref[...], wide_right(stack))
    local = jnp.concatenate(
        [zbelow_ref[after : after + REACH, 0:LANES]] * fields
        + [zabove_ref[after : after + REACH, 0:LANES]] * fields,
        axis=0,
    )
    image = image + local * near
    y = lax.broadcasted_iota(jnp.int32, (2 * rows, LANES), 1) % ny
    width = cx * ny
    for k in range(1, REACH + 1):
        sides = pltpu.roll(outer, ny * k, 1) + pltpu.roll(outer, width - ny * k, 1)
        sides = sides[:, 0:LANES] + jnp.where(y >= k, pltpu.roll(near, k, 1), 0.0)
        sides = sides + jnp.where(y < ny - k, pltpu.roll(near, LANES - k, 1), 0.0)
        image = image + SIDE[k] * sides
    reached = mul(back_ref[...], wide_right(jnp.concatenate([image, near], axis=0)))
    turned = around(reached[2 * rows : 4 * rows], ny)

    for f in range(fields):
        h_ref[f] = mul(wide, fix_ref[f]).reshape(reach, ny, nz)
    zero = jnp.zeros((reach, 16, nz), jnp.float32)
    pad_ref[0] = zero
    pad_ref[1] = zero
    edge_ref[...] = jnp.zeros(edge_ref.shape, jnp.float32)
    for f in range(fields):
        for x in range(reach):
            at = (f * reach + x) * REACH
            pad_ref[0, x, 8 - REACH : 8, :] = below_ref[at : at + REACH, :]
            pad_ref[1, x, 8 : 8 + REACH, :] = above_ref[at : at + REACH, :]
        for x in range(reach):
            low = SIDE[1] * pad_ref[0, x, 7:15, :]
            high = SIDE[1] * pad_ref[1, x, 1:9, :]
            for k in range(2, REACH + 1):
                low = low + SIDE[k] * pad_ref[0, x, 8 - k : 16 - k, :]
                high = high + SIDE[k] * pad_ref[1, x, k : 8 + k, :]
            total = h_ref[f, x] + inner_ref[f, x]
            middle = [total[8 : ny - 8]] if ny > 16 else []
            first, last = total[0:8] + low, total[ny - 8 : ny] + high
            h_ref[f, x] = jnp.concatenate([first] + middle + [last], axis=0)
            if x < owned:
                u = jnp.concatenate([first + low] + middle + [last + 3.0 * high], axis=0)
                spot = pl.ds(x * ny, ny)
                edge_ref[spot, :] = gather_edges(edge_ref[spot, :], f, u)

    for f in range(fields):
        own = h_ref[f, 0:owned].reshape(owned * ny, nz)
        step_ref[f] = mul(wide_left(own), half_ref[...]).reshape(owned, ny, nz)
        at = f * reach * REACH
        far_ref[f] = mul(wide_left(above_ref[at : at + owned * REACH, :]), both_ref[...])

    quad_row = lax.broadcasted_iota(jnp.int32, (8, nz), 0) % REACH
    early = lax.broadcasted_iota(jnp.int32, (8, nz), 0) < REACH

    def top(ref, f, x):
        return jnp.where(early, pltpu.roll(ref[f, x, ny - 8 : ny, :], REACH, 0), ref[f, x + 1, ny - 8 : ny, :])

    def lowered(lower, upper, k):
        if k == REACH:
            return lower
        return jnp.where(quad_row >= k, pltpu.roll(upper, k, 0), pltpu.roll(lower, REACH + k, 0))

    def raised(lower, upper, k):
        if k == REACH:
            return upper
        return jnp.where(quad_row < REACH - k, pltpu.roll(lower, 8 - k, 0), pltpu.roll(upper, REACH - k, 0))

    for f in range(fields):
        for x in range(0, reach, 2):
            own = top(h_ref, f, x)
            pull = SIDE[REACH] * own
            for k in range(1, REACH):
                pull = pull + SIDE[k] * jnp.where(quad_row < k, pltpu.roll(own, REACH + k, 0), 0.0)
            at = (f * reach + x) * REACH
            pull_ref[at : at + 8, :] = pull

    row = lax.broadcasted_iota(jnp.int32, (ny, nz), 0)
    inside = [row < ny - k for k in range(REACH + 1)]
    for s in range(srcs):
        total = [jnp.zeros((ny, nz), jnp.float32) for _ in range(8)]
        for x in range(owned):
            local = pot_ref[x]
            b = (b_ref[s, x], b_ref[srcs + s, x])
            h, g = [], []
            for part in range(2):
                f = part * srcs + s
                own = h_ref[f, x]
                value = step_ref[f, x] + local * own
                for k in range(1, REACH + 1):
                    up = jnp.where(inside[k], pltpu.roll(own, ny - k, 0), 0.0)
                    value = value + (2.0 * SIDE[k]) * (h_ref[f, (x + k) % cx] + up)
                h.append(own)
                g.append(value)
            terms = product(b, b) + product(b, h) + product(h, h) + product(h, g)
            total = [t + v for t, v in zip(total, terms)]
        cross = [jnp.zeros((8, nz), jnp.float32) for _ in range(2)]
        for x in range(0, owned, 2):
            at = (fields * (reach + owned) + x) * REACH
            local = above_ref[at : at + 8, :]
            left, right, first, pulls = [], [], [], []
            for part in range(2):
                f = part * srcs + s
                at = (f * reach + x) * REACH
                own = top(b_ref, f, x)
                first_layers = above_ref[at : at + 8, :]
                start = (fields * reach + f * owned + x) * REACH
                more = above_ref[start : start + 8, :]
                value = far_ref[f, x * REACH : x * REACH + 8, :] + local * first_layers
                pull = 0.0
                for k in range(1, REACH + 1):
                    sides = above_ref[at + k * REACH : at + k * REACH + 8, :]
                    sides = sides + raised(first_layers, more, k) + lowered(own, first_layers, k)
                    value = value + SIDE[k] * sides
                    pull = pull + SIDE[k] * pull_ref[at + k * REACH : at + k * REACH + 8, :]
                left.append(pull_ref[at : at + 8, :])
                right.append(value)
                first.append(first_layers)
                pulls.append(pull)
            for c, (one, two) in enumerate(zip(product(left, right), product(first, pulls))):
                cross[c] = cross[c] + (one + two)
        for i in range(8):
            value = fold(total[i])
            if i >= 6:
                value = value + 2.0 * fold(cross[i - 6])
            acc_ref[i * srcs + s : i * srcs + s + 1, :] = value

    gathered = edge_ref[...].T
    part = rows // 2
    both = [0.0, 0.0]
    for side in range(2):
        at = (1 - side) * REACH + REACH
        u = jnp.concatenate(
            [gathered[4 * REACH * f + at : 4 * REACH * f + at + REACH] for f in range(fields)], axis=0
        )
        base = side * rows
        for left, right in ((u, reached), (edges_ref[base : base + rows], turned)):
            terms = product(
                (left[0:part], left[part:rows]), (right[base : base + part], right[base + part : base + rows])
            )
            both = [t + v for t, v in zip(both, terms)]
    for c in range(2):
        for s in range(srcs):
            at = (6 + c) * srcs + s
            acc_ref[at : at + 1, :] = acc_ref[at : at + 1, :] + fold(both[c][s * REACH : (s + 1) * REACH])

    column = jnp.sum(acc_ref[...], axis=1, keepdims=True)
    row = lax.broadcasted_iota(jnp.int32, acc_ref.shape, 0)
    lane = lax.broadcasted_iota(jnp.int32, acc_ref.shape, 1)
    out_ref[...] = jnp.broadcast_to(fold(jnp.where(row == lane, column, 0.0)), out_ref.shape)


def complex_mul(left, right):
    return (left[0] * right[0] - left[1] * right[1], left[0] * right[1] + left[1] * right[0])


def complex_div(left, right):
    norm_sq = right[0] * right[0] + right[1] * right[1]
    return (
        (left[0] * right[0] + left[1] * right[1]) / norm_sq,
        (left[1] * right[0] - left[0] * right[1]) / norm_sq,
    )


def output_kernel(tot_ref, table_ref, b_ref, h_ref, out_hbm, coef_ref, buf_ref, sems):
    fields, cx, ny, nz = b_ref.shape
    srcs = fields // 2
    planes = buf_ref.shape[3]
    shape = (srcs, LANES)
    wide = jnp.broadcast_to(fold(tot_ref[...]), (8 * srcs, LANES))
    row = lax.broadcasted_iota(jnp.int32, wide.shape, 0)
    lane = lax.broadcasted_iota(jnp.int32, wide.shape, 1)
    wide = jnp.broadcast_to(jnp.sum(jnp.where(row == lane, wide, 0.0), axis=1, keepdims=True), wide.shape)
    nu = [
        (wide[2 * k * srcs : (2 * k + 1) * srcs], wide[(2 * k + 1) * srcs : (2 * k + 2) * srcs])
        for k in range(4)
    ]
    zeta = (
        jnp.broadcast_to(table_ref[0:1, :], shape),
        jnp.broadcast_to(table_ref[1:2, :], shape),
    )
    scaled = complex_mul(zeta, nu[0])
    alpha_first = complex_div(nu[0], (scaled[0] - nu[1][0], scaled[1] - nu[1][1]))
    mean = complex_div(nu[1], nu[0])
    t = complex_mul(mean, nu[1])
    spread2 = (nu[2][0] - t[0], nu[2][1] - t[1])
    t = complex_mul(mean, (nu[2][0] + spread2[0], nu[2][1] + spread2[1]))
    spread3 = (nu[3][0] - t[0], nu[3][1] - t[1])
    square = complex_mul(alpha_first, alpha_first)
    rho_next = complex_mul(square, spread2)
    beta = complex_div(rho_next, nu[0])
    first_part = complex_mul(zeta, rho_next)
    second = complex_mul(square, spread3)
    third = complex_div(complex_mul(beta, rho_next), alpha_first)
    alpha_next = complex_div(
        rho_next, (first_part[0] - second[0] - third[0], first_part[1] - second[1] - third[1])
    )
    t = complex_mul(alpha_first, mean)
    carried = complex_mul(alpha_next, (beta[0] - t[0], beta[1] - t[1]))
    on_source = (alpha_first[0] + carried[0], alpha_first[1] + carried[1])
    on_image = complex_mul(alpha_next, alpha_first)
    for k in range(MOMS):
        weight = (
            jnp.broadcast_to(table_ref[2 + 2 * k : 3 + 2 * k, :], shape),
            jnp.broadcast_to(table_ref[3 + 2 * k : 4 + 2 * k, :], shape),
        )
        for n, value in enumerate((on_source, on_image)):
            both = complex_mul(weight, value)
            for c in range(2):
                column = jnp.sum(both[c], axis=1, keepdims=True)
                coef_ref[4 * k + 2 * n + c, 0:srcs, :] = jnp.broadcast_to(column, shape)

    copies = []
    for s in range(srcs):
        for k in range(MOMS):
            c = [
                jnp.broadcast_to(coef_ref[4 * k + n, s : s + 1, :], (ny, nz)) for n in range(4)
            ]
            for x in range(planes):
                br, bi = b_ref[s, x], b_ref[srcs + s, x]
                hr, hi = h_ref[s, x], h_ref[srcs + s, x]
                buf_ref[s, k, 0, x] = c[0] * br - c[1] * bi + (c[2] * hr - c[3] * hi)
                buf_ref[s, k, 1, x] = c[0] * bi + c[1] * br + (c[2] * hi + c[3] * hr)
        copy = pltpu.make_async_copy(buf_ref.at[s], out_hbm.at[:, :, s], sems.at[s])
        copy.start()
        copies.append(copy)
    for copy in copies:
        copy.wait()


def ring(count, step):
    return [(i, (i + step) % count) for i in range(count)]


ANY = pl.BlockSpec(memory_space=pl.ANY)
HBM = pl.BlockSpec(memory_space=pltpu.HBM)
VMEM = pl.BlockSpec(memory_space=pltpu.VMEM)
SMEM = pl.BlockSpec(memory_space=pltpu.SMEM)


def shaped(*dims):
    return jax.ShapeDtypeStruct(dims, jnp.float32)


def small(mib):
    return pltpu.CompilerParams(vmem_limit_bytes=mib << 20)


def cost(flops, nbytes):
    return pl.CostEstimate(flops=flops, bytes_accessed=nbytes, transcendentals=0)


def per_device(source_real, source_imag, potential, center, radius):
    srcs, cx, ny, nz = source_real.shape
    fields = 2 * srcs
    py, pz, quads = lax.axis_size("py"), lax.axis_size("pz"), lax.axis_size("quad")
    owned = cx // quads
    reach = min(cx, owned + REACH)
    cells = reach * ny * nz
    rows = fields * REACH

    source_real, source_imag, potential = (
        pltpu.with_memory_space_constraint(a, pltpu.HBM)
        for a in (source_real, source_imag, potential)
    )
    part = shaped(fields, reach, ny, nz)
    flat = shaped(rows + rows // 2 + 2 * REACH, cx * ny)
    b, pot, up, down, zup, zdown = pl.pallas_call(
        functools.partial(load_kernel, owned),
        out_shape=(
            shaped(fields, cx, ny, nz),
            shaped(cx, ny, nz),
            shaped(fields * reach * REACH, nz),
            shaped((fields * (reach + owned) + owned) * REACH, nz),
            flat,
            flat,
        ),
        in_specs=[HBM] * 3,
        out_specs=(VMEM,) * 6,
        scratch_shapes=[
            pltpu.VMEM((cx * ny, nz), jnp.float32),
            pltpu.SemaphoreType.DMA((fields + 1, quads)),
        ],
        compiler_params=small(8),
        name="load",
    )(source_real, source_imag, potential)
    above = lax.ppermute(down, "py", ring(py, -1))
    below = lax.ppermute(up, "py", ring(py, 1))
    zabove = lax.ppermute(zdown, "pz", ring(pz, -1))
    zbelow = lax.ppermute(zup, "pz", ring(pz, 1))

    half = lambda *dims: jax.ShapeDtypeStruct(dims, jnp.bfloat16)
    inner, *weights = pl.pallas_call(
        functools.partial(inner_kernel, owned),
        out_shape=(
            part,
            half(3 * nz, nz),
            half(3 * nz, nz),
            half(2 * rows, 24 * rows),
            half(4 * rows, 12 * rows),
            half(fields, 6 * rows, nz),
            shaped(2 * rows, LANES),
        ),
        in_specs=[VMEM] * 4,
        out_specs=(VMEM,) * 7,
        scratch_shapes=[pltpu.VMEM((reach, ny + 16, nz), jnp.float32)],
        compiler_params=small(12),
        cost_estimate=cost(fields * cells * 60, fields * cells * 12),
        name="inner",
    )(b, pot, zup, zdown)

    devices = quads * py * pz
    image, partial = pl.pallas_call(
        functools.partial(main_kernel, owned),
        out_shape=(part, shaped(devices, LANES)),
        in_specs=[VMEM] * 15,
        out_specs=(VMEM,) * 2,
        scratch_shapes=[
            pltpu.VMEM((2, reach, 16, nz), jnp.float32),
            pltpu.VMEM((LANES, nz), jnp.float32),
            pltpu.VMEM((8 * srcs, nz), jnp.float32),
            pltpu.VMEM((fields, owned, ny, nz), jnp.float32),
            pltpu.VMEM((fields, owned * REACH, nz), jnp.float32),
            pltpu.VMEM((fields * reach * REACH, nz), jnp.float32),
        ],
        compiler_params=small(12),
        name="main",
    )(b, pot, inner, below, above, zup, zdown, zbelow, zabove, *weights)

    total = lax.all_to_all(partial, ("quad", "py", "pz"), 0, 0)

    table = jnp.asarray(phase_table())
    row = lax.broadcasted_iota(jnp.int32, table.shape, 0)
    table = radius * table + jnp.where(row == 0, center - MIDDLE, 0.0)
    return pl.pallas_call(
        output_kernel,
        out_shape=shaped(MOMS, 2, srcs, owned, ny, nz),
        in_specs=[VMEM] * 4,
        out_specs=HBM,
        scratch_shapes=[
            pltpu.VMEM((4 * MOMS, 8, LANES), jnp.float32),
            pltpu.VMEM((srcs, MOMS, 2, owned, ny, nz), jnp.float32),
            pltpu.SemaphoreType.DMA((srcs,)),
        ],
        compiler_params=small(12),
        name="output",
    )(total, table, b, image)


def solution(mesh):
    in_specs = (P(None, None, "py", "pz"), P(None, None, "py", "pz"), P(None, "py", "pz"), P(), P())
    out_specs = P(None, None, None, "quad", "py", "pz")
    return jax.shard_map(
        per_device, mesh=mesh, in_specs=in_specs, out_specs=out_specs, check_vma=False
    )
```

time: 30.9 us -> 29.7 us (0.961)
  waiting for transfers between devices: 8.5 us -> 7.57 us
    ppermute x1, waiting for transfers between devices: 0.55 us -> 0.01 us  [per_device(): zbelow = lax.ppermute(zup, 'pz', ring(pz, 1))]
    ppermute x1, waiting for transfers between devices: 0.9 us -> 0.41 us  [per_device(): zabove = lax.ppermute(zdown, 'pz', ring(pz, -1))]
    pallas_call x3 -> x2, Pallas kernels: 4.62 us -> 4.4 us  [the longest x1 2.9 us: per_device(): pl.pallas_call(functools.partial(main_kernel, owned), out_shape=(part, sh...]
  transfers between devices with their start and end apart: 5 -> 5, of which waited for: 3 -> 3; matrix products, arithmetic and copies ran while one was open for 0% -> 0% of each run, Pallas kernels for 4% -> 5%
where the time goes in v5:
time: 29.7 us; the launch traced here: 29.5 us
  starting transfers between devices  12.2 us (41%)
  Pallas kernels  8.27 us (28%)
  waiting for transfers between devices  7.57 us (25%)
  between operations  1.36 us (5%)
    all_to_all x1, waiting for transfers between devices, per_device(): total = lax.all_to_all(partial, ('quad', 'py', 'pz'), 0, 0)  7.04 us
    all_to_all x1, starting transfers between devices, per_device(): total = lax.all_to_all(partial, ('quad', 'py', 'pz'), 0, 0)  5.91 us
    pallas_call x1, Pallas kernels, per_device(): pl.pallas_call(functools.partial(main_kernel, owned), out_shape=(part, sh...  2.9 us
    ppermute x1, starting transfers between devices, per_device(): above = lax.ppermute(down, 'py', ring(py, -1))  2.49 us
    ppermute x1, starting transfers between devices, per_device(): zabove = lax.ppermute(zdown, 'pz', ring(pz, -1))  2.25 us
    pallas_call x1, Pallas kernels, per_device(): pl.pallas_call(functools.partial(load_kernel, owned), out_shape=(shaped(f...  2.17 us
    pallas_call x1, Pallas kernels, per_device(): pl.pallas_call(output_kernel, out_shape=shaped(MOMS, 2, srcs, owned, ny,...  1.7 us
    ppermute x1, starting transfers between devices, per_device(): zbelow = lax.ppermute(zup, 'pz', ring(pz, 1))  1.58 us
  transfers between devices with their start and end apart: 5, of which 3 were waited for; matrix products, arithmetic and copies ran while one was open for 0% of the time, Pallas kernels for 5%

profile of v5, /device:TPU:0, one launch (start us, length us, event | category | flops | bytes accessed | tf_op | source)
XLA Modules:
  0.0 29.5 jit_solution(8172531384152072685)
XLA Ops:
  0.0 2.2 %load.1 = (f32[8,16,16,128]{3,2,1,0:T(8,128)S(1)}, f32[16,16,128]{2,1,0:T(8,128)S(1)}, f32[384,128]{1,0:T(8,128)S(1)}, f32[672,128]{1,0:T(8,128)S(1)}, f32[56,256]{1,0:T(8,128)S(1)}, /*index=5*/f32[56,256]{1,0:T(8,128)S(1)}) custom-call(f32[4,16,16,128]{3,2,1,0:T(8,128)} %re_hbm.1, f32[4,16,16,128]{3,2,1,0:T(8,128)} %im_hbm.1, f32[16,16,128]{2,1,0:T(8,128)} %pot_hbm.1), custom_call_target="tpu_custom_call" | custom-call | tf_op jit(solution)/shard_map/load/pallas_call | solution.py:545
  2.2 2.5 %collective-permute-start.1 = (f32[672,128]{1,0:T(8,128)S(1)}, f32[672,128]{1,0:T(8,128)S(1)}, u32[]{:S(2)}, u32[]{:S(2)}) collective-permute-start(f32[672,128]{1,0:T(8,128)S(1)} %get-tuple-element.26), channel_id=1, source_target_pairs={{0,12},{4,0},{8,4},{12,8},{1,13},{5,1},{9,5},{13,9},{2,14},{6,2},{... | collective-permute-start | bytes 1032200 | tf_op jit(solution)/shard_map/ppermute | solution.py:564
  4.7 0.0 collective-permute-start
  4.7 1.6 %collective-permute-start.2 = (f32[56,256]{1,0:T(8,128)S(1)}, f32[56,256]{1,0:T(8,128)S(1)}, u32[]{:S(2)}, u32[]{:S(2)}) collective-permute-start(f32[56,256]{1,0:T(8,128)S(1)} %get-tuple-element.22.zup_ref), channel_id=1, source_target_pairs={{0,1},{1,2},{2,3},{3,0},{4,5},{5,6},{6,7},{7,4},{8,9},{9,10},{10,1... | collective-permute-start | bytes 172040 | tf_op jit(solution)/shard_map/ppermute | solution.py:567
  6.2 2.2 %collective-permute-start.3 = (f32[56,256]{1,0:T(8,128)S(1)}, f32[56,256]{1,0:T(8,128)S(1)}, u32[]{:S(2)}, u32[]{:S(2)}) collective-permute-start(f32[56,256]{1,0:T(8,128)S(1)} %get-tuple-element.23.zdown_ref), channel_id=1, source_target_pairs={{0,3},{1,0},{2,1},{3,2},{4,7},{5,4},{6,5},{7,6},{8,11},{9,8},{10,9... | collective-permute-start | bytes 172040 | tf_op jit(solution)/shard_map/ppermute | solution.py:566
  9.8 1.5 %inner.1 = (f32[8,12,16,128]{3,2,1,0:T(8,128)S(1)}, bf16[384,128]{1,0:T(8,128)(2,1)S(1)}, bf16[384,128]{1,0:T(8,128)(2,1)S(1)}, bf16[64,768]{1,0:T(8,128)(2,1)S(...) custom-call(f32[8,16,16,128]{3,2,1,0:T(8,128)S(1)} %get-tuple-element.20.b_ref, ...), custom_call_target="tpu_custom_call" | custom-call | flops 11796480 | bytes 2359296 | tf_op jit(solution)/shard_map/inner/pallas_call | solution.py:570
  11.3 0.0 copy-start
  11.3 0.0 collective-permute-done.2.zbelow_ref
  11.3 0.4 %collective-permute-done.3.zabove_ref = f32[56,256]{1,0:T(8,128)S(1)} collective-permute-done((f32[56,256]{1,0:T(8,128)S(1)}, f32[56,256]{1,0:T(8,128)S(1)}, u32[]{:S(2)}, u32[]{:S(2)}) %collective-permute-start.3) | collective-permute-done | bytes 57376 | tf_op jit(solution)/shard_map/ppermute | solution.py:566
  11.8 0.1 collective-permute-done.below_ref
  11.9 0.0 collective-permute-done.1.above_ref
  11.9 2.9 %main.1 = (f32[8,12,16,128]{3,2,1,0:T(8,128)S(1)}, f32[32,128]{1,0:T(8,128)}) custom-call(f32[8,16,16,128]{3,2,1,0:T(8,128)S(1)} %get-tuple-element.20.b_ref, f32[16,16,128]{2,1,0:T(8,128)S(1)} %get-tuple-element.21.pot_ref, f32[8,12,16,128]{3,2,1,0:T(8,128)S(1)} %get-tuple-element.24.inner_ref, f32[384,128]{1,0:T(8,128)S(1)} %collective-permute-done.below_ref, ...), custom_call_target="tpu_custom_call" | custom-call | tf_op jit(solution)/shard_map/main/pallas_call | solution.py:590
  14.8 5.9 %all-to-all-start = ((f32[32,1,128]{2,1,0:T(1,128)}), f32[32,1,128]{2,1,0:T(1,128)S(1)}, u32[]{:S(2)}, u32[]{:S(2)}) async-start(f32[32,1,128]{2,1,0:T(1,128)} %bitcast.1), calls=%async_computation | async-start | bytes 32768 | tf_op jit(solution)/shard_map/all_to_all | solution.py:607
  20.7 0.0 copy-done
  20.7 0.1 multiply_add_fusion.table_ref
  20.8 7.0 %all-to-all-done = f32[32,1,128]{2,1,0:T(1,128)S(1)} async-done(((f32[32,1,128]{2,1,0:T(1,128)}), f32[32,1,128]{2,1,0:T(1,128)S(1)}, u32[]{:S(2)}, u32[]{:S(2)}) %all-to-all-start) | async-done | bytes 16416 | tf_op jit(solution)/shard_map/all_to_all | solution.py:607
  27.8 1.7 %output.1 = f32[4,2,4,8,16,128]{5,4,3,2,1,0:T(8,128)} custom-call(f32[32,128]{1,0:T(8,128)S(1)} %bitcast.7, f32[16,128]{1,0:T(8,128)S(1)} %multiply_add_fusion.table_ref, f32[8,16,16,128]{3,2,1,0:T(8,128)S(1)} %get-tuple-element.20.b_ref, f32[8,12,16,128]{3,2,1,0:T(8,128)S(1)} %get-tuple-element.34.h_ref), custom_call_target="tpu_custom_call" | custom-call | tf_op jit(solution)/shard_map/output/pallas_call | solution.py:612
  (1 shorter events, 0.0 us)
Async XLA Ops:
  2.2 9.7 %collective-permute-start.1 = (f32[672,128]{1,0:T(8,128)S(1)}, f32[672,128]{1,0:T(8,128)S(1)}, u32[]{:S(2)}, u32[]{:S(2)}) collective-permute-start(f32[672,128]{1,0:T(8,128)S(1)} %get-tuple-element.26), channel_id=1, source_target_pairs={{0,12},{4,0},{8,4},{12,8},{1,13},{5,1},{9,5},{13,9},{2,14},{6,2},{... | collective-permute-start | bytes 1032200 | tf_op jit(solution)/shard_map/ppermute | solution.py:564
  4.7 7.2 %collective-permute-start = (f32[384,128]{1,0:T(8,128)S(1)}, f32[384,128]{1,0:T(8,128)S(1)}, u32[]{:S(2)}, u32[]{:S(2)}) collective-permute-start(f32[384,128]{1,0:T(8,128)S(1)} %get-tuple-element.25), channel_id=1, source_target_pairs={{0,4},{4,8},{8,12},{12,0},{1,5},{5,9},{9,13},{13,1},{2,6},{6,10},{... | collective-permute-start | bytes 589832 | tf_op jit(solution)/shard_map/ppermute | solution.py:565
  4.7 6.7 %collective-permute-start.2 = (f32[56,256]{1,0:T(8,128)S(1)}, f32[56,256]{1,0:T(8,128)S(1)}, u32[]{:S(2)}, u32[]{:S(2)}) collective-permute-start(f32[56,256]{1,0:T(8,128)S(1)} %get-tuple-element.22.zup_ref), channel_id=1, source_target_pairs={{0,1},{1,2},{2,3},{3,0},{4,5},{5,6},{6,7},{7,4},{8,9},{9,10},{10,1... | collective-permute-start | bytes 172040 | tf_op jit(solution)/shard_map/ppermute | solution.py:567
  6.2 5.5 %collective-permute-start.3 = (f32[56,256]{1,0:T(8,128)S(1)}, f32[56,256]{1,0:T(8,128)S(1)}, u32[]{:S(2)}, u32[]{:S(2)}) collective-permute-start(f32[56,256]{1,0:T(8,128)S(1)} %get-tuple-element.23.zdown_ref), channel_id=1, source_target_pairs={{0,3},{1,0},{2,1},{3,2},{4,7},{5,4},{6,5},{7,6},{8,11},{9,8},{10,9... | collective-permute-start | bytes 172040 | tf_op jit(solution)/shard_map/ppermute | solution.py:566
  11.3 9.4 %copy-start = (f32[16,128]{1,0:T(8,128)S(1)}, f32[16,128]{1,0:T(8,128)}, u32[]{:S(2)}) copy-start(f32[16,128]{1,0:T(8,128)} %constant.9.clone) | copy-start | bytes 24580
  14.8 13.0 %all-to-all-start = ((f32[32,1,128]{2,1,0:T(1,128)}), f32[32,1,128]{2,1,0:T(1,128)S(1)}, u32[]{:S(2)}, u32[]{:S(2)}) async-start(f32[32,1,128]{2,1,0:T(1,128)} %bitcast.1), calls=%async_computation | async-start | bytes 32768 | tf_op jit(solution)/shard_map/all_to_all | solution.py:607

commit v6 on v5

--- a/solution.py
+++ b/solution.py
@@ -62,7 +62,7 @@
 
 
 def load_kernel(
-    owned, re_hbm, im_hbm, pot_hbm, b_ref, pot_ref, up_ref, down_ref, zup_ref, zdown_ref, edge_ref, sems
+    owned, re_hbm, im_hbm, pot_hbm, b_ref, pot_ref, up_ref, down_ref, zup_ref, zdown_ref, pick_ref, sems
 ):
     fields, cx, ny, nz = b_ref.shape
     srcs = fields // 2
@@ -85,7 +85,13 @@
     for group in copies:
         for copy in group:
             copy.start()
-    edge_ref[...] = jnp.zeros(edge_ref.shape, jnp.float32)
+    shape = (2 * nz, nz)
+    layer = lax.broadcasted_iota(jnp.int32, shape, 0) % nz
+    lane = lax.broadcasted_iota(jnp.int32, shape, 1)
+    spot = lax.rem(layer + 2 * REACH, nz)
+    for f in range(fields):
+        chosen = (spot < 4 * REACH) & (lane == spot + 4 * REACH * f)
+        pick_ref[f] = jnp.where(chosen, 1.0, 0.0).astype(jnp.bfloat16)
     far = fields * reach
     for f in range(fields):
         for copy in copies[f]:
@@ -97,7 +103,6 @@
         for x in range(owned):
             at = (far + f * owned + x) * REACH
             down_ref[at : at + REACH, :] = b_ref[f, x, REACH : 2 * REACH, :]
-        edge_ref[...] = gather_edges(edge_ref[...], f, b_ref[f].reshape(cx * ny, nz))
     for copy in copies[fields]:
         copy.wait()
     pot_ref[...] = pot_ref[...] + (DIAG - MIDDLE)
@@ -110,7 +115,9 @@
     zup_ref[after : after + REACH, :] = turned[REACH : 2 * REACH]
     zup_ref[after + REACH : after + 2 * REACH, :] = turned[0:REACH]
     zdown_ref[after : after + 2 * REACH, :] = turned[2 * REACH : 4 * REACH]
-    turned = edge_ref[...].T
+    pieces = [split(b_ref[f].reshape(cx * ny, nz)) for f in range(fields)]
+    wide = jnp.concatenate([half for pair in pieces for half in pair], axis=1)
+    turned = mul(wide, pick_ref[...].reshape(2 * fields * nz, nz)).T
     for f in range(fields):
         at = 4 * REACH * f
         low, high = f * REACH, (f + 1) * REACH
@@ -171,10 +178,13 @@
     beyond_ref,
     back_ref,
     fix_ref,
+    pairs_ref,
     edges_ref,
+    base_ref,
     pad_ref,
 ):
     fields, cx, ny, nz = b_ref.shape
+    srcs = fields // 2
     reach = out_ref.shape[1]
     rows = fields * REACH
     both_ref[...] = wide_right(band((nz, nz), 0, (1, -1)))
@@ -199,6 +209,16 @@
         return 0
 
     lax.fori_loop(0, fields, field, 0)
+
+    shape = (owned * ny, reach * ny)
+    to = lax.broadcasted_iota(jnp.int32, shape, 0)
+    of = lax.broadcasted_iota(jnp.int32, shape, 1)
+    planes, row_steps = of // ny - to // ny, of % ny - to % ny
+    pairs = jnp.zeros(shape, jnp.float32)
+    for k in range(1, REACH + 1):
+        hit = ((planes == k) & (row_steps == 0)) | ((planes == 0) & (row_steps == k))
+        pairs = jnp.where(hit, 2.0 * SIDE[k], pairs)
+    pairs_ref[...] = wide_left(pairs)
 
     shape = (2 * rows, 8 * rows)
     row_at, row_field = layer_of(lax.broadcasted_iota(jnp.int32, shape, 0), (-REACH, nz), rows)
@@ -221,6 +241,14 @@
     weight = jnp.where(lane < owned * ny, jnp.where(lane % ny >= ny // 2, 3.0, 1.0), 0.0)
     edges = jnp.concatenate([zdown_ref[0:rows, 0:LANES], zup_ref[0:rows, 0:LANES]], axis=0)
     edges_ref[...] = around(edges, ny) * weight
+    for s in range(srcs):
+        re = im = jnp.zeros((ny, nz), jnp.float32)
+        for x in range(owned):
+            br, bi = b_ref[s, x], b_ref[srcs + s, x]
+            re = re + (br * br - bi * bi)
+            im = im + br * bi
+        base_ref[s : s + 1, :] = fold(re)
+        base_ref[srcs + s : srcs + s + 1, :] = fold(2.0 * im)
 
 
 def fold(value):
@@ -247,7 +275,9 @@
     beyond_ref,
     back_ref,
     fix_ref,
+    pairs_ref,
     edges_ref,
+    base_ref,
     h_ref,
     out_ref,
     pad_ref,
@@ -264,7 +294,8 @@
     after = rows + rows // 2
 
     outer = jnp.concatenate([zbelow_ref[0:rows], zabove_ref[0:rows]], axis=0)
-    wide = wide_left(outer.T[0 : reach * ny])
+    high = outer.astype(jnp.bfloat16).astype(jnp.float32)
+    wide = jnp.concatenate([high, outer - high, high], axis=0).T[0 : reach * ny].astype(jnp.bfloat16)
     near = outer[:, 0:LANES]
 
     def second(ref):
@@ -279,29 +310,13 @@
         axis=0,
     )
     image = mul(beyond_ref[...], wide_right(stack))
-    local = jnp.concatenate(
-        [zbelow_ref[after : after + REACH, 0:LANES]] * fields
-        + [zabove_ref[after : after + REACH, 0:LANES]] * fields,
-        axis=0,
-    )
-    image = image + local * near
-    y = lax.broadcasted_iota(jnp.int32, (2 * rows, LANES), 1) % ny
-    width = cx * ny
-    for k in range(1, REACH + 1):
-        sides = pltpu.roll(outer, ny * k, 1) + pltpu.roll(outer, width - ny * k, 1)
-        sides = sides[:, 0:LANES] + jnp.where(y >= k, pltpu.roll(near, k, 1), 0.0)
-        sides = sides + jnp.where(y < ny - k, pltpu.roll(near, LANES - k, 1), 0.0)
-        image = image + SIDE[k] * sides
-    reached = mul(back_ref[...], wide_right(jnp.concatenate([image, near], axis=0)))
-    turned = around(reached[2 * rows : 4 * rows], ny)
-
     for f in range(fields):
         h_ref[f] = mul(wide, fix_ref[f]).reshape(reach, ny, nz)
     zero = jnp.zeros((reach, 16, nz), jnp.float32)
     pad_ref[0] = zero
     pad_ref[1] = zero
     edge_ref[...] = jnp.zeros(edge_ref.shape, jnp.float32)
-    for f in range(fields):
+    def border(f):
         for x in range(reach):
             at = (f * reach + x) * REACH
             pad_ref[0, x, 8 - REACH : 8, :] = below_ref[at : at + REACH, :]
@@ -321,9 +336,40 @@
                 spot = pl.ds(x * ny, ny)
                 edge_ref[spot, :] = gather_edges(edge_ref[spot, :], f, u)
 
-    for f in range(fields):
-        own = h_ref[f, 0:owned].reshape(owned * ny, nz)
-        step_ref[f] = mul(wide_left(own), half_ref[...]).reshape(owned, ny, nz)
+    cuts = [fields * n // 4 for n in range(5)]
+    for f in range(cuts[0], cuts[1]):
+        border(f)
+    local = jnp.concatenate(
+        [zbelow_ref[after : after + REACH, 0:LANES]] * fields
+        + [zabove_ref[after : after + REACH, 0:LANES]] * fields,
+        axis=0,
+    )
+    image = image + local * near
+    y = lax.broadcasted_iota(jnp.int32, (2 * rows, LANES), 1) % ny
+    width = cx * ny
+    for k in range(1, REACH + 1):
+        sides = pltpu.roll(outer, ny * k, 1) + pltpu.roll(outer, width - ny * k, 1)
+        sides = sides[:, 0:LANES] + jnp.where(y >= k, pltpu.roll(near, k, 1), 0.0)
+        sides = sides + jnp.where(y < ny - k, pltpu.roll(near, LANES - k, 1), 0.0)
+        image = image + SIDE[k] * sides
+    for f in range(cuts[1], cuts[2]):
+        border(f)
+    reached = mul(back_ref[...], wide_right(jnp.concatenate([image, near], axis=0)))
+    for f in range(cuts[2], cuts[3]):
+        border(f)
+    turned = around(reached[2 * rows : 4 * rows], ny)
+    for f in range(cuts[3], cuts[4]):
+        border(f)
+
+    for s in range(srcs):
+        values = [h_ref[f].reshape(reach * ny, nz) for f in (s, srcs + s)]
+        along = mul(pairs_ref[...], jnp.concatenate([wide_right(v) for v in values], axis=1))
+        for part in range(2):
+            f = part * srcs + s
+            own = values[part][0 : owned * ny]
+            step = mul(wide_left(own), half_ref[...]) + along[:, part * nz : (part + 1) * nz]
+            step_ref[f] = step.reshape(owned, ny, nz)
+    for f in range(fields):
         at = f * reach * REACH
         far_ref[f] = mul(wide_left(above_ref[at : at + owned * REACH, :]), both_ref[...])
 
@@ -352,24 +398,15 @@
             at = (f * reach + x) * REACH
             pull_ref[at : at + 8, :] = pull
 
-    row = lax.broadcasted_iota(jnp.int32, (ny, nz), 0)
-    inside = [row < ny - k for k in range(REACH + 1)]
     for s in range(srcs):
-        total = [jnp.zeros((ny, nz), jnp.float32) for _ in range(8)]
+        total = [jnp.zeros((ny, nz), jnp.float32) for _ in range(6)]
         for x in range(owned):
             local = pot_ref[x]
             b = (b_ref[s, x], b_ref[srcs + s, x])
-            h, g = [], []
-            for part in range(2):
-                f = part * srcs + s
-                own = h_ref[f, x]
-                value = step_ref[f, x] + local * own
-                for k in range(1, REACH + 1):
-                    up = jnp.where(inside[k], pltpu.roll(own, ny - k, 0), 0.0)
-                    value = value + (2.0 * SIDE[k]) * (h_ref[f, (x + k) % cx] + up)
-                h.append(own)
-                g.append(value)
-            terms = product(b, b) + product(b, h) + product(h, h) + product(h, g)
+            h = (h_ref[s, x], h_ref[srcs + s, x])
+            g = [step_ref[part * srcs + s, x] + local * h[part] for part in range(2)]
+            squares = (h[0] * h[0] - h[1] * h[1], h[0] * h[1])
+            terms = product(b, h) + squares + product(h, g)
             total = [t + v for t, v in zip(total, terms)]
         cross = [jnp.zeros((8, nz), jnp.float32) for _ in range(2)]
         for x in range(0, owned, 2):
@@ -396,12 +433,15 @@
                 pulls.append(pull)
             for c, (one, two) in enumerate(zip(product(left, right), product(first, pulls))):
                 cross[c] = cross[c] + (one + two)
-        for i in range(8):
-            value = fold(total[i])
+        for i in range(2, 8):
+            value = fold(total[i - 2])
+            if i == 5:
+                value = 2.0 * value
             if i >= 6:
                 value = value + 2.0 * fold(cross[i - 6])
             acc_ref[i * srcs + s : i * srcs + s + 1, :] = value
 
+    acc_ref[0 : 2 * srcs, :] = base_ref[...]
     gathered = edge_ref[...].T
     part = rows // 2
     both = [0.0, 0.0]
@@ -498,9 +538,9 @@
                 hr, hi = h_ref[s, x], h_ref[srcs + s, x]
                 buf_ref[s, k, 0, x] = c[0] * br - c[1] * bi + (c[2] * hr - c[3] * hi)
                 buf_ref[s, k, 1, x] = c[0] * bi + c[1] * br + (c[2] * hi + c[3] * hr)
-        copy = pltpu.make_async_copy(buf_ref.at[s], out_hbm.at[:, :, s], sems.at[s])
-        copy.start()
-        copies.append(copy)
+            copy = pltpu.make_async_copy(buf_ref.at[s, k], out_hbm.at[k, :, s], sems.at[s, k])
+            copy.start()
+            copies.append(copy)
     for copy in copies:
         copy.wait()
 
@@ -555,7 +595,7 @@
         in_specs=[HBM] * 3,
         out_specs=(VMEM,) * 6,
         scratch_shapes=[
-            pltpu.VMEM((cx * ny, nz), jnp.float32),
+            pltpu.VMEM((fields, 2 * nz, nz), jnp.bfloat16),
             pltpu.SemaphoreType.DMA((fields + 1, quads)),
         ],
         compiler_params=small(8),
@@ -576,10 +616,12 @@
             half(2 * rows, 24 * rows),
             half(4 * rows, 12 * rows),
             half(fields, 6 * rows, nz),
+            half(owned * ny, 3 * reach * ny),
             shaped(2 * rows, LANES),
+            shaped(2 * srcs, nz),
         ),
         in_specs=[VMEM] * 4,
-        out_specs=(VMEM,) * 7,
+        out_specs=(VMEM,) * 9,
         scratch_shapes=[pltpu.VMEM((reach, ny + 16, nz), jnp.float32)],
         compiler_params=small(12),
         cost_estimate=cost(fields * cells * 60, fields * cells * 12),
@@ -590,7 +632,7 @@
     image, partial = pl.pallas_call(
         functools.partial(main_kernel, owned),
         out_shape=(part, shaped(devices, LANES)),
-        in_specs=[VMEM] * 15,
+        in_specs=[VMEM] * 17,
         out_specs=(VMEM,) * 2,
         scratch_shapes=[
             pltpu.VMEM((2, reach, 16, nz), jnp.float32),
@@ -617,7 +659,7 @@
         scratch_shapes=[
             pltpu.VMEM((4 * MOMS, 8, LANES), jnp.float32),
             pltpu.VMEM((srcs, MOMS, 2, owned, ny, nz), jnp.float32),
-            pltpu.SemaphoreType.DMA((srcs,)),
+            pltpu.SemaphoreType.DMA((srcs, MOMS)),
         ],
         compiler_params=small(12),
         name="output",

time: 29.7 us -> 29.2 us (0.983)
  Pallas kernels: 8.27 us -> 7.91 us
    pallas_call x1, Pallas kernels: 2.9 us -> 2.56 us  [per_device(): pl.pallas_call(functools.partial(main_kernel, owned), out_shape=(part, sh...]
  transfers between devices with their start and end apart: 5 -> 5, of which waited for: 3 -> 3; matrix products, arithmetic and copies ran while one was open for 0% -> 0% of each run, Pallas kernels for 5% -> 6%
where the time goes in v6:
time: 29.2 us; the launch traced here: 28.9 us
  starting transfers between devices  12.2 us (42%)
  Pallas kernels  7.91 us (27%)
  waiting for transfers between devices  7.36 us (25%)
  between operations  1.36 us (5%)
    all_to_all x1, waiting for transfers between devices, per_device(): total = lax.all_to_all(partial, ('quad', 'py', 'pz'), 0, 0)  7.04 us
    all_to_all x1, starting transfers between devices, per_device(): total = lax.all_to_all(partial, ('quad', 'py', 'pz'), 0, 0)  5.91 us
    pallas_call x1, Pallas kernels, per_device(): pl.pallas_call(functools.partial(main_kernel, owned), out_shape=(part, sh...  2.56 us
    ppermute x1, starting transfers between devices, per_device(): above = lax.ppermute(down, 'py', ring(py, -1))  2.49 us
    ppermute x1, starting transfers between devices, per_device(): zabove = lax.ppermute(zdown, 'pz', ring(pz, -1))  2.25 us
    pallas_call x1, Pallas kernels, per_device(): pl.pallas_call(functools.partial(load_kernel, owned), out_shape=(shaped(f...  1.95 us
    pallas_call x1, Pallas kernels, per_device(): pl.pallas_call(functools.partial(inner_kernel, owned), out_shape=(part, h...  1.71 us
    pallas_call x1, Pallas kernels, per_device(): pl.pallas_call(output_kernel, out_shape=shaped(MOMS, 2, srcs, owned, ny,...  1.68 us
  transfers between devices with their start and end apart: 5, of which 3 were waited for; matrix products, arithmetic and copies ran while one was open for 0% of the time, Pallas kernels for 6%

profile of v6, /device:TPU:0, one launch (start us, length us, event | category | flops | bytes accessed | tf_op | source)
XLA Modules:
  0.0 28.9 jit_solution(3721834933074086982)
XLA Ops:
  0.0 1.9 %load.1 = (f32[8,16,16,128]{3,2,1,0:T(8,128)S(1)}, f32[16,16,128]{2,1,0:T(8,128)S(1)}, f32[384,128]{1,0:T(8,128)S(1)}, f32[672,128]{1,0:T(8,128)S(1)}, f32[56,256]{1,0:T(8,128)S(1)}, /*index=5*/f32[56,256]{1,0:T(8,128)S(1)}) custom-call(f32[4,16,16,128]{3,2,1,0:T(8,128)} %re_hbm.1, f32[4,16,16,128]{3,2,1,0:T(8,128)} %im_hbm.1, f32[16,16,128]{2,1,0:T(8,128)} %pot_hbm.1), custom_call_target="tpu_custom_call" | custom-call | tf_op jit(solution)/shard_map/load/pallas_call | solution.py:585
  2.0 2.5 %collective-permute-start.1 = (f32[672,128]{1,0:T(8,128)S(1)}, f32[672,128]{1,0:T(8,128)S(1)}, u32[]{:S(2)}, u32[]{:S(2)}) collective-permute-start(f32[672,128]{1,0:T(8,128)S(1)} %get-tuple-element.28), channel_id=1, source_target_pairs={{0,12},{4,0},{8,4},{12,8},{1,13},{5,1},{9,5},{13,9},{2,14},{6,2},{... | collective-permute-start | bytes 1032200 | tf_op jit(solution)/shard_map/ppermute | solution.py:604
  4.4 0.0 collective-permute-start
  4.4 1.6 %collective-permute-start.2 = (f32[56,256]{1,0:T(8,128)S(1)}, f32[56,256]{1,0:T(8,128)S(1)}, u32[]{:S(2)}, u32[]{:S(2)}) collective-permute-start(f32[56,256]{1,0:T(8,128)S(1)} %get-tuple-element.24.zup_ref), channel_id=1, source_target_pairs={{0,1},{1,2},{2,3},{3,0},{4,5},{5,6},{6,7},{7,4},{8,9},{9,10},{10,1... | collective-permute-start | bytes 172040 | tf_op jit(solution)/shard_map/ppermute | solution.py:607
  6.0 2.2 %collective-permute-start.3 = (f32[56,256]{1,0:T(8,128)S(1)}, f32[56,256]{1,0:T(8,128)S(1)}, u32[]{:S(2)}, u32[]{:S(2)}) collective-permute-start(f32[56,256]{1,0:T(8,128)S(1)} %get-tuple-element.25.zdown_ref), channel_id=1, source_target_pairs={{0,3},{1,0},{2,1},{3,2},{4,7},{5,4},{6,5},{7,6},{8,11},{9,8},{10,9... | collective-permute-start | bytes 172040 | tf_op jit(solution)/shard_map/ppermute | solution.py:606
  9.6 1.7 %inner.1 = (f32[8,12,16,128]{3,2,1,0:T(8,128)S(1)}, bf16[384,128]{1,0:T(8,128)(2,1)S(1)}, bf16[384,128]{1,0:T(8,128)(2,1)S(1)}, bf16[64,768]{1,0:T(8,128)(2,1)S(...) custom-call(f32[8,16,16,128]{3,2,1,0:T(8,128)S(1)} %get-tuple-elemen, ...), custom_call_target="tpu_custom_call" | custom-call | flops 11796480 | bytes 2359296 | tf_op jit(solution)/shard_map/inner/pallas_call | solution.py:610
  11.3 0.0 copy-start
  11.3 0.0 collective-permute-done.2.zbelow_ref
  11.3 0.2 collective-permute-done.3.zabove_ref
  11.5 0.1 collective-permute-done.below_ref
  11.6 0.0 collective-permute-done.1.above_ref
  11.6 2.6 %main.1 = (f32[8,12,16,128]{3,2,1,0:T(8,128)S(1)}, f32[32,128]{1,0:T(8,128)}) custom-call(f32[8,16,16,128]{3,2,1,0:T(8,128)S(1)} %get-tuple-element.22.b_ref, f32[16,16,128]{2,1,0:T(8,128)S(1)} %get-tuple-element.23.pot_ref, f32[8,12,16,128]{3,2,1,0:T(8,128)S(1)} %get-tuple-element.26.inner_ref, f32[384,128]{1,0:T(8,128)S(1)} %collective-permute-done.below_ref, ...), custom_call_target="tpu_custom_call" | custom-call | tf_op jit(solution)/shard_map/main/pallas_call | solution.py:632
  14.2 5.9 %all-to-all-start = ((f32[32,1,128]{2,1,0:T(1,128)}), f32[32,1,128]{2,1,0:T(1,128)S(1)}, u32[]{:S(2)}, u32[]{:S(2)}) async-start(f32[32,1,128]{2,1,0:T(1,128)} %bitcast.1), calls=%async_computation | async-start | bytes 32768 | tf_op jit(solution)/shard_map/all_to_all | solution.py:649
  20.1 0.0 copy-done
  20.1 0.1 multiply_add_fusion.table_ref
  20.2 7.0 %all-to-all-done = f32[32,1,128]{2,1,0:T(1,128)S(1)} async-done(((f32[32,1,128]{2,1,0:T(1,128)}), f32[32,1,128]{2,1,0:T(1,128)S(1)}, u32[]{:S(2)}, u32[]{:S(2)}) %all-to-all-start) | async-done | bytes 16416 | tf_op jit(solution)/shard_map/all_to_all | solution.py:649
  27.2 1.7 %output.1 = f32[4,2,4,8,16,128]{5,4,3,2,1,0:T(8,128)} custom-call(f32[32,128]{1,0:T(8,128)S(1)} %bitcast.7, f32[16,128]{1,0:T(8,128)S(1)} %multiply_add_fusion.table_ref, f32[8,16,16,128]{3,2,1,0:T(8,128)S(1)} %get-tuple-element.22.b_ref, f32[8,12,16,128]{3,2,1,0:T(8,128)S(1)} %get-tuple-element.38.h_ref), custom_call_target="tpu_custom_call" | custom-call | tf_op jit(solution)/shard_map/output/pallas_call | solution.py:654
  (1 shorter events, 0.0 us)
Async XLA Ops:
  2.0 9.7 %collective-permute-start.1 = (f32[672,128]{1,0:T(8,128)S(1)}, f32[672,128]{1,0:T(8,128)S(1)}, u32[]{:S(2)}, u32[]{:S(2)}) collective-permute-start(f32[672,128]{1,0:T(8,128)S(1)} %get-tuple-element.28), channel_id=1, source_target_pairs={{0,12},{4,0},{8,4},{12,8},{1,13},{5,1},{9,5},{13,9},{2,14},{6,2},{... | collective-permute-start | bytes 1032200 | tf_op jit(solution)/shard_map/ppermute | solution.py:604
  4.4 7.2 %collective-permute-start = (f32[384,128]{1,0:T(8,128)S(1)}, f32[384,128]{1,0:T(8,128)S(1)}, u32[]{:S(2)}, u32[]{:S(2)}) collective-permute-start(f32[384,128]{1,0:T(8,128)S(1)} %get-tuple-element.27), channel_id=1, source_target_pairs={{0,4},{4,8},{8,12},{12,0},{1,5},{5,9},{9,13},{13,1},{2,6},{6,10},{... | collective-permute-start | bytes 589832 | tf_op jit(solution)/shard_map/ppermute | solution.py:605
  4.4 6.9 %collective-permute-start.2 = (f32[56,256]{1,0:T(8,128)S(1)}, f32[56,256]{1,0:T(8,128)S(1)}, u32[]{:S(2)}, u32[]{:S(2)}) collective-permute-start(f32[56,256]{1,0:T(8,128)S(1)} %get-tuple-element.24.zup_ref), channel_id=1, source_target_pairs={{0,1},{1,2},{2,3},{3,0},{4,5},{5,6},{6,7},{7,4},{8,9},{9,10},{10,1... | collective-permute-start | bytes 172040 | tf_op jit(solution)/shard_map/ppermute | solution.py:607
  6.0 5.5 %collective-permute-start.3 = (f32[56,256]{1,0:T(8,128)S(1)}, f32[56,256]{1,0:T(8,128)S(1)}, u32[]{:S(2)}, u32[]{:S(2)}) collective-permute-start(f32[56,256]{1,0:T(8,128)S(1)} %get-tuple-element.25.zdown_ref), channel_id=1, source_target_pairs={{0,3},{1,0},{2,1},{3,2},{4,7},{5,4},{6,5},{7,6},{8,11},{9,8},{10,9... | collective-permute-start | bytes 172040 | tf_op jit(solution)/shard_map/ppermute | solution.py:606
  11.3 8.8 %copy-start = (f32[16,128]{1,0:T(8,128)S(1)}, f32[16,128]{1,0:T(8,128)}, u32[]{:S(2)}) copy-start(f32[16,128]{1,0:T(8,128)} %constant.9.clone) | copy-start | bytes 24580
  14.2 13.0 %all-to-all-start = ((f32[32,1,128]{2,1,0:T(1,128)}), f32[32,1,128]{2,1,0:T(1,128)S(1)}, u32[]{:S(2)}, u32[]{:S(2)}) async-start(f32[32,1,128]{2,1,0:T(1,128)} %bitcast.1), calls=%async_computation | async-start | bytes 32768 | tf_op jit(solution)/shard_map/all_to_all | solution.py:649

commit v7 on v6

--- a/solution.py
+++ b/solution.py
@@ -9,6 +9,7 @@
 from jax.experimental.pallas import tpu as pltpu
 from jax.sharding import PartitionSpec as P
 
+
 QPTS = 8
 MOMS = 4
 REACH = 4
@@ -18,13 +19,6 @@
 DIAG = -1.5 * stencil_weights[0]
 MIDDLE = 5.25
 SIDE = tuple(-0.5 * w for w in stencil_weights)
-HIGHEST = lax.Precision.HIGHEST
-
-
-def dot(left, right, dims):
-    return lax.dot_general(
-        left, right, (dims, ((), ())), precision=HIGHEST, preferred_element_type=jnp.float32
-    )
 
 
 def band(shape, offset, signs, scale=1.0):
@@ -62,7 +56,7 @@
 
 
 def load_kernel(
-    owned, re_hbm, im_hbm, pot_hbm, b_ref, pot_ref, up_ref, down_ref, zup_ref, zdown_ref, pick_ref, sems
+    owned, re_hbm, im_hbm, pot_hbm, b_ref, pot_ref, up_ref, down_ref, far_ref, zup_ref, zdown_ref, pick_ref, sems
 ):
     fields, cx, ny, nz = b_ref.shape
     srcs = fields // 2
@@ -92,7 +86,6 @@
     for f in range(fields):
         chosen = (spot < 4 * REACH) & (lane == spot + 4 * REACH * f)
         pick_ref[f] = jnp.where(chosen, 1.0, 0.0).astype(jnp.bfloat16)
-    far = fields * reach
     for f in range(fields):
         for copy in copies[f]:
             copy.wait()
@@ -101,14 +94,14 @@
             up_ref[at : at + REACH, :] = b_ref[f, x, ny - REACH : ny, :]
             down_ref[at : at + REACH, :] = b_ref[f, x, 0:REACH, :]
         for x in range(owned):
-            at = (far + f * owned + x) * REACH
-            down_ref[at : at + REACH, :] = b_ref[f, x, REACH : 2 * REACH, :]
+            at = (f * owned + x) * REACH
+            far_ref[at : at + REACH, :] = b_ref[f, x, REACH : 2 * REACH, :]
     for copy in copies[fields]:
         copy.wait()
     pot_ref[...] = pot_ref[...] + (DIAG - MIDDLE)
     for x in range(owned):
-        at = (far + fields * owned + x) * REACH
-        down_ref[at : at + REACH, :] = pot_ref[x, 0:REACH, :]
+        at = (fields * owned + x) * REACH
+        far_ref[at : at + REACH, :] = pot_ref[x, 0:REACH, :]
     turned = pltpu.roll(pot_ref[...].reshape(cx * ny, nz), 2 * REACH, 1).T
     rows = fields * REACH
     after = rows + rows // 2
@@ -270,7 +263,6 @@
     zdown_ref,
     zbelow_ref,
     zabove_ref,
-    both_ref,
     half_ref,
     beyond_ref,
     back_ref,
@@ -279,13 +271,10 @@
     edges_ref,
     base_ref,
     h_ref,
-    out_ref,
+    acc_ref,
     pad_ref,
     edge_ref,
-    acc_ref,
     step_ref,
-    far_ref,
-    pull_ref,
 ):
     fields, reach, ny, nz = inner_ref.shape
     cx = b_ref.shape[1]
@@ -316,6 +305,7 @@
     pad_ref[0] = zero
     pad_ref[1] = zero
     edge_ref[...] = jnp.zeros(edge_ref.shape, jnp.float32)
+
     def border(f):
         for x in range(reach):
             at = (f * reach + x) * REACH
@@ -369,35 +359,6 @@
             own = values[part][0 : owned * ny]
             step = mul(wide_left(own), half_ref[...]) + along[:, part * nz : (part + 1) * nz]
             step_ref[f] = step.reshape(owned, ny, nz)
-    for f in range(fields):
-        at = f * reach * REACH
-        far_ref[f] = mul(wide_left(above_ref[at : at + owned * REACH, :]), both_ref[...])
-
-    quad_row = lax.broadcasted_iota(jnp.int32, (8, nz), 0) % REACH
-    early = lax.broadcasted_iota(jnp.int32, (8, nz), 0) < REACH
-
-    def top(ref, f, x):
-        return jnp.where(early, pltpu.roll(ref[f, x, ny - 8 : ny, :], REACH, 0), ref[f, x + 1, ny - 8 : ny, :])
-
-    def lowered(lower, upper, k):
-        if k == REACH:
-            return lower
-        return jnp.where(quad_row >= k, pltpu.roll(upper, k, 0), pltpu.roll(lower, REACH + k, 0))
-
-    def raised(lower, upper, k):
-        if k == REACH:
-            return upper
-        return jnp.where(quad_row < REACH - k, pltpu.roll(lower, 8 - k, 0), pltpu.roll(upper, REACH - k, 0))
-
-    for f in range(fields):
-        for x in range(0, reach, 2):
-            own = top(h_ref, f, x)
-            pull = SIDE[REACH] * own
-            for k in range(1, REACH):
-                pull = pull + SIDE[k] * jnp.where(quad_row < k, pltpu.roll(own, REACH + k, 0), 0.0)
-            at = (f * reach + x) * REACH
-            pull_ref[at : at + 8, :] = pull
-
     for s in range(srcs):
         total = [jnp.zeros((ny, nz), jnp.float32) for _ in range(6)]
         for x in range(owned):
@@ -408,37 +369,10 @@
             squares = (h[0] * h[0] - h[1] * h[1], h[0] * h[1])
             terms = product(b, h) + squares + product(h, g)
             total = [t + v for t, v in zip(total, terms)]
-        cross = [jnp.zeros((8, nz), jnp.float32) for _ in range(2)]
-        for x in range(0, owned, 2):
-            at = (fields * (reach + owned) + x) * REACH
-            local = above_ref[at : at + 8, :]
-            left, right, first, pulls = [], [], [], []
-            for part in range(2):
-                f = part * srcs + s
-                at = (f * reach + x) * REACH
-                own = top(b_ref, f, x)
-                first_layers = above_ref[at : at + 8, :]
-                start = (fields * reach + f * owned + x) * REACH
-                more = above_ref[start : start + 8, :]
-                value = far_ref[f, x * REACH : x * REACH + 8, :] + local * first_layers
-                pull = 0.0
-                for k in range(1, REACH + 1):
-                    sides = above_ref[at + k * REACH : at + k * REACH + 8, :]
-                    sides = sides + raised(first_layers, more, k) + lowered(own, first_layers, k)
-                    value = value + SIDE[k] * sides
-                    pull = pull + SIDE[k] * pull_ref[at + k * REACH : at + k * REACH + 8, :]
-                left.append(pull_ref[at : at + 8, :])
-                right.append(value)
-                first.append(first_layers)
-                pulls.append(pull)
-            for c, (one, two) in enumerate(zip(product(left, right), product(first, pulls))):
-                cross[c] = cross[c] + (one + two)
         for i in range(2, 8):
             value = fold(total[i - 2])
             if i == 5:
                 value = 2.0 * value
-            if i >= 6:
-                value = value + 2.0 * fold(cross[i - 6])
             acc_ref[i * srcs + s : i * srcs + s + 1, :] = value
 
     acc_ref[0 : 2 * srcs, :] = base_ref[...]
@@ -461,6 +395,70 @@
             at = (6 + c) * srcs + s
             acc_ref[at : at + 1, :] = acc_ref[at : at + 1, :] + fold(both[c][s * REACH : (s + 1) * REACH])
 
+
+def tail_kernel(owned, b_ref, h_ref, above_ref, more_ref, both_ref, sums_ref, out_ref, acc_ref, far_ref, pull_ref):
+    fields, reach, ny, nz = h_ref.shape
+    srcs = fields // 2
+    for f in range(fields):
+        at = f * reach * REACH
+        far_ref[f] = mul(wide_left(above_ref[at : at + owned * REACH, :]), both_ref[...])
+
+    quad_row = lax.broadcasted_iota(jnp.int32, (8, nz), 0) % REACH
+    early = lax.broadcasted_iota(jnp.int32, (8, nz), 0) < REACH
+
+    def top(ref, f, x):
+        return jnp.where(early, pltpu.roll(ref[f, x, ny - 8 : ny, :], REACH, 0), ref[f, x + 1, ny - 8 : ny, :])
+
+    def lowered(lower, upper, k):
+        if k == REACH:
+            return lower
+        return jnp.where(quad_row >= k, pltpu.roll(upper, k, 0), pltpu.roll(lower, REACH + k, 0))
+
+    def raised(lower, upper, k):
+        if k == REACH:
+            return upper
+        return jnp.where(quad_row < REACH - k, pltpu.roll(lower, 8 - k, 0), pltpu.roll(upper, REACH - k, 0))
+
+    for f in range(fields):
+        for x in range(0, reach, 2):
+            own = top(h_ref, f, x)
+            pull = SIDE[REACH] * own
+            for k in range(1, REACH):
+                pull = pull + SIDE[k] * jnp.where(quad_row < k, pltpu.roll(own, REACH + k, 0), 0.0)
+            at = (f * reach + x) * REACH
+            pull_ref[at : at + 8, :] = pull
+
+    acc_ref[...] = sums_ref[...]
+    for s in range(srcs):
+        cross = [jnp.zeros((8, nz), jnp.float32) for _ in range(2)]
+        for x in range(0, owned, 2):
+            at = (fields * owned + x) * REACH
+            local = more_ref[at : at + 8, :]
+            left, right, first, pulls = [], [], [], []
+            for part in range(2):
+                f = part * srcs + s
+                at = (f * reach + x) * REACH
+                own = top(b_ref, f, x)
+                first_layers = above_ref[at : at + 8, :]
+                start = (f * owned + x) * REACH
+                more = more_ref[start : start + 8, :]
+                value = far_ref[f, x * REACH : x * REACH + 8, :] + local * first_layers
+                pull = 0.0
+                for k in range(1, REACH + 1):
+                    sides = above_ref[at + k * REACH : at + k * REACH + 8, :]
+                    sides = sides + raised(first_layers, more, k) + lowered(own, first_layers, k)
+                    value = value + SIDE[k] * sides
+                    pull = pull + SIDE[k] * pull_ref[at + k * REACH : at + k * REACH + 8, :]
+                left.append(pull_ref[at : at + 8, :])
+                right.append(value)
+                first.append(first_layers)
+                pulls.append(pull)
+            for c, (one, two) in enumerate(zip(product(left, right), product(first, pulls))):
+                cross[c] = cross[c] + (one + two)
+        for c in range(2):
+            at = (6 + c) * srcs + s
+            acc_ref[at : at + 1, :] = acc_ref[at : at + 1, :] + 2.0 * fold(cross[c])
+
     column = jnp.sum(acc_ref[...], axis=1, keepdims=True)
     row = lax.broadcasted_iota(jnp.int32, acc_ref.shape, 0)
     lane = lax.broadcasted_iota(jnp.int32, acc_ref.shape, 1)
@@ -480,7 +478,7 @@
 
 
 def output_kernel(tot_ref, table_ref, b_ref, h_ref, out_hbm, coef_ref, buf_ref, sems):
-    fields, cx, ny, nz = b_ref.shape
+    fields, _, ny, nz = b_ref.shape
     srcs = fields // 2
     planes = buf_ref.shape[3]
     shape = (srcs, LANES)
@@ -549,6 +547,10 @@
     return [(i, (i + step) % count) for i in range(count)]
 
 
+def shift(value, axis, step):
+    return lax.ppermute(value, axis, ring(lax.axis_size(axis), step))
+
+
 ANY = pl.BlockSpec(memory_space=pl.ANY)
 HBM = pl.BlockSpec(memory_space=pltpu.HBM)
 VMEM = pl.BlockSpec(memory_space=pltpu.VMEM)
@@ -582,18 +584,19 @@
     )
     part = shaped(fields, reach, ny, nz)
     flat = shaped(rows + rows // 2 + 2 * REACH, cx * ny)
-    b, pot, up, down, zup, zdown = pl.pallas_call(
+    b, pot, up, down, far, zup, zdown = pl.pallas_call(
         functools.partial(load_kernel, owned),
         out_shape=(
             shaped(fields, cx, ny, nz),
             shaped(cx, ny, nz),
             shaped(fields * reach * REACH, nz),
-            shaped((fields * (reach + owned) + owned) * REACH, nz),
+            shaped(fields * reach * REACH, nz),
+            shaped((fields + 1) * owned * REACH, nz),
             flat,
             flat,
         ),
         in_specs=[HBM] * 3,
-        out_specs=(VMEM,) * 6,
+        out_specs=(VMEM,) * 7,
         scratch_shapes=[
             pltpu.VMEM((fields, 2 * nz, nz), jnp.bfloat16),
             pltpu.SemaphoreType.DMA((fields + 1, quads)),
@@ -601,10 +604,11 @@
         compiler_params=small(8),
         name="load",
     )(source_real, source_imag, potential)
-    above = lax.ppermute(down, "py", ring(py, -1))
-    below = lax.ppermute(up, "py", ring(py, 1))
-    zabove = lax.ppermute(zdown, "pz", ring(pz, -1))
-    zbelow = lax.ppermute(zup, "pz", ring(pz, 1))
+    above = shift(down, "py", -1)
+    below = shift(up, "py", 1)
+    zabove = shift(zdown, "pz", -1)
+    zbelow = shift(zup, "pz", 1)
+    more = shift(far, "py", -1)
 
     half = lambda *dims: jax.ShapeDtypeStruct(dims, jnp.bfloat16)
     inner, *weights = pl.pallas_call(
@@ -628,23 +632,35 @@
         name="inner",
     )(b, pot, zup, zdown)
 
-    devices = quads * py * pz
-    image, partial = pl.pallas_call(
+    both, *weights = weights
+    image, sums = pl.pallas_call(
         functools.partial(main_kernel, owned),
-        out_shape=(part, shaped(devices, LANES)),
-        in_specs=[VMEM] * 17,
+        out_shape=(part, shaped(8 * srcs, nz)),
+        in_specs=[VMEM] * 16,
         out_specs=(VMEM,) * 2,
         scratch_shapes=[
             pltpu.VMEM((2, reach, 16, nz), jnp.float32),
             pltpu.VMEM((LANES, nz), jnp.float32),
+            pltpu.VMEM((fields, owned, ny, nz), jnp.float32),
+        ],
+        compiler_params=small(12),
+        cost_estimate=cost(fields * cells * 60, fields * cells * 12),
+        name="main",
+    )(b, pot, inner, below, above, zup, zdown, zbelow, zabove, *weights)
+
+    partial = pl.pallas_call(
+        functools.partial(tail_kernel, owned),
+        out_shape=shaped(quads * py * pz, LANES),
+        in_specs=[VMEM] * 6,
+        out_specs=VMEM,
+        scratch_shapes=[
             pltpu.VMEM((8 * srcs, nz), jnp.float32),
-            pltpu.VMEM((fields, owned, ny, nz), jnp.float32),
             pltpu.VMEM((fields, owned * REACH, nz), jnp.float32),
             pltpu.VMEM((fields * reach * REACH, nz), jnp.float32),
         ],
-        compiler_params=small(12),
-        name="main",
-    )(b, pot, inner, below, above, zup, zdown, zbelow, zabove, *weights)
+        compiler_params=small(8),
+        name="tail",
+    )(b, image, above, more, both, sums)
 
     total = lax.all_to_all(partial, ("quad", "py", "pz"), 0, 0)
 
@@ -669,6 +685,7 @@
 def solution(mesh):
     in_specs = (P(None, None, "py", "pz"), P(None, None, "py", "pz"), P(None, "py", "pz"), P(), P())
     out_specs = P(None, None, None, "quad", "py", "pz")
+
     return jax.shard_map(
         per_device, mesh=mesh, in_specs=in_specs, out_specs=out_specs, check_vma=False
     )

time: 29.2 us -> 29.1 us (level)
  waiting for transfers between devices: 7.36 us -> 7.05 us
    ppermute x4 -> x5, starting transfers between devices: 6.31 us -> 8.06 us  [shift(): return lax.ppermute(value, axis, ring(lax.axis_size(axis), step))]
    all_to_all x1, starting transfers between devices: 5.91 us -> 4.26 us  [per_device(): total = lax.all_to_all(partial, ('quad', 'py', 'pz'), 0, 0)]
    pallas_call x0 -> x1, Pallas kernels: none -> 1.15 us  [per_device(): pl.pallas_call(functools.partial(tail_kernel, owned), out_shape=shaped(qu...]
    pallas_call x1, Pallas kernels: 2.56 us -> 1.52 us  [per_device(): pl.pallas_call(functools.partial(main_kernel, owned), out_shape=(part, sh...]
    ppermute x4 -> x5, waiting for transfers between devices: 0.32 us -> 0.01 us  [shift(): return lax.ppermute(value, axis, ring(lax.axis_size(axis), step))]
  transfers between devices with their start and end apart: 5 -> 6, of which waited for: 3 -> 1; matrix products, arithmetic and copies ran while one was open for 0% -> 0% of each run, Pallas kernels for 6% -> 11%
where the time goes in v7:
time: 29.1 us; the launch traced here: 28.9 us
  starting transfers between devices  12.3 us (42%)
  Pallas kernels  8.02 us (28%)
  waiting for transfers between devices  7.05 us (24%)
  between operations  1.39 us (5%)
    ppermute x5, starting transfers between devices, shift(): return lax.ppermute(value, axis, ring(lax.axis_size(axis), step))  8.06 us
    all_to_all x1, waiting for transfers between devices, per_device(): total = lax.all_to_all(partial, ('quad', 'py', 'pz'), 0, 0)  7.04 us
    all_to_all x1, starting transfers between devices, per_device(): total = lax.all_to_all(partial, ('quad', 'py', 'pz'), 0, 0)  4.26 us
    pallas_call x1, Pallas kernels, per_device(): pl.pallas_call(functools.partial(load_kernel, owned), out_shape=(shaped(f...  1.95 us
    pallas_call x1, Pallas kernels, per_device(): pl.pallas_call(functools.partial(inner_kernel, owned), out_shape=(part, h...  1.71 us
    pallas_call x1, Pallas kernels, per_device(): pl.pallas_call(output_kernel, out_shape=shaped(MOMS, 2, srcs, owned, ny,...  1.68 us
    pallas_call x1, Pallas kernels, per_device(): pl.pallas_call(functools.partial(main_kernel, owned), out_shape=(part, sh...  1.52 us
    pallas_call x1, Pallas kernels, per_device(): pl.pallas_call(functools.partial(tail_kernel, owned), out_shape=shaped(qu...  1.15 us
  transfers between devices with their start and end apart: 6, of which 1 were waited for; matrix products, arithmetic and copies ran while one was open for 0% of the time, Pallas kernels for 11%

profile of v7, /device:TPU:0, one launch (start us, length us, event | category | flops | bytes accessed | tf_op | source)
XLA Modules:
  0.0 28.9 jit_solution(18383354912444262373)
XLA Ops:
  0.0 1.9 %load.1 = (f32[8,16,16,128]{3,2,1,0:T(8,128)S(1)}, f32[16,16,128]{2,1,0:T(8,128)S(1)}, f32[384,128]{1,0:T(8,128)S(1)}, f32[384,128]{1,0:T(8,128)S(1)}, f32[288,1...) custom-call(f32[4,16,16,128]{3,2,1,0:T(8,128)} %re_hbm.1, f32[4,16,16,128]{3,2,1,0:T(8,128)} %im_hbm.1, ...), custom_call_target="tpu_custom_call" | custom-call | tf_op jit(solution)/shard_map/load/pallas_call | solution.py:587
  2.0 2.5 %collective-permute-start.1 = (f32[384,128]{1,0:T(8,128)S(1)}, f32[384,128]{1,0:T(8,128)S(1)}, u32[]{:S(2)}, u32[]{:S(2)}) collective-permute-start(f32[384,128]{1,0:T(8,128)S(1)} %get-tuple-element.29), channel_id=1, source_target_pairs={{0,12},{4,0},{8,4},{12,8},{1,13},{5,1},{9,5},{13,9},{2,14},{6,2},{... | collective-permute-start | bytes 589832 | tf_op jit(solution)/shard_map/ppermute | solution.py:551
  4.4 0.0 collective-permute-start
  4.4 1.7 %collective-permute-start.4 = (f32[288,128]{1,0:T(8,128)S(1)}, f32[288,128]{1,0:T(8,128)S(1)}, u32[]{:S(2)}, u32[]{:S(2)}) collective-permute-start(f32[288,128]{1,0:T(8,128)S(1)} %get-tuple-element.38), channel_id=1, source_target_pairs={{0,12},{4,0},{8,4},{12,8},{1,13},{5,1},{9,5},{13,9},{2,14},{6,2},{... | collective-permute-start | bytes 442376 | tf_op jit(solution)/shard_map/ppermute | solution.py:551
  6.2 1.6 %collective-permute-start.2 = (f32[56,256]{1,0:T(8,128)S(1)}, f32[56,256]{1,0:T(8,128)S(1)}, u32[]{:S(2)}, u32[]{:S(2)}) collective-permute-start(f32[56,256]{1,0:T(8,128)S(1)} %get-tuple-element.25.zup_ref), channel_id=1, source_target_pairs={{0,1},{1,2},{2,3},{3,0},{4,5},{5,6},{6,7},{7,4},{8,9},{9,10},{10,1... | collective-permute-start | bytes 172040 | tf_op jit(solution)/shard_map/ppermute | solution.py:551
  7.8 2.2 %collective-permute-start.3 = (f32[56,256]{1,0:T(8,128)S(1)}, f32[56,256]{1,0:T(8,128)S(1)}, u32[]{:S(2)}, u32[]{:S(2)}) collective-permute-start(f32[56,256]{1,0:T(8,128)S(1)} %get-tuple-element.26.zdown_ref), channel_id=1, source_target_pairs={{0,3},{1,0},{2,1},{3,2},{4,7},{5,4},{6,5},{7,6},{8,11},{9,8},{10,9... | collective-permute-start | bytes 172040 | tf_op jit(solution)/shard_map/ppermute | solution.py:551
  11.3 1.7 %inner.1 = (f32[8,12,16,128]{3,2,1,0:T(8,128)S(1)}, bf16[384,128]{1,0:T(8,128)(2,1)S(1)}, bf16[384,128]{1,0:T(8,128)(2,1)S(1)}, bf16[64,768]{1,0:T(8,128)(2,1)S(...) custom-call(f32[8,16,16,128]{3,2,1,0:T(8,128)S(1)} %get-tuple-elemen, ...), custom_call_target="tpu_custom_call" | custom-call | flops 11796480 | bytes 2359296 | tf_op jit(solution)/shard_map/inner/pallas_call | solution.py:614
  13.0 0.0 collective-permute-done.2.zbelow_ref
  13.1 0.0 collective-permute-done.3.zabove_ref
  13.1 0.0 collective-permute-done.1.above_ref
  13.1 0.0 collective-permute-done.below_ref
  13.1 0.0 copy-start
  13.1 1.5 %main.1 = (f32[8,12,16,128]{3,2,1,0:T(8,128)S(1)}, f32[32,128]{1,0:T(8,128)S(1)}) custom-call(f32[8,16,16,128]{3,2,1,0:T(8,128)S(1)} %get-tuple-element.23.b_ref, f32[16,16,128]{2,1,0:T(8,128)S(1)} %get-tuple-element.24.pot_ref, f32[8,12,16,128]{3,2,1,0:T(8,128)S(1)} %get-tuple-element.27.inner_ref, f32[384,128]{1,0:T(8,128)S(1)} %collective-permute-done.below_ref, ...), custom_call_target="tpu_custom_call" | custom-call | flops 11796480 | bytes 2359296 | tf_op jit(solution)/shard_map/main/pallas_call | solution.py:636
  14.6 0.0 collective-permute-done.4.more_ref
  14.6 1.2 %tail.1 = f32[32,128]{1,0:T(8,128)} custom-call(f32[8,16,16,128]{3,2,1,0:T(8,128)S(1)} %get-tuple-element.23.b_ref, f32[8,12,16,128]{3,2,1,0:T(8,128)S(1)} %get-tuple-element.37.h_ref, f32[384,128]{1,0:T(8,128)S(1)} %collective-permute-done.1.above_ref, f32[288,128]{1,0:T(8,128)S(1)} %collective-permute-done.4.more_ref, ...), custom_call_target="tpu_custom_call" | custom-call | tf_op jit(solution)/shard_map/tail/pallas_call | solution.py:651
  15.8 4.3 %all-to-all-start = ((f32[32,1,128]{2,1,0:T(1,128)}), f32[32,1,128]{2,1,0:T(1,128)S(1)}, u32[]{:S(2)}, u32[]{:S(2)}) async-start(f32[32,1,128]{2,1,0:T(1,128)} %bitcast.1), calls=%async_computation | async-start | bytes 32768 | tf_op jit(solution)/shard_map/all_to_all | solution.py:665
  20.1 0.0 copy-done
  20.1 0.1 multiply_add_fusion.table_ref
  20.1 7.0 %all-to-all-done = f32[32,1,128]{2,1,0:T(1,128)S(1)} async-done(((f32[32,1,128]{2,1,0:T(1,128)}), f32[32,1,128]{2,1,0:T(1,128)S(1)}, u32[]{:S(2)}, u32[]{:S(2)}) %all-to-all-start) | async-done | bytes 16416 | tf_op jit(solution)/shard_map/all_to_all | solution.py:665
  27.2 1.7 %output.1 = f32[4,2,4,8,16,128]{5,4,3,2,1,0:T(8,128)} custom-call(f32[32,128]{1,0:T(8,128)S(1)} %bitcast.7, f32[16,128]{1,0:T(8,128)S(1)} %multiply_add_fusion.table_ref, f32[8,16,16,128]{3,2,1,0:T(8,128)S(1)} %get-tuple-element.23.b_ref, f32[8,12,16,128]{3,2,1,0:T(8,128)S(1)} %get-tuple-element.37.h_ref), custom_call_target="tpu_custom_call" | custom-call | tf_op jit(solution)/shard_map/output/pallas_call | solution.py:670
  (1 shorter events, 0.0 us)
Async XLA Ops:
  2.0 11.1 %collective-permute-start.1 = (f32[384,128]{1,0:T(8,128)S(1)}, f32[384,128]{1,0:T(8,128)S(1)}, u32[]{:S(2)}, u32[]{:S(2)}) collective-permute-start(f32[384,128]{1,0:T(8,128)S(1)} %get-tuple-element.29), channel_id=1, source_target_pairs={{0,12},{4,0},{8,4},{12,8},{1,13},{5,1},{9,5},{13,9},{2,14},{6,2},{... | collective-permute-start | bytes 589832 | tf_op jit(solution)/shard_map/ppermute | solution.py:551
  4.4 8.6 %collective-permute-start = (f32[384,128]{1,0:T(8,128)S(1)}, f32[384,128]{1,0:T(8,128)S(1)}, u32[]{:S(2)}, u32[]{:S(2)}) collective-permute-start(f32[384,128]{1,0:T(8,128)S(1)} %get-tuple-element.28), channel_id=1, source_target_pairs={{0,4},{4,8},{8,12},{12,0},{1,5},{5,9},{9,13},{13,1},{2,6},{6,10},{... | collective-permute-start | bytes 589832 | tf_op jit(solution)/shard_map/ppermute | solution.py:551
  4.4 10.2 %collective-permute-start.4 = (f32[288,128]{1,0:T(8,128)S(1)}, f32[288,128]{1,0:T(8,128)S(1)}, u32[]{:S(2)}, u32[]{:S(2)}) collective-permute-start(f32[288,128]{1,0:T(8,128)S(1)} %get-tuple-element.38), channel_id=1, source_target_pairs={{0,12},{4,0},{8,4},{12,8},{1,13},{5,1},{9,5},{13,9},{2,14},{6,2},{... | collective-permute-start | bytes 442376 | tf_op jit(solution)/shard_map/ppermute | solution.py:551
  6.2 6.9 %collective-permute-start.2 = (f32[56,256]{1,0:T(8,128)S(1)}, f32[56,256]{1,0:T(8,128)S(1)}, u32[]{:S(2)}, u32[]{:S(2)}) collective-permute-start(f32[56,256]{1,0:T(8,128)S(1)} %get-tuple-element.25.zup_ref), channel_id=1, source_target_pairs={{0,1},{1,2},{2,3},{3,0},{4,5},{5,6},{6,7},{7,4},{8,9},{9,10},{10,1... | collective-permute-start | bytes 172040 | tf_op jit(solution)/shard_map/ppermute | solution.py:551
  7.8 5.3 %collective-permute-start.3 = (f32[56,256]{1,0:T(8,128)S(1)}, f32[56,256]{1,0:T(8,128)S(1)}, u32[]{:S(2)}, u32[]{:S(2)}) collective-permute-start(f32[56,256]{1,0:T(8,128)S(1)} %get-tuple-element.26.zdown_ref), channel_id=1, source_target_pairs={{0,3},{1,0},{2,1},{3,2},{4,7},{5,4},{6,5},{7,6},{8,11},{9,8},{10,9... | collective-permute-start | bytes 172040 | tf_op jit(solution)/shard_map/ppermute | solution.py:551
  13.1 7.0 %copy-start = (f32[16,128]{1,0:T(8,128)S(1)}, f32[16,128]{1,0:T(8,128)}, u32[]{:S(2)}) copy-start(f32[16,128]{1,0:T(8,128)} %constant.9.clone) | copy-start | bytes 24580
  15.8 11.4 %all-to-all-start = ((f32[32,1,128]{2,1,0:T(1,128)}), f32[32,1,128]{2,1,0:T(1,128)S(1)}, u32[]{:S(2)}, u32[]{:S(2)}) async-start(f32[32,1,128]{2,1,0:T(1,128)} %bitcast.1), calls=%async_computation | async-start | bytes 32768 | tf_op jit(solution)/shard_map/all_to_all | solution.py:665

commit v8 on v7

--- a/solution.py
+++ b/solution.py
@@ -64,17 +64,18 @@
     reach = up_ref.shape[0] // (fields * REACH)
     first = lax.axis_index("quad")
     copies = []
-    for f in range(fields + 1):
-        source = pot_hbm if f == fields else (re_hbm, im_hbm)[f // srcs].at[f % srcs]
-        target = pot_ref if f == fields else b_ref.at[f]
+    for n, (source, target) in enumerate(
+        ((pot_hbm, pot_ref), (re_hbm, b_ref.at[pl.ds(0, srcs)]), (im_hbm, b_ref.at[pl.ds(srcs, srcs)]))
+    ):
         group = []
         for j in range(parts):
             at = pl.multiple_of(lax.rem(first + j, parts) * owned, owned)
-            group.append(
-                pltpu.make_async_copy(
-                    source.at[pl.ds(at, owned)], target.at[pl.ds(j * owned, owned)], sems.at[f, j]
-                )
-            )
+            spot = pl.ds(j * owned, owned)
+            if n == 0:
+                ends = source.at[pl.ds(at, owned)], target.at[spot]
+            else:
+                ends = source.at[:, pl.ds(at, owned)], target.at[:, spot]
+            group.append(pltpu.make_async_copy(*ends, sems.at[n, j]))
         copies.append(group)
     for group in copies:
         for copy in group:
@@ -87,8 +88,9 @@
         chosen = (spot < 4 * REACH) & (lane == spot + 4 * REACH * f)
         pick_ref[f] = jnp.where(chosen, 1.0, 0.0).astype(jnp.bfloat16)
     for f in range(fields):
-        for copy in copies[f]:
-            copy.wait()
+        if f % srcs == 0:
+            for copy in copies[1 + f // srcs]:
+                copy.wait()
         for x in range(reach):
             at = (f * reach + x) * REACH
             up_ref[at : at + REACH, :] = b_ref[f, x, ny - REACH : ny, :]
@@ -96,7 +98,7 @@
         for x in range(owned):
             at = (f * owned + x) * REACH
             far_ref[at : at + REACH, :] = b_ref[f, x, REACH : 2 * REACH, :]
-    for copy in copies[fields]:
+    for copy in copies[0]:
         copy.wait()
     pot_ref[...] = pot_ref[...] + (DIAG - MIDDLE)
     for x in range(owned):
@@ -599,7 +601,7 @@
         out_specs=(VMEM,) * 7,
         scratch_shapes=[
             pltpu.VMEM((fields, 2 * nz, nz), jnp.bfloat16),
-            pltpu.SemaphoreType.DMA((fields + 1, quads)),
+            pltpu.SemaphoreType.DMA((3, quads)),
         ],
         compiler_params=small(8),
         name="load",

time: 29.1 us -> 29 us (level)
  no operation moved by 1% of the time
where the time goes in v8:
time: 29 us; the launch traced here: 28.8 us
  starting transfers between devices  12.3 us (42%)
  Pallas kernels  7.95 us (27%)
  waiting for transfers between devices  7.05 us (24%)
  between operations  1.39 us (5%)
    ppermute x5, starting transfers between devices, shift(): return lax.ppermute(value, axis, ring(lax.axis_size(axis), step))  8.06 us
    all_to_all x1, waiting for transfers between devices, per_device(): total = lax.all_to_all(partial, ('quad', 'py', 'pz'), 0, 0)  7.04 us
    all_to_all x1, starting transfers between devices, per_device(): total = lax.all_to_all(partial, ('quad', 'py', 'pz'), 0, 0)  4.26 us
    pallas_call x1, Pallas kernels, per_device(): pl.pallas_call(functools.partial(load_kernel, owned), out_shape=(shaped(f...  1.88 us
    pallas_call x1, Pallas kernels, per_device(): pl.pallas_call(functools.partial(inner_kernel, owned), out_shape=(part, h...  1.71 us
    pallas_call x1, Pallas kernels, per_device(): pl.pallas_call(output_kernel, out_shape=shaped(MOMS, 2, srcs, owned, ny,...  1.68 us
    pallas_call x1, Pallas kernels, per_device(): pl.pallas_call(functools.partial(main_kernel, owned), out_shape=(part, sh...  1.52 us
    pallas_call x1, Pallas kernels, per_device(): pl.pallas_call(functools.partial(tail_kernel, owned), out_shape=shaped(qu...  1.15 us
  transfers between devices with their start and end apart: 6, of which 1 were waited for; matrix products, arithmetic and copies ran while one was open for 0% of the time, Pallas kernels for 11%

profile of v8, /device:TPU:0, one launch (start us, length us, event | category | flops | bytes accessed | tf_op | source)
XLA Modules:
  0.0 28.8 jit_solution(6757512658683491732)
XLA Ops:
  0.0 1.9 %load.1 = (f32[8,16,16,128]{3,2,1,0:T(8,128)S(1)}, f32[16,16,128]{2,1,0:T(8,128)S(1)}, f32[384,128]{1,0:T(8,128)S(1)}, f32[384,128]{1,0:T(8,128)S(1)}, f32[288,1...) custom-call(f32[4,16,16,128]{3,2,1,0:T(8,128)} %re_hbm.1, f32[4,16,16,128]{3,2,1,0:T(8,128)} %im_hbm.1, ...), custom_call_target="tpu_custom_call" | custom-call | tf_op jit(solution)/shard_map/load/pallas_call | solution.py:589
  1.9 2.5 %collective-permute-start.1 = (f32[384,128]{1,0:T(8,128)S(1)}, f32[384,128]{1,0:T(8,128)S(1)}, u32[]{:S(2)}, u32[]{:S(2)}) collective-permute-start(f32[384,128]{1,0:T(8,128)S(1)} %get-tuple-element.29), channel_id=1, source_target_pairs={{0,12},{4,0},{8,4},{12,8},{1,13},{5,1},{9,5},{13,9},{2,14},{6,2},{... | collective-permute-start | bytes 589832 | tf_op jit(solution)/shard_map/ppermute | solution.py:553
  4.4 0.0 collective-permute-start
  4.4 1.7 %collective-permute-start.4 = (f32[288,128]{1,0:T(8,128)S(1)}, f32[288,128]{1,0:T(8,128)S(1)}, u32[]{:S(2)}, u32[]{:S(2)}) collective-permute-start(f32[288,128]{1,0:T(8,128)S(1)} %get-tuple-element.38), channel_id=1, source_target_pairs={{0,12},{4,0},{8,4},{12,8},{1,13},{5,1},{9,5},{13,9},{2,14},{6,2},{... | collective-permute-start | bytes 442376 | tf_op jit(solution)/shard_map/ppermute | solution.py:553
  6.1 1.6 %collective-permute-start.2 = (f32[56,256]{1,0:T(8,128)S(1)}, f32[56,256]{1,0:T(8,128)S(1)}, u32[]{:S(2)}, u32[]{:S(2)}) collective-permute-start(f32[56,256]{1,0:T(8,128)S(1)} %get-tuple-element.25.zup_ref), channel_id=1, source_target_pairs={{0,1},{1,2},{2,3},{3,0},{4,5},{5,6},{6,7},{7,4},{8,9},{9,10},{10,1... | collective-permute-start | bytes 172040 | tf_op jit(solution)/shard_map/ppermute | solution.py:553
  7.7 2.2 %collective-permute-start.3 = (f32[56,256]{1,0:T(8,128)S(1)}, f32[56,256]{1,0:T(8,128)S(1)}, u32[]{:S(2)}, u32[]{:S(2)}) collective-permute-start(f32[56,256]{1,0:T(8,128)S(1)} %get-tuple-element.26.zdown_ref), channel_id=1, source_target_pairs={{0,3},{1,0},{2,1},{3,2},{4,7},{5,4},{6,5},{7,6},{8,11},{9,8},{10,9... | collective-permute-start | bytes 172040 | tf_op jit(solution)/shard_map/ppermute | solution.py:553
  11.2 1.7 %inner.1 = (f32[8,12,16,128]{3,2,1,0:T(8,128)S(1)}, bf16[384,128]{1,0:T(8,128)(2,1)S(1)}, bf16[384,128]{1,0:T(8,128)(2,1)S(1)}, bf16[64,768]{1,0:T(8,128)(2,1)S(...) custom-call(f32[8,16,16,128]{3,2,1,0:T(8,128)S(1)} %get-tuple-elemen, ...), custom_call_target="tpu_custom_call" | custom-call | flops 11796480 | bytes 2359296 | tf_op jit(solution)/shard_map/inner/pallas_call | solution.py:616
  13.0 0.0 collective-permute-done.2.zbelow_ref
  13.0 0.0 collective-permute-done.3.zabove_ref
  13.0 0.0 collective-permute-done.1.above_ref
  13.0 0.0 collective-permute-done.below_ref
  13.0 0.0 copy-start
  13.0 1.5 %main.1 = (f32[8,12,16,128]{3,2,1,0:T(8,128)S(1)}, f32[32,128]{1,0:T(8,128)S(1)}) custom-call(f32[8,16,16,128]{3,2,1,0:T(8,128)S(1)} %get-tuple-element.23.b_ref, f32[16,16,128]{2,1,0:T(8,128)S(1)} %get-tuple-element.24.pot_ref, f32[8,12,16,128]{3,2,1,0:T(8,128)S(1)} %get-tuple-element.27.inner_ref, f32[384,128]{1,0:T(8,128)S(1)} %collective-permute-done.below_ref, ...), custom_call_target="tpu_custom_call" | custom-call | flops 11796480 | bytes 2359296 | tf_op jit(solution)/shard_map/main/pallas_call | solution.py:638
  14.6 0.0 collective-permute-done.4.more_ref
  14.6 1.2 %tail.1 = f32[32,128]{1,0:T(8,128)} custom-call(f32[8,16,16,128]{3,2,1,0:T(8,128)S(1)} %get-tuple-element.23.b_ref, f32[8,12,16,128]{3,2,1,0:T(8,128)S(1)} %get-tuple-element.37.h_ref, f32[384,128]{1,0:T(8,128)S(1)} %collective-permute-done.1.above_ref, f32[288,128]{1,0:T(8,128)S(1)} %collective-permute-done.4.more_ref, ...), custom_call_target="tpu_custom_call" | custom-call | tf_op jit(solution)/shard_map/tail/pallas_call | solution.py:653
  15.7 4.3 %all-to-all-start = ((f32[32,1,128]{2,1,0:T(1,128)}), f32[32,1,128]{2,1,0:T(1,128)S(1)}, u32[]{:S(2)}, u32[]{:S(2)}) async-start(f32[32,1,128]{2,1,0:T(1,128)} %bitcast.1), calls=%async_computation | async-start | bytes 32768 | tf_op jit(solution)/shard_map/all_to_all | solution.py:667
  20.0 0.0 copy-done
  20.0 0.1 multiply_add_fusion.table_ref
  20.1 7.0 %all-to-all-done = f32[32,1,128]{2,1,0:T(1,128)S(1)} async-done(((f32[32,1,128]{2,1,0:T(1,128)}), f32[32,1,128]{2,1,0:T(1,128)S(1)}, u32[]{:S(2)}, u32[]{:S(2)}) %all-to-all-start) | async-done | bytes 16416 | tf_op jit(solution)/shard_map/all_to_all | solution.py:667
  27.1 1.7 %output.1 = f32[4,2,4,8,16,128]{5,4,3,2,1,0:T(8,128)} custom-call(f32[32,128]{1,0:T(8,128)S(1)} %bitcast.7, f32[16,128]{1,0:T(8,128)S(1)} %multiply_add_fusion.table_ref, f32[8,16,16,128]{3,2,1,0:T(8,128)S(1)} %get-tuple-element.23.b_ref, f32[8,12,16,128]{3,2,1,0:T(8,128)S(1)} %get-tuple-element.37.h_ref), custom_call_target="tpu_custom_call" | custom-call | tf_op jit(solution)/shard_map/output/pallas_call | solution.py:672
  (1 shorter events, 0.0 us)
Async XLA Ops:
  1.9 11.1 %collective-permute-start.1 = (f32[384,128]{1,0:T(8,128)S(1)}, f32[384,128]{1,0:T(8,128)S(1)}, u32[]{:S(2)}, u32[]{:S(2)}) collective-permute-start(f32[384,128]{1,0:T(8,128)S(1)} %get-tuple-element.29), channel_id=1, source_target_pairs={{0,12},{4,0},{8,4},{12,8},{1,13},{5,1},{9,5},{13,9},{2,14},{6,2},{... | collective-permute-start | bytes 589832 | tf_op jit(solution)/shard_map/ppermute | solution.py:553
  4.4 8.6 %collective-permute-start = (f32[384,128]{1,0:T(8,128)S(1)}, f32[384,128]{1,0:T(8,128)S(1)}, u32[]{:S(2)}, u32[]{:S(2)}) collective-permute-start(f32[384,128]{1,0:T(8,128)S(1)} %get-tuple-element.28), channel_id=1, source_target_pairs={{0,4},{4,8},{8,12},{12,0},{1,5},{5,9},{9,13},{13,1},{2,6},{6,10},{... | collective-permute-start | bytes 589832 | tf_op jit(solution)/shard_map/ppermute | solution.py:553
  4.4 10.2 %collective-permute-start.4 = (f32[288,128]{1,0:T(8,128)S(1)}, f32[288,128]{1,0:T(8,128)S(1)}, u32[]{:S(2)}, u32[]{:S(2)}) collective-permute-start(f32[288,128]{1,0:T(8,128)S(1)} %get-tuple-element.38), channel_id=1, source_target_pairs={{0,12},{4,0},{8,4},{12,8},{1,13},{5,1},{9,5},{13,9},{2,14},{6,2},{... | collective-permute-start | bytes 442376 | tf_op jit(solution)/shard_map/ppermute | solution.py:553
  6.1 6.9 %collective-permute-start.2 = (f32[56,256]{1,0:T(8,128)S(1)}, f32[56,256]{1,0:T(8,128)S(1)}, u32[]{:S(2)}, u32[]{:S(2)}) collective-permute-start(f32[56,256]{1,0:T(8,128)S(1)} %get-tuple-element.25.zup_ref), channel_id=1, source_target_pairs={{0,1},{1,2},{2,3},{3,0},{4,5},{5,6},{6,7},{7,4},{8,9},{9,10},{10,1... | collective-permute-start | bytes 172040 | tf_op jit(solution)/shard_map/ppermute | solution.py:553
  7.7 5.3 %collective-permute-start.3 = (f32[56,256]{1,0:T(8,128)S(1)}, f32[56,256]{1,0:T(8,128)S(1)}, u32[]{:S(2)}, u32[]{:S(2)}) collective-permute-start(f32[56,256]{1,0:T(8,128)S(1)} %get-tuple-element.26.zdown_ref), channel_id=1, source_target_pairs={{0,3},{1,0},{2,1},{3,2},{4,7},{5,4},{6,5},{7,6},{8,11},{9,8},{10,9... | collective-permute-start | bytes 172040 | tf_op jit(solution)/shard_map/ppermute | solution.py:553
  13.0 7.0 %copy-start = (f32[16,128]{1,0:T(8,128)S(1)}, f32[16,128]{1,0:T(8,128)}, u32[]{:S(2)}) copy-start(f32[16,128]{1,0:T(8,128)} %constant.9.clone) | copy-start | bytes 24580
  15.7 11.4 %all-to-all-start = ((f32[32,1,128]{2,1,0:T(1,128)}), f32[32,1,128]{2,1,0:T(1,128)S(1)}, u32[]{:S(2)}, u32[]{:S(2)}) async-start(f32[32,1,128]{2,1,0:T(1,128)} %bitcast.1), calls=%async_computation | async-start | bytes 32768 | tf_op jit(solution)/shard_map/all_to_all | solution.py:667

commit v9 on v7

--- a/solution.py
+++ b/solution.py
@@ -159,12 +159,57 @@
     return out
 
 
+def places(planes, rows, layers):
+    grid = np.meshgrid(np.asarray(planes), np.asarray(rows), np.asarray(layers), indexing="ij")
+    return np.stack([g.reshape(-1) for g in grid])
+
+
+def couple(to, of, up_planes, rows=True):
+    step = of[:, None, :] - to[:, :, None]
+    out = np.zeros(step.shape[1:])
+    for k in range(1, REACH + 1):
+        if rows:
+            out[(step[0] == 0) & (np.abs(step[1]) == k) & (step[2] == 0)] = SIDE[k]
+        out[(step[0] == 0) & (step[1] == 0) & (np.abs(step[2]) == k)] = SIDE[k]
+        if up_planes:
+            out[(step[0] == k) & (step[1] == 0) & (step[2] == 0)] = SIDE[k]
+    return out
+
+
+def halves(matrix):
+    matrix = np.asarray(matrix, np.float32)
+    high = matrix.astype(jnp.bfloat16)
+    return high, (matrix - high.astype(np.float32)).astype(jnp.bfloat16)
+
+
+def table_left(matrix):
+    high, low = halves(matrix)
+    return np.concatenate([high, low, high], axis=1)
+
+
+def above_tables(owned, reach, ny):
+    four = np.arange(REACH)
+    over = places(np.arange(reach), ny + four, [0])
+    target = places(np.arange(owned), ny + four, [0])
+    sources = [
+        over,
+        places(np.arange(owned), ny + REACH + four, [0]),
+        places(np.arange(owned), ny - REACH + four, [0]),
+    ]
+    image = couple(target, np.concatenate(sources, axis=1), True)
+    pull = couple(over, places(np.arange(reach), ny - REACH + four, [0]), False)
+    chain = couple(target, over, True, rows=False) @ pull
+    return table_left(image), table_left(np.concatenate([pull[: owned * REACH], chain], 0))
+
+
 def inner_kernel(
     owned,
     b_ref,
     pot_ref,
     zup_ref,
     zdown_ref,
+    image_hbm,
+    pull_hbm,
     out_ref,
     both_ref,
     half_ref,
@@ -174,10 +219,20 @@
     pairs_ref,
     edges_ref,
     base_ref,
+    top_ref,
+    image_ref,
+    pull_ref,
     pad_ref,
+    sems,
 ):
     fields, cx, ny, nz = b_ref.shape
     srcs = fields // 2
+    copies = (
+        pltpu.make_async_copy(image_hbm, image_ref, sems.at[0]),
+        pltpu.make_async_copy(pull_hbm, pull_ref, sems.at[1]),
+    )
+    for copy in copies:
+        copy.start()
     reach = out_ref.shape[1]
     rows = fields * REACH
     both_ref[...] = wide_right(band((nz, nz), 0, (1, -1)))
@@ -242,6 +297,12 @@
             im = im + br * bi
         base_ref[s : s + 1, :] = fold(re)
         base_ref[srcs + s : srcs + s + 1, :] = fold(2.0 * im)
+    for f in range(fields):
+        for x in range(owned):
+            at = (f * owned + x) * REACH
+            top_ref[at : at + REACH, :] = b_ref[f, x, ny - REACH : ny, :]
+    for copy in copies:
+        copy.wait()
 
 
 def fold(value):
@@ -272,6 +333,7 @@
     base_ref,
     h_ref,
     acc_ref,
+    last_ref,
     pad_ref,
     edge_ref,
     step_ref,
@@ -321,6 +383,8 @@
             middle = [total[8 : ny - 8]] if ny > 16 else []
             first, last = total[0:8] + low, total[ny - 8 : ny] + high
             h_ref[f, x] = jnp.concatenate([first] + middle + [last], axis=0)
+            at = (f * reach + x) * REACH
+            last_ref[at : at + REACH, :] = last[8 - REACH : 8]
             if x < owned:
                 u = jnp.concatenate([first + low] + middle + [last + 3.0 * high], axis=0)
                 spot = pl.ds(x * ny, ny)
@@ -396,68 +460,56 @@
             acc_ref[at : at + 1, :] = acc_ref[at : at + 1, :] + fold(both[c][s * REACH : (s + 1) * REACH])
 
 
-def tail_kernel(owned, b_ref, h_ref, above_ref, more_ref, both_ref, sums_ref, out_ref, acc_ref, far_ref, pull_ref):
-    fields, reach, ny, nz = h_ref.shape
+def tail_kernel(
+    owned,
+    above_ref,
+    more_ref,
+    top_ref,
+    last_ref,
+    both_ref,
+    image_ref,
+    pull_ref,
+    sums_ref,
+    out_ref,
+    acc_ref,
+):
+    cut = owned * REACH
+    fields = top_ref.shape[0] // cut
+    span = last_ref.shape[0] // fields
+    nz = top_ref.shape[1]
     srcs = fields // 2
-    for f in range(fields):
-        at = f * reach * REACH
-        far_ref[f] = mul(wide_left(above_ref[at : at + owned * REACH, :]), both_ref[...])
-
-    quad_row = lax.broadcasted_iota(jnp.int32, (8, nz), 0) % REACH
-    early = lax.broadcasted_iota(jnp.int32, (8, nz), 0) < REACH
-
-    def top(ref, f, x):
-        return jnp.where(early, pltpu.roll(ref[f, x, ny - 8 : ny, :], REACH, 0), ref[f, x + 1, ny - 8 : ny, :])
-
-    def lowered(lower, upper, k):
-        if k == REACH:
-            return lower
-        return jnp.where(quad_row >= k, pltpu.roll(upper, k, 0), pltpu.roll(lower, REACH + k, 0))
-
-    def raised(lower, upper, k):
-        if k == REACH:
-            return upper
-        return jnp.where(quad_row < REACH - k, pltpu.roll(lower, 8 - k, 0), pltpu.roll(upper, REACH - k, 0))
-
-    for f in range(fields):
-        for x in range(0, reach, 2):
-            own = top(h_ref, f, x)
-            pull = SIDE[REACH] * own
-            for k in range(1, REACH):
-                pull = pull + SIDE[k] * jnp.where(quad_row < k, pltpu.roll(own, REACH + k, 0), 0.0)
-            at = (f * reach + x) * REACH
-            pull_ref[at : at + 8, :] = pull
+
+    def over(f):
+        return jnp.concatenate(
+            [
+                above_ref[f * span : (f + 1) * span, :],
+                more_ref[f * cut : (f + 1) * cut, :],
+                top_ref[f * cut : (f + 1) * cut, :],
+            ],
+            axis=0,
+        )
+
+    def paired(table_ref, rows_of, s):
+        parts = [wide_right(rows_of(part * srcs + s)) for part in range(2)]
+        return mul(table_ref[...], jnp.concatenate(parts, axis=1))
 
     acc_ref[...] = sums_ref[...]
+    local = more_ref[fields * cut : (fields + 1) * cut, :]
     for s in range(srcs):
-        cross = [jnp.zeros((8, nz), jnp.float32) for _ in range(2)]
-        for x in range(0, owned, 2):
-            at = (fields * owned + x) * REACH
-            local = more_ref[at : at + 8, :]
-            left, right, first, pulls = [], [], [], []
-            for part in range(2):
-                f = part * srcs + s
-                at = (f * reach + x) * REACH
-                own = top(b_ref, f, x)
-                first_layers = above_ref[at : at + 8, :]
-                start = (f * owned + x) * REACH
-                more = more_ref[start : start + 8, :]
-                value = far_ref[f, x * REACH : x * REACH + 8, :] + local * first_layers
-                pull = 0.0
-                for k in range(1, REACH + 1):
-                    sides = above_ref[at + k * REACH : at + k * REACH + 8, :]
-                    sides = sides + raised(first_layers, more, k) + lowered(own, first_layers, k)
-                    value = value + SIDE[k] * sides
-                    pull = pull + SIDE[k] * pull_ref[at + k * REACH : at + k * REACH + 8, :]
-                left.append(pull_ref[at : at + 8, :])
-                right.append(value)
-                first.append(first_layers)
-                pulls.append(pull)
-            for c, (one, two) in enumerate(zip(product(left, right), product(first, pulls))):
-                cross[c] = cross[c] + (one + two)
-        for c in range(2):
+        image = paired(image_ref, over, s)
+        pull = paired(pull_ref, lambda f: last_ref[f * span : (f + 1) * span, :], s)
+        left, right, first, pulls = [], [], [], []
+        for part in range(2):
+            at = (part * srcs + s) * span
+            lanes = slice(part * nz, (part + 1) * nz)
+            close = above_ref[at : at + cut, :]
+            right.append(image[:, lanes] + mul(wide_left(close), both_ref[...]) + local * close)
+            left.append(pull[0:cut, lanes])
+            first.append(close)
+            pulls.append(pull[cut : 2 * cut, lanes])
+        for c, (one, two) in enumerate(zip(product(left, right), product(first, pulls))):
             at = (6 + c) * srcs + s
-            acc_ref[at : at + 1, :] = acc_ref[at : at + 1, :] + 2.0 * fold(cross[c])
+            acc_ref[at : at + 1, :] = acc_ref[at : at + 1, :] + 2.0 * fold(one + two)
 
     column = jnp.sum(acc_ref[...], axis=1, keepdims=True)
     row = lax.broadcasted_iota(jnp.int32, acc_ref.shape, 0)
@@ -610,6 +662,7 @@
     zbelow = shift(zup, "pz", 1)
     more = shift(far, "py", -1)
 
+    tables = above_tables(owned, reach, ny)
     half = lambda *dims: jax.ShapeDtypeStruct(dims, jnp.bfloat16)
     inner, *weights = pl.pallas_call(
         functools.partial(inner_kernel, owned),
@@ -623,21 +676,26 @@
             half(owned * ny, 3 * reach * ny),
             shaped(2 * rows, LANES),
             shaped(2 * srcs, nz),
+            shaped(fields * owned * REACH, nz),
+            *(jax.ShapeDtypeStruct(t.shape, t.dtype) for t in tables),
         ),
-        in_specs=[VMEM] * 4,
-        out_specs=(VMEM,) * 9,
-        scratch_shapes=[pltpu.VMEM((reach, ny + 16, nz), jnp.float32)],
+        in_specs=[VMEM] * 4 + [HBM] * 2,
+        out_specs=(VMEM,) * 12,
+        scratch_shapes=[
+            pltpu.VMEM((reach, ny + 16, nz), jnp.float32),
+            pltpu.SemaphoreType.DMA((2,)),
+        ],
         compiler_params=small(12),
         cost_estimate=cost(fields * cells * 60, fields * cells * 12),
         name="inner",
-    )(b, pot, zup, zdown)
-
-    both, *weights = weights
-    image, sums = pl.pallas_call(
+    )(b, pot, zup, zdown, *(pltpu.with_memory_space_constraint(jnp.asarray(t), pltpu.HBM) for t in tables))
+
+    both, *weights, top, image_table, pull_table = weights
+    image, sums, last = pl.pallas_call(
         functools.partial(main_kernel, owned),
-        out_shape=(part, shaped(8 * srcs, nz)),
+        out_shape=(part, shaped(8 * srcs, nz), shaped(fields * reach * REACH, nz)),
         in_specs=[VMEM] * 16,
-        out_specs=(VMEM,) * 2,
+        out_specs=(VMEM,) * 3,
         scratch_shapes=[
             pltpu.VMEM((2, reach, 16, nz), jnp.float32),
             pltpu.VMEM((LANES, nz), jnp.float32),
@@ -651,16 +709,12 @@
     partial = pl.pallas_call(
         functools.partial(tail_kernel, owned),
         out_shape=shaped(quads * py * pz, LANES),
-        in_specs=[VMEM] * 6,
+        in_specs=[VMEM] * 8,
         out_specs=VMEM,
-        scratch_shapes=[
-            pltpu.VMEM((8 * srcs, nz), jnp.float32),
-            pltpu.VMEM((fields, owned * REACH, nz), jnp.float32),
-            pltpu.VMEM((fields * reach * REACH, nz), jnp.float32),
-        ],
+        scratch_shapes=[pltpu.VMEM((8 * srcs, nz), jnp.float32)],
         compiler_params=small(8),
         name="tail",
-    )(b, image, above, more, both, sums)
+    )(above, more, top, last, both, image_table, pull_table, sums)
 
     total = lax.all_to_all(partial, ("quad", "py", "pz"), 0, 0)
 

time: 29.1 us -> 29.1 us (level)
  no operation moved by 1% of the time
where the time goes in v9:
time: 29.1 us; the launch traced here: 28.8 us
  starting transfers between devices  12.3 us (42%)
  Pallas kernels  8.03 us (28%)
  waiting for transfers between devices  7.05 us (24%)
  between operations  1.39 us (5%)
    ppermute x5, starting transfers between devices, shift(): return lax.ppermute(value, axis, ring(lax.axis_size(axis), step))  8.06 us
    all_to_all x1, waiting for transfers between devices, per_device(): total = lax.all_to_all(partial, ('quad', 'py', 'pz'), 0, 0)  7.04 us
    all_to_all x1, starting transfers between devices, per_device(): total = lax.all_to_all(partial, ('quad', 'py', 'pz'), 0, 0)  4.22 us
    pallas_call x1, Pallas kernels, per_device(): pl.pallas_call(functools.partial(load_kernel, owned), out_shape=(shaped(f...  1.95 us
    pallas_call x1, Pallas kernels, per_device(): pl.pallas_call(functools.partial(inner_kernel, owned), out_shape=(part, h...  1.74 us
    pallas_call x1, Pallas kernels, per_device(): pl.pallas_call(output_kernel, out_shape=shaped(MOMS, 2, srcs, owned, ny,...  1.68 us
    pallas_call x1, Pallas kernels, per_device(): pl.pallas_call(functools.partial(main_kernel, owned), out_shape=(part, sh...  1.53 us
    pallas_call x1, Pallas kernels, per_device(): pl.pallas_call(functools.partial(tail_kernel, owned), out_shape=shaped(qu...  1.12 us
  transfers between devices with their start and end apart: 6, of which 1 were waited for; matrix products, arithmetic and copies ran while one was open for 0% of the time, Pallas kernels for 11%

profile of v9, /device:TPU:0, one launch (start us, length us, event | category | flops | bytes accessed | tf_op | source)
XLA Modules:
  0.0 28.8 jit_solution(5599125165757981147)
XLA Ops:
  0.0 1.9 %load.1 = (f32[8,16,16,128]{3,2,1,0:T(8,128)S(1)}, f32[16,16,128]{2,1,0:T(8,128)S(1)}, f32[384,128]{1,0:T(8,128)S(1)}, f32[384,128]{1,0:T(8,128)S(1)}, f32[288,1...) custom-call(f32[4,16,16,128]{3,2,1,0:T(8,128)} %re_hbm.1, f32[4,16,16,128]{3,2,1,0:T(8,128)} %im_hbm.1, ...), custom_call_target="tpu_custom_call" | custom-call | tf_op jit(solution)/shard_map/load/pallas_call | solution.py:639
  2.0 2.5 %collective-permute-start = (f32[384,128]{1,0:T(8,128)S(1)}, f32[384,128]{1,0:T(8,128)S(1)}, u32[]{:S(2)}, u32[]{:S(2)}) collective-permute-start(f32[384,128]{1,0:T(8,128)S(1)} %get-tuple-element.27), channel_id=1, source_target_pairs={{0,12},{4,0},{8,4},{12,8},{1,13},{5,1},{9,5},{13,9},{2,14},{6,2},{... | collective-permute-start | bytes 589832 | tf_op jit(solution)/shard_map/ppermute | solution.py:603
  4.4 0.0 collective-permute-start.2
  4.4 1.7 %collective-permute-start.1 = (f32[288,128]{1,0:T(8,128)S(1)}, f32[288,128]{1,0:T(8,128)S(1)}, u32[]{:S(2)}, u32[]{:S(2)}) collective-permute-start(f32[288,128]{1,0:T(8,128)S(1)} %get-tuple-element.28), channel_id=1, source_target_pairs={{0,12},{4,0},{8,4},{12,8},{1,13},{5,1},{9,5},{13,9},{2,14},{6,2},{... | collective-permute-start | bytes 442376 | tf_op jit(solution)/shard_map/ppermute | solution.py:603
  6.2 1.6 %collective-permute-start.3 = (f32[56,256]{1,0:T(8,128)S(1)}, f32[56,256]{1,0:T(8,128)S(1)}, u32[]{:S(2)}, u32[]{:S(2)}) collective-permute-start(f32[56,256]{1,0:T(8,128)S(1)} %get-tuple-element.31.zup_ref), channel_id=1, source_target_pairs={{0,1},{1,2},{2,3},{3,0},{4,5},{5,6},{6,7},{7,4},{8,9},{9,10},{10,1... | collective-permute-start | bytes 172040 | tf_op jit(solution)/shard_map/ppermute | solution.py:603
  7.8 2.2 %collective-permute-start.4 = (f32[56,256]{1,0:T(8,128)S(1)}, f32[56,256]{1,0:T(8,128)S(1)}, u32[]{:S(2)}, u32[]{:S(2)}) collective-permute-start(f32[56,256]{1,0:T(8,128)S(1)} %get-tuple-element.32.zdown_ref), channel_id=1, source_target_pairs={{0,3},{1,0},{2,1},{3,2},{4,7},{5,4},{6,5},{7,6},{8,11},{9,8},{10,9... | collective-permute-start | bytes 172040 | tf_op jit(solution)/shard_map/ppermute | solution.py:603
  11.3 1.7 %inner.1 = (f32[8,12,16,128]{3,2,1,0:T(8,128)S(1)}, bf16[384,128]{1,0:T(8,128)(2,1)S(1)}, bf16[384,128]{1,0:T(8,128)(2,1)S(1)}, bf16[64,768]{1,0:T(8,128)(2,1)S(...) custom-call(f32[8,16,16,128]{3,2,1,0:T(8,128)S(1)} %get-tuple-elemen, ...), custom_call_target="tpu_custom_call" | custom-call | flops 11796480 | bytes 2359296 | tf_op jit(solution)/shard_map/inner/pallas_call | solution.py:667
  13.1 0.0 collective-permute-done.3.zbelow_ref
  13.1 0.0 collective-permute-done.4.zabove_ref
  13.1 0.0 collective-permute-done.above_ref
  13.1 0.0 collective-permute-done.2.below_ref
  13.1 0.0 copy-start
  13.1 1.5 %main.1 = (f32[8,12,16,128]{3,2,1,0:T(8,128)S(1)}, f32[32,128]{1,0:T(8,128)S(1)}, f32[384,128]{1,0:T(8,128)S(1)}) custom-call(f32[8,16,16,128]{3,2,1,0:T(8,128)S(1)} %get-tuple-element.29.b_ref, f32[16,16,128]{2,1,0:T(8,128)S(1)} %get-tuple-element.30.pot_ref, f32[8,12,16,128]{3,2,1,0:T(8,128)S(1)} %get-tuple-element.34.inner_ref, ...), custom_call_target="tpu_custom_call" | custom-call | flops 11796480 | bytes 2359296 | tf_op jit(solution)/shard_map/main/pallas_call | solution.py:694
  14.7 0.0 collective-permute-done.1.more_ref
  14.7 1.1 %tail.1 = f32[32,128]{1,0:T(8,128)} custom-call(f32[384,128]{1,0:T(8,128)S(1)} %collective-permute-done.above_ref, f32[288,128]{1,0:T(8,128)S(1)} %collective-permute-done.1.more_ref, f32[256,128]{1,0:T(8,128)S(1)} %get-tuple-element.33.top_ref, f32[384,128]{1,0:T(8,128)S(1)} %get-tuple-element.43.last_ref, bf16[384,128]{1,0:T(8,128)(2,1)S(1)} %get-tuple-element.44.both_ref, ...), custom_call_target="tpu_custom_call" | custom-call | tf_op jit(solution)/shard_map/tail/pallas_call | solution.py:709
  15.8 4.2 %all-to-all-start = ((f32[32,1,128]{2,1,0:T(1,128)}), f32[32,1,128]{2,1,0:T(1,128)S(1)}, u32[]{:S(2)}, u32[]{:S(2)}) async-start(f32[32,1,128]{2,1,0:T(1,128)} %bitcast.1), calls=%async_computation | async-start | bytes 32768 | tf_op jit(solution)/shard_map/all_to_all | solution.py:719
  20.0 0.0 copy-done
  20.0 0.1 multiply_add_fusion.table_ref
  20.1 7.0 %all-to-all-done = f32[32,1,128]{2,1,0:T(1,128)S(1)} async-done(((f32[32,1,128]{2,1,0:T(1,128)}), f32[32,1,128]{2,1,0:T(1,128)S(1)}, u32[]{:S(2)}, u32[]{:S(2)}) %all-to-all-start) | async-done | bytes 16416 | tf_op jit(solution)/shard_map/all_to_all | solution.py:719
  27.2 1.7 %output.1 = f32[4,2,4,8,16,128]{5,4,3,2,1,0:T(8,128)} custom-call(f32[32,128]{1,0:T(8,128)S(1)} %bitcast.7, f32[16,128]{1,0:T(8,128)S(1)} %multiply_add_fusion.table_ref, f32[8,16,16,128]{3,2,1,0:T(8,128)S(1)} %get-tuple-element.29.b_ref, f32[8,12,16,128]{3,2,1,0:T(8,128)S(1)} %get-tuple-element.48.h_ref), custom_call_target="tpu_custom_call" | custom-call | tf_op jit(solution)/shard_map/output/pallas_call | solution.py:724
  (1 shorter events, 0.0 us)
Async XLA Ops:
  2.0 11.1 %collective-permute-start = (f32[384,128]{1,0:T(8,128)S(1)}, f32[384,128]{1,0:T(8,128)S(1)}, u32[]{:S(2)}, u32[]{:S(2)}) collective-permute-start(f32[384,128]{1,0:T(8,128)S(1)} %get-tuple-element.27), channel_id=1, source_target_pairs={{0,12},{4,0},{8,4},{12,8},{1,13},{5,1},{9,5},{13,9},{2,14},{6,2},{... | collective-permute-start | bytes 589832 | tf_op jit(solution)/shard_map/ppermute | solution.py:603
  4.4 8.7 %collective-permute-start.2 = (f32[384,128]{1,0:T(8,128)S(1)}, f32[384,128]{1,0:T(8,128)S(1)}, u32[]{:S(2)}, u32[]{:S(2)}) collective-permute-start(f32[384,128]{1,0:T(8,128)S(1)} %get-tuple-element.35), channel_id=1, source_target_pairs={{0,4},{4,8},{8,12},{12,0},{1,5},{5,9},{9,13},{13,1},{2,6},{6,10},{... | collective-permute-start | bytes 589832 | tf_op jit(solution)/shard_map/ppermute | solution.py:603
  4.4 10.2 %collective-permute-start.1 = (f32[288,128]{1,0:T(8,128)S(1)}, f32[288,128]{1,0:T(8,128)S(1)}, u32[]{:S(2)}, u32[]{:S(2)}) collective-permute-start(f32[288,128]{1,0:T(8,128)S(1)} %get-tuple-element.28), channel_id=1, source_target_pairs={{0,12},{4,0},{8,4},{12,8},{1,13},{5,1},{9,5},{13,9},{2,14},{6,2},{... | collective-permute-start | bytes 442376 | tf_op jit(solution)/shard_map/ppermute | solution.py:603
  6.2 6.9 %collective-permute-start.3 = (f32[56,256]{1,0:T(8,128)S(1)}, f32[56,256]{1,0:T(8,128)S(1)}, u32[]{:S(2)}, u32[]{:S(2)}) collective-permute-start(f32[56,256]{1,0:T(8,128)S(1)} %get-tuple-element.31.zup_ref), channel_id=1, source_target_pairs={{0,1},{1,2},{2,3},{3,0},{4,5},{5,6},{6,7},{7,4},{8,9},{9,10},{10,1... | collective-permute-start | bytes 172040 | tf_op jit(solution)/shard_map/ppermute | solution.py:603
  7.8 5.3 %collective-permute-start.4 = (f32[56,256]{1,0:T(8,128)S(1)}, f32[56,256]{1,0:T(8,128)S(1)}, u32[]{:S(2)}, u32[]{:S(2)}) collective-permute-start(f32[56,256]{1,0:T(8,128)S(1)} %get-tuple-element.32.zdown_ref), channel_id=1, source_target_pairs={{0,3},{1,0},{2,1},{3,2},{4,7},{5,4},{6,5},{7,6},{8,11},{9,8},{10,9... | collective-permute-start | bytes 172040 | tf_op jit(solution)/shard_map/ppermute | solution.py:603
  13.1 6.9 %copy-start = (f32[16,128]{1,0:T(8,128)S(1)}, f32[16,128]{1,0:T(8,128)}, u32[]{:S(2)}) copy-start(f32[16,128]{1,0:T(8,128)} %constant.15.clone) | copy-start | bytes 24580
  15.8 11.4 %all-to-all-start = ((f32[32,1,128]{2,1,0:T(1,128)}), f32[32,1,128]{2,1,0:T(1,128)S(1)}, u32[]{:S(2)}, u32[]{:S(2)}) async-start(f32[32,1,128]{2,1,0:T(1,128)} %bitcast.1), calls=%async_computation | async-start | bytes 32768 | tf_op jit(solution)/shard_map/all_to_all | solution.py:719
